TPU v7x, 512 devices: a whole 4x4x16 slice. The times are simulated.
512 devices in a mesh: dp: 16 (over z), ctx: 32 (over y, x, core).
Axes of the slice: x: 4, y: 4, z: 16, core: 2. Of those that a mesh axis runs over, the one named last changes fastest.
Arguments:
- queries: bfloat16 [16, 4096, 4096], P('dp', 'ctx'), may hold values from -216 to 216
- keys: bfloat16 [16, 4096, 1024], P('dp', 'ctx'), may hold values from -6 to 6
- values: bfloat16 [16, 4096, 1024], P('dp', 'ctx'), may hold values from -6 to 6
- out_grad: bfloat16 [16, 4096, 4096], P('dp', 'ctx'), may hold values from -6 to 6
- block_mask: int32 [32, 32, 32], replicated, may hold values from 0 to 1, as said below
Outputs:
- query_grad: bfloat16 [16, 4096, 4096], P('dp', 'ctx')
- key_grad: bfloat16 [16, 4096, 1024], P('dp', 'ctx')
- value_grad: bfloat16 [16, 4096, 1024], P('dp', 'ctx')
- z_loss: float32 [32], P('ctx')
Inputs may be any that keep to these rules, and one draw needn't show every extreme that they name: block_mask[h, a, b] is 1 only where b <= a; block_mask[h, a, a] = 1 and block_mask[h, a, 0] = 1 for every head h and query block a.
All inputs are finite; a program needn't handle non-finite values.
Results may differ from a plain program's by a relative error of at most 0.014.
Values may be sent and summed in bfloat16 or wider, within the bound.
No kernel may reach another device: no remote copies, remote signals or barrier semaphores. Data moves between devices by JAX's collectives and lax.ppermute only.
A program may use at most 128 MiB of HBM per device.

v0:
```python
import jax
import jax.numpy as jnp
from jax import lax
from jax.sharding import PartitionSpec as P

H = 32
KVH = 8
HD = 128
BLK = 128


ZLOSS = 0.05
NEG = -1e30


def key_block_order(rows_mask, block_count):
    active = jnp.max(rows_mask, axis=0)
    active_count = jnp.sum(active)
    positions = jnp.arange(block_count, dtype=jnp.int32)
    block_order = jnp.argsort(jnp.where(active > 0, positions, positions + block_count))
    return (block_order, active_count)


def body(queries, keys, values, out_grad, block_mask):
    tok_rows = queries.shape[1]
    ctx_size = lax.axis_size("ctx")
    my_index = lax.axis_index("ctx")
    seq_len = tok_rows * ctx_size
    tile_rows = 4 * BLK
    tile_count = seq_len // tile_rows
    block_count = seq_len // BLK
    pair_slots = block_count // 2
    per_device = H // ctx_size
    group_size = H // KVH
    softmax_scale = HD ** (-0.5)
    query_tok = queries[0].reshape(tok_rows, H, HD)
    grad_tok = out_grad[0].reshape(tok_rows, H, HD)
    key_tok = keys[0].reshape(tok_rows, KVH, HD)
    value_tok = values[0].reshape(tok_rows, KVH, HD)
    device_ids = jnp.arange(ctx_size, dtype=jnp.int32)[:, None]
    slot_ids = jnp.arange(per_device, dtype=jnp.int32)[None, :]
    own_head = device_ids * per_device + slot_ids
    head_table = jnp.stack([own_head, own_head], axis=2)
    kv_table = own_head // group_size
    slot_table = jnp.stack([slot_ids + 0 * device_ids] * 2, axis=2)
    send_q = query_tok.reshape(tok_rows, ctx_size, per_device, HD)
    send_grad = grad_tok.reshape(tok_rows, ctx_size, per_device, HD)
    kv_slots = kv_table.shape[1]
    kv_flat = kv_table.reshape(-1)
    send_key = jnp.take(key_tok, kv_flat, axis=1).reshape(tok_rows, ctx_size, kv_slots, HD)
    send_value = jnp.take(value_tok, kv_flat, axis=1).reshape(tok_rows, ctx_size, kv_slots, HD)
    query_pack = jnp.stack([send_q, send_grad], axis=2)
    kv_pack = jnp.stack([send_key, send_value], axis=2)
    query_heads, kv_heads = (
        lax.all_to_all(query_pack, "ctx", split_axis=1, concat_axis=0, tiled=True),
        lax.all_to_all(kv_pack, "ctx", split_axis=1, concat_axis=0, tiled=True),
    )
    head_query = query_heads[:, 0, 0]
    head_grad = query_heads[:, 0, 1]
    head_key = kv_heads[:, 0, 0]
    head_value = kv_heads[:, 0, 1]
    my_heads = head_table[my_index]
    my_slots = slot_table[my_index]

    def one_tile(work_item, state_in):
        dq_all, kv_grad, z_parts = state_in
        slot_pos = work_item // tile_count
        tile_pos = work_item % tile_count
        tile_half = (tile_pos + 1) // 2 % 2
        head_now = my_heads[slot_pos, tile_half]
        kv_slot = my_slots[slot_pos, tile_half]
        first_row = tile_pos * tile_rows
        q_tile = lax.dynamic_slice(head_query, (first_row, slot_pos, 0), (tile_rows, 1, HD))[:, 0]
        g_tile = lax.dynamic_slice(head_grad, (first_row, slot_pos, 0), (tile_rows, 1, HD))[:, 0]
        key_blocks = lax.dynamic_index_in_dim(head_key, kv_slot, axis=1, keepdims=False).reshape(
            block_count, BLK, HD
        )
        value_blocks = lax.dynamic_index_in_dim(
            head_value, kv_slot, axis=1, keepdims=False
        ).reshape(block_count, BLK, HD)
        rows_mask = lax.dynamic_slice(block_mask, (head_now, tile_pos * 4, 0), (1, 4, block_count))[
            0
        ]
        block_order, active_count = key_block_order(rows_mask, block_count)
        group_total = (active_count + 1) // 2
        query_pos = first_row + jnp.arange(tile_rows, dtype=jnp.int32)

        def pair_blocks(pair_pos):
            block_index = lax.dynamic_slice(block_order, (2 * pair_pos,), (2,))
            usable = 2 * pair_pos + jnp.arange(2, dtype=jnp.int32) < active_count
            keys_here = key_blocks[block_index].reshape(2 * BLK, HD)
            values_here = value_blocks[block_index].reshape(2 * BLK, HD)
            block_on = (rows_mask[:, block_index] > 0) & usable[None, :]
            allowed = jnp.broadcast_to(block_on[:, None, :, None], (4, BLK, 2, BLK)).reshape(
                tile_rows, 2 * BLK
            )
            key_pos = (
                block_index[:, None] * BLK + jnp.arange(BLK, dtype=jnp.int32)[None, :]
            ).reshape(-1)
            allowed = allowed & (key_pos[None, :] <= query_pos[:, None])
            return (block_index, keys_here, values_here, allowed)

        def max_step(pair_pos, state_max):
            run_max, run_sum, score_store = state_max
            keys_here, allowed = pair_blocks(pair_pos)[1::2]
            scores = (
                jnp.einsum("qd,kd->qk", q_tile, keys_here, preferred_element_type=jnp.float32)
                * softmax_scale
            )
            score_store = lax.dynamic_update_slice(score_store, scores[None], (pair_pos, 0, 0))
            masked = jnp.where(allowed, scores, NEG)
            new_max = jnp.maximum(run_max, jnp.max(masked, axis=1))
            weights = jnp.where(allowed, jnp.exp(scores - new_max[:, None]), 0.0)
            return (
                new_max,
                run_sum * jnp.exp(run_max - new_max) + jnp.sum(weights, axis=1),
                score_store,
            )

        start_max = jnp.full((tile_rows,), NEG, jnp.float32)
        start_sum = jnp.zeros((tile_rows,), jnp.float32)
        start_store = jnp.zeros((pair_slots, tile_rows, 2 * BLK), jnp.float32)
        run_max, run_sum, score_store = lax.fori_loop(
            0, group_total, max_step, (start_max, start_sum, start_store)
        )
        log_norm = run_max + jnp.log(run_sum)

        def out_step(pair_pos, out_acc):
            values_here, allowed = pair_blocks(pair_pos)[2:]
            scores = lax.dynamic_index_in_dim(score_store, pair_pos, axis=0, keepdims=False)
            probs_low = jnp.where(allowed, jnp.exp(scores - log_norm[:, None]), 0.0).astype(
                jnp.bfloat16
            )
            return out_acc + jnp.dot(probs_low, values_here, preferred_element_type=jnp.float32)

        out_acc = lax.fori_loop(0, group_total, out_step, jnp.zeros((tile_rows, HD), jnp.float32))
        attn_out = out_acc.astype(jnp.bfloat16)
        row_delta = jnp.sum(g_tile.astype(jnp.float32) * attn_out.astype(jnp.float32), axis=1)
        zloss_pull = 2.0 * ZLOSS * log_norm

        def grad_step(pair_pos, state_grad):
            dq_acc, kv_acc = state_grad
            block_index, keys_here, values_here, allowed = pair_blocks(pair_pos)
            scores = lax.dynamic_index_in_dim(score_store, pair_pos, axis=0, keepdims=False)
            probs = jnp.where(allowed, jnp.exp(scores - log_norm[:, None]), 0.0)
            probs_low = probs.astype(jnp.bfloat16)
            prob_grad = jnp.einsum(
                "qd,kd->qk", g_tile, values_here, preferred_element_type=jnp.float32
            )
            dscore = (probs * (prob_grad - row_delta[:, None] + zloss_pull[:, None])).astype(
                jnp.bfloat16
            )
            dq_acc = dq_acc + jnp.dot(dscore, keys_here, preferred_element_type=jnp.float32)
            key_part = (
                jnp.einsum("qk,qd->kd", dscore, q_tile, preferred_element_type=jnp.float32)
                * softmax_scale
            )
            value_part = jnp.einsum(
                "qk,qd->kd", probs_low, g_tile, preferred_element_type=jnp.float32
            )
            kv_acc = kv_acc.at[block_index, :, 0, kv_slot].add(key_part.reshape(2, BLK, HD))
            kv_acc = kv_acc.at[block_index, :, 1, kv_slot].add(value_part.reshape(2, BLK, HD))
            return (dq_acc, kv_acc)

        dq_acc, kv_grad = lax.fori_loop(
            0, group_total, grad_step, (jnp.zeros((tile_rows, HD), jnp.float32), kv_grad)
        )
        dq_tile = (softmax_scale * dq_acc).astype(jnp.bfloat16)
        dq_all = lax.dynamic_update_slice(dq_all, dq_tile[:, None, :], (first_row, slot_pos, 0))
        z_parts = z_parts.at[slot_pos, tile_half].add(jnp.sum(log_norm * log_norm))
        return (dq_all, kv_grad, z_parts)

    start_dq = jnp.zeros((seq_len, per_device, HD), jnp.bfloat16)
    start_kv = jnp.zeros((block_count, BLK, 2, kv_slots, HD), jnp.float32)
    start_z = jnp.zeros((per_device, 2), jnp.float32)
    dq_all, kv_grad, z_parts = lax.fori_loop(
        0, per_device * tile_count, one_tile, (start_dq, start_kv, start_z)
    )
    dq_back = lax.all_to_all(
        dq_all.reshape(seq_len, 1, per_device, HD), "ctx", split_axis=0, concat_axis=1, tiled=True
    )
    kv_back = lax.all_to_all(
        kv_grad.reshape(seq_len, 1, 2, kv_slots, HD).astype(jnp.bfloat16),
        "ctx",
        split_axis=0,
        concat_axis=1,
        tiled=True,
    ).astype(jnp.float32)
    query_grad = dq_back.reshape(tok_rows, H * HD)
    one_hot = (kv_table[:, :, None] == jnp.arange(KVH, dtype=jnp.int32)[None, None, :]).astype(
        jnp.float32
    )
    kv_sum = jnp.einsum("tjcud,jug->tcgd", kv_back, one_hot, precision=lax.Precision.HIGHEST)
    key_grad = kv_sum[:, 0].reshape(tok_rows, KVH * HD).astype(jnp.bfloat16)
    value_grad = kv_sum[:, 1].reshape(tok_rows, KVH * HD).astype(jnp.bfloat16)
    z_full = jnp.zeros((H,), jnp.float32).at[my_heads.reshape(-1)].add(z_parts.reshape(-1))
    z_total = lax.psum(z_full, ("dp", "ctx"))
    z_own = lax.dynamic_slice(z_total, (my_index * per_device,), (per_device,)) * (
        ZLOSS / (seq_len * lax.axis_size("dp"))
    )
    return (query_grad[None], key_grad[None], value_grad[None], z_own)


def solution(mesh):
    return jax.shard_map(
        body,
        mesh=mesh,
        in_specs=(
            P("dp", "ctx", None),
            P("dp", "ctx", None),
            P("dp", "ctx", None),
            P("dp", "ctx", None),
            P(),
        ),
        out_specs=(P("dp", "ctx", None), P("dp", "ctx", None), P("dp", "ctx", None), P("ctx")),
        check_vma=False,
    )
```

profile of v0, /device:TPU:1, one launch (start us, length us, event | category | flops | bytes accessed | tf_op | source)
XLA Modules:
  0.0 1665.5 jit_solution(11246638832345743886)
XLA Ops:
  6.7 10.5 all-to-all-start
  28.0 17.2 %all-to-all-done = bf16[128,32,2,1,128]{4,0,3,2,1:T(8,128)(2,1)S(1)} async-done(((bf16[128,32,2,1,128]{4,0,3,2,1:T(8,128)(2,1)}), bf16[128,32,2,1,128]{4,0,3,2,1:T(8,128)(2,1)S(1)}, u32[]{:S(2)}, u32[]{:S(2)}) %all-to-all-start) | async-done | bytes 2097184 | tf_op jit(solution)/shard_map/all_to_all | solution.py:56
  53.6 26.3 %all-to-all-done.1 = bf16[128,32,2,1,128]{4,0,2,3,1:T(8,128)(2,1)} async-done(((bf16[128,32,2,1,128]{4,0,2,3,1:T(8,128)(2,1)}), bf16[128,32,2,1,128]{4,0,2,3,1:T(8,128)(2,1)}, u32[]{:S(2)}, u32[]{:S(2)}) %all-to-all-start.1) | async-done | bytes 2097184 | tf_op jit(solution)/shard_map/all_to_all | solution.py:55
  87.1 1168.1 %while.153 = (s32[]{:T(128)}, bf16[4096,1,128]{2,0,1:T(8,128)(2,1)}, f32[32,128,2,1,128]{4,1,2,0,3:T(8,128)}, f32[1,2]{1,0:T(1,128)S(1)}, s32[1,2]{1,0:T(1,128)S...) while((s32[]{:T(128)}, bf16[4096,1,128]{2,0,1:T(8,128)(2,1)}, ...), condition=%wide.region_17.19_spmd, body=%wide.region_0.18_spmd.sunk | while | flops 205693264 | bytes 23033788 | solution.py:176
  98.6 7.1 while.154
  110.5 13.2 while.155
  124.8 23.3 %while.156 = (s32[]{:T(128)}, f32[512,128]{1,0:T(8,128)S(1)}, f32[32,128,2,1,128]{4,1,2,0,3:T(8,128)}, s32[]{:T(128)}, s32[32]{0:T(128)S(1)}, /*index=5*/s32[4,3...) while((s32[]{:T(128)}, f32[512,128]{1,0:T(8,128)S(1)}, ...), condition=%wide.region_14.15_spmd.clone, body=%wide.region_11.14_spmd.clone.sunk | while | flops 136087360 | bytes 5133853 | solution.py:165
  160.2 14.2 while.154
  179.2 26.4 %while.155 = (s32[]{:T(128)}, f32[512,128]{1,0:T(8,128)S(1)}, s32[]{:T(128)}, s32[32]{0:T(128)S(1)}, s32[4,32]{0,1:T(8,128)S(1)}, /*index=5*/s32[]{:T(128)}, f32...) while((s32[]{:T(128)}, f32[512,128]{1,0:T(8,128)S(1)}, ...), condition=%wide.region_9.10_spmd.clone, body=%wide.region_8.9_spmd.clone.sunk | while | flops 34277156 | bytes 4927917 | solution.py:136
  206.7 46.5 %while.156 = (s32[]{:T(128)}, f32[512,128]{1,0:T(8,128)S(1)}, f32[32,128,2,1,128]{4,1,2,0,3:T(8,128)}, s32[]{:T(128)}, s32[32]{0:T(128)S(1)}, /*index=5*/s32[4,3...) while((s32[]{:T(128)}, f32[512,128]{1,0:T(8,128)S(1)}, ...), condition=%wide.region_14.15_spmd.clone, body=%wide.region_11.14_spmd.clone.sunk | while | flops 136087360 | bytes 5133853 | solution.py:165
  265.4 17.7 %while.154 = (s32[]{:T(128)}, f32[512]{0:T(512)S(1)}, f32[512]{0:T(512)S(1)}, f32[16,512,256]{1,2,0:T(8,128)}, s32[]{:T(128)}, /*index=5*/s32[32]{0:T(128)S(1)},...) while((s32[]{:T(128)}, f32[512]{0:T(512)S(1)}, ...), condition=%wide.region_7.8_spmd.clone, body=%wide.region_4.7_spmd.clone.sunk | while | flops 34868000 | bytes 2858405 | solution.py:123
  288.0 33.0 %while.155 = (s32[]{:T(128)}, f32[512,128]{1,0:T(8,128)S(1)}, s32[]{:T(128)}, s32[32]{0:T(128)S(1)}, s32[4,32]{0,1:T(8,128)S(1)}, /*index=5*/s32[]{:T(128)}, f32...) while((s32[]{:T(128)}, f32[512,128]{1,0:T(8,128)S(1)}, ...), condition=%wide.region_9.10_spmd.clone, body=%wide.region_8.9_spmd.clone.sunk | while | flops 34277156 | bytes 4927917 | solution.py:136
  322.1 58.1 %while.156 = (s32[]{:T(128)}, f32[512,128]{1,0:T(8,128)S(1)}, f32[32,128,2,1,128]{4,1,2,0,3:T(8,128)}, s32[]{:T(128)}, s32[32]{0:T(128)S(1)}, /*index=5*/s32[4,3...) while((s32[]{:T(128)}, f32[512,128]{1,0:T(8,128)S(1)}, ...), condition=%wide.region_14.15_spmd.clone, body=%wide.region_11.14_spmd.clone.sunk | while | flops 136087360 | bytes 5133853 | solution.py:165
  392.4 17.8 %while.154 = (s32[]{:T(128)}, f32[512]{0:T(512)S(1)}, f32[512]{0:T(512)S(1)}, f32[16,512,256]{1,2,0:T(8,128)}, s32[]{:T(128)}, /*index=5*/s32[32]{0:T(128)S(1)},...) while((s32[]{:T(128)}, f32[512]{0:T(512)S(1)}, ...), condition=%wide.region_7.8_spmd.clone, body=%wide.region_4.7_spmd.clone.sunk | while | flops 34868000 | bytes 2858405 | solution.py:123
  414.9 33.0 %while.155 = (s32[]{:T(128)}, f32[512,128]{1,0:T(8,128)S(1)}, s32[]{:T(128)}, s32[32]{0:T(128)S(1)}, s32[4,32]{0,1:T(8,128)S(1)}, /*index=5*/s32[]{:T(128)}, f32...) while((s32[]{:T(128)}, f32[512,128]{1,0:T(8,128)S(1)}, ...), condition=%wide.region_9.10_spmd.clone, body=%wide.region_8.9_spmd.clone.sunk | while | flops 34277156 | bytes 4927917 | solution.py:136
  449.1 58.1 %while.156 = (s32[]{:T(128)}, f32[512,128]{1,0:T(8,128)S(1)}, f32[32,128,2,1,128]{4,1,2,0,3:T(8,128)}, s32[]{:T(128)}, s32[32]{0:T(128)S(1)}, /*index=5*/s32[4,3...) while((s32[]{:T(128)}, f32[512,128]{1,0:T(8,128)S(1)}, ...), condition=%wide.region_14.15_spmd.clone, body=%wide.region_11.14_spmd.clone.sunk | while | flops 136087360 | bytes 5133853 | solution.py:165
  519.3 24.8 %while.154 = (s32[]{:T(128)}, f32[512]{0:T(512)S(1)}, f32[512]{0:T(512)S(1)}, f32[16,512,256]{1,2,0:T(8,128)}, s32[]{:T(128)}, /*index=5*/s32[32]{0:T(128)S(1)},...) while((s32[]{:T(128)}, f32[512]{0:T(512)S(1)}, ...), condition=%wide.region_7.8_spmd.clone, body=%wide.region_4.7_spmd.clone.sunk | while | flops 34868000 | bytes 2858405 | solution.py:123
  549.0 46.2 %while.155 = (s32[]{:T(128)}, f32[512,128]{1,0:T(8,128)S(1)}, s32[]{:T(128)}, s32[32]{0:T(128)S(1)}, s32[4,32]{0,1:T(8,128)S(1)}, /*index=5*/s32[]{:T(128)}, f32...) while((s32[]{:T(128)}, f32[512,128]{1,0:T(8,128)S(1)}, ...), condition=%wide.region_9.10_spmd.clone, body=%wide.region_8.9_spmd.clone.sunk | while | flops 34277156 | bytes 4927917 | solution.py:136
  596.3 81.4 %while.156 = (s32[]{:T(128)}, f32[512,128]{1,0:T(8,128)S(1)}, f32[32,128,2,1,128]{4,1,2,0,3:T(8,128)}, s32[]{:T(128)}, s32[32]{0:T(128)S(1)}, /*index=5*/s32[4,3...) while((s32[]{:T(128)}, f32[512,128]{1,0:T(8,128)S(1)}, ...), condition=%wide.region_14.15_spmd.clone, body=%wide.region_11.14_spmd.clone.sunk | while | flops 136087360 | bytes 5133853 | solution.py:165
  689.8 24.8 %while.154 = (s32[]{:T(128)}, f32[512]{0:T(512)S(1)}, f32[512]{0:T(512)S(1)}, f32[16,512,256]{1,2,0:T(8,128)}, s32[]{:T(128)}, /*index=5*/s32[32]{0:T(128)S(1)},...) while((s32[]{:T(128)}, f32[512]{0:T(512)S(1)}, ...), condition=%wide.region_7.8_spmd.clone, body=%wide.region_4.7_spmd.clone.sunk | while | flops 34868000 | bytes 2858405 | solution.py:123
  719.5 46.2 %while.155 = (s32[]{:T(128)}, f32[512,128]{1,0:T(8,128)S(1)}, s32[]{:T(128)}, s32[32]{0:T(128)S(1)}, s32[4,32]{0,1:T(8,128)S(1)}, /*index=5*/s32[]{:T(128)}, f32...) while((s32[]{:T(128)}, f32[512,128]{1,0:T(8,128)S(1)}, ...), condition=%wide.region_9.10_spmd.clone, body=%wide.region_8.9_spmd.clone.sunk | while | flops 34277156 | bytes 4927917 | solution.py:136
  766.8 81.4 %while.156 = (s32[]{:T(128)}, f32[512,128]{1,0:T(8,128)S(1)}, f32[32,128,2,1,128]{4,1,2,0,3:T(8,128)}, s32[]{:T(128)}, s32[32]{0:T(128)S(1)}, /*index=5*/s32[4,3...) while((s32[]{:T(128)}, f32[512,128]{1,0:T(8,128)S(1)}, ...), condition=%wide.region_14.15_spmd.clone, body=%wide.region_11.14_spmd.clone.sunk | while | flops 136087360 | bytes 5133853 | solution.py:165
  860.3 28.4 %while.154 = (s32[]{:T(128)}, f32[512]{0:T(512)S(1)}, f32[512]{0:T(512)S(1)}, f32[16,512,256]{1,2,0:T(8,128)}, s32[]{:T(128)}, /*index=5*/s32[32]{0:T(128)S(1)},...) while((s32[]{:T(128)}, f32[512]{0:T(512)S(1)}, ...), condition=%wide.region_7.8_spmd.clone, body=%wide.region_4.7_spmd.clone.sunk | while | flops 34868000 | bytes 2858405 | solution.py:123
  893.6 52.8 %while.155 = (s32[]{:T(128)}, f32[512,128]{1,0:T(8,128)S(1)}, s32[]{:T(128)}, s32[32]{0:T(128)S(1)}, s32[4,32]{0,1:T(8,128)S(1)}, /*index=5*/s32[]{:T(128)}, f32...) while((s32[]{:T(128)}, f32[512,128]{1,0:T(8,128)S(1)}, ...), condition=%wide.region_9.10_spmd.clone, body=%wide.region_8.9_spmd.clone.sunk | while | flops 34277156 | bytes 4927917 | solution.py:136
  947.5 93.0 %while.156 = (s32[]{:T(128)}, f32[512,128]{1,0:T(8,128)S(1)}, f32[32,128,2,1,128]{4,1,2,0,3:T(8,128)}, s32[]{:T(128)}, s32[32]{0:T(128)S(1)}, /*index=5*/s32[4,3...) while((s32[]{:T(128)}, f32[512,128]{1,0:T(8,128)S(1)}, ...), condition=%wide.region_14.15_spmd.clone, body=%wide.region_11.14_spmd.clone.sunk | while | flops 136087360 | bytes 5133853 | solution.py:165
  1052.6 32.0 %while.154 = (s32[]{:T(128)}, f32[512]{0:T(512)S(1)}, f32[512]{0:T(512)S(1)}, f32[16,512,256]{1,2,0:T(8,128)}, s32[]{:T(128)}, /*index=5*/s32[32]{0:T(128)S(1)},...) while((s32[]{:T(128)}, f32[512]{0:T(512)S(1)}, ...), condition=%wide.region_7.8_spmd.clone, body=%wide.region_4.7_spmd.clone.sunk | while | flops 34868000 | bytes 2858405 | solution.py:123
  1089.4 59.4 %while.155 = (s32[]{:T(128)}, f32[512,128]{1,0:T(8,128)S(1)}, s32[]{:T(128)}, s32[32]{0:T(128)S(1)}, s32[4,32]{0,1:T(8,128)S(1)}, /*index=5*/s32[]{:T(128)}, f32...) while((s32[]{:T(128)}, f32[512,128]{1,0:T(8,128)S(1)}, ...), condition=%wide.region_9.10_spmd.clone, body=%wide.region_8.9_spmd.clone.sunk | while | flops 34277156 | bytes 4927917 | solution.py:136
  1149.9 104.6 %while.156 = (s32[]{:T(128)}, f32[512,128]{1,0:T(8,128)S(1)}, f32[32,128,2,1,128]{4,1,2,0,3:T(8,128)}, s32[]{:T(128)}, s32[32]{0:T(128)S(1)}, /*index=5*/s32[4,3...) while((s32[]{:T(128)}, f32[512,128]{1,0:T(8,128)S(1)}, ...), condition=%wide.region_14.15_spmd.clone, body=%wide.region_11.14_spmd.clone.sunk | while | flops 136087360 | bytes 5133853 | solution.py:165
  1259.5 243.4 %all-to-all-start.2 = ((bf16[32,2,8192]{2,1,0:T(2,128)(2,1)}), bf16[32,2,8192]{2,1,0:T(2,128)(2,1)S(1)}, u32[]{:S(2)}, u32[]{:S(2)}) async-start(bf16[32,2,8192]{2,1,0:T(2,128)(2,1)} %reshape.651), calls=%async_computation.2 | async-start | bytes 2097152 | tf_op jit(solution)/shard_map/all_to_all | solution.py:179
  1505.5 18.1 %copy.98 = bf16[4096,1,2,1,128]{4,2,3,1,0:T(2,128)(2,1)} copy(bf16[4096,1,2,1,128]{4,0,2,3,1:T(8,128)(2,1)S(1)} %bitcast.316) | data formatting | bytes 4194304 | tf_op jit(solution)/shard_map/convert_element_type | solution.py:183
  1523.6 7.4 all-to-all-start.3
  1531.7 123.8 %psum.7 = f32[32]{0:T(128)S(1)} all-reduce(f32[32]{0:T(128)S(1)} %scatter_custom_fusion.2), channel_id=1, replica_groups=mesh['dp'=16,'ctx'=32] {'dp','ctx'}, use_global_device_ids=true, to_apply=%region_19.21 | all-reduce | flops 32 | bytes 256 | tf_op jit(solution)/shard_map/psum | solution.py:197
  (2454 shorter events, 1168.4 us)
Async XLA Ops:
  6.7 38.5 %all-to-all-start = ((bf16[128,32,2,1,128]{4,0,3,2,1:T(8,128)(2,1)}), bf16[128,32,2,1,128]{4,0,3,2,1:T(8,128)(2,1)S(1)}, u32[]{:S(2)}, u32[]{:S(2)}) async-start(bf16[128,32,2,1,128]{4,0,3,2,1:T(8,128)(2,1)} %copy.89), calls=%async_computation | async-start | bytes 4194304 | tf_op jit(solution)/shard_map/all_to_all | solution.py:56
  45.2 34.7 %all-to-all-start.1 = ((bf16[128,32,2,1,128]{4,0,2,3,1:T(8,128)(2,1)}), bf16[128,32,2,1,128]{4,0,2,3,1:T(8,128)(2,1)}, u32[]{:S(2)}, u32[]{:S(2)}) async-start(bf16[128,32,2,1,128]{4,0,2,3,1:T(8,128)(2,1)} %copy.93), calls=%async_computation.1 | async-start | bytes 4194304 | tf_op jit(solution)/shard_map/all_to_all | solution.py:55
  53.6 28.1 %copy-start = (bf16[128,32,2,1,128]{4,0,1,2,3:T(8,128)(2,1)S(1)}, bf16[128,32,2,1,128]{4,0,1,2,3:T(8,128)(2,1)}, u32[]{:S(2)}) copy-start(bf16[128,32,2,1,128]{4,0,1,2,3:T(8,128)(2,1)} %copy.90) | copy-start | bytes 6291460
  1259.5 264.1 %all-to-all-start.2 = ((bf16[32,2,8192]{2,1,0:T(2,128)(2,1)}), bf16[32,2,8192]{2,1,0:T(2,128)(2,1)S(1)}, u32[]{:S(2)}, u32[]{:S(2)}) async-start(bf16[32,2,8192]{2,1,0:T(2,128)(2,1)} %reshape.651), calls=%async_computation.2 | async-start | bytes 2097152 | tf_op jit(solution)/shard_map/all_to_all | solution.py:179
  1523.6 136.3 %all-to-all-start.3 = ((bf16[4096,1,2,1,128]{4,2,3,1,0:T(2,128)(2,1)}), bf16[4096,1,2,1,128]{4,2,3,1,0:T(2,128)(2,1)}, u32[]{:S(2)}, u32[]{:S(2)}) async-start(bf16[4096,1,2,1,128]{4,2,3,1,0:T(2,128)(2,1)} %copy.98), calls=%async_computation.3 | async-start | bytes 4194304 | tf_op jit(solution)/shard_map/all_to_all | solution.py:182
where the time goes:
time: 1690 us; the launch traced here: 1670 us
  other arithmetic  528 us (31%)
  local copies, waits for them, and re-layouts  528 us (31%)
  starting transfers between devices  268 us (16%)
  matrix products  124 us (7%)
  blocking collectives  124 us (7%)
  loops' own time  47.7 us (3%)
  waiting for transfers between devices  43.5 us (3%)
    all_to_all x1, starting transfers between devices, body(): lax.all_to_all(dq_all.reshape(seq_len, 1, per_device, HD), 'ctx', split_a...  243 us
    gather x94, local copies, waits for them, and re-layouts, pair_blocks(): values_here = value_blocks[block_index].reshape(2 * BLK, HD)  168 us
    psum x1, blocking collectives, body(): z_total = lax.psum(z_full, ('dp', 'ctx'))  124 us
    scatter-add x47, other arithmetic, grad_step(): kv_acc.at[block_index, :, 0, kv_slot].add(key_part.reshape(2, BLK, HD))  99.4 us
    scatter-add x47, other arithmetic, grad_step(): kv_acc.at[block_index, :, 1, kv_slot].add(value_part.reshape(2, BLK, HD))  99.3 us
    lt x141, other arithmetic, pair_blocks(): usable = 2 * pair_pos + jnp.arange(2, dtype=jnp.int32) < active_count  90.1 us
    gather x141, local copies, waits for them, and re-layouts, pair_blocks(): block_on = (rows_mask[:, block_index] > 0) & usable[None, :]  78.6 us
    convert_element_type x47, other arithmetic, out_step(): jnp.where(allowed, jnp.exp(scores - log_norm[:, None]), 0.0)  67.1 us
  transfers between devices with their start and end apart: 4, of which 2 were waited for; matrix products, arithmetic and copies ran while one was open for 2% of the time, Pallas kernels for 0%

commit v1 on v0

v1 whole, which is shorter than its diff:
```python
import functools
import math

import jax
import jax.numpy as jnp
from jax import lax
from jax.experimental import pallas as pl
from jax.experimental.pallas import tpu as pltpu
from jax.sharding import PartitionSpec as P

H = 32
KVH = 8
HD = 128
BLK = 128
GRP = H // KVH

ZLOSS = 0.05
NEG = -1e30
LOG2E = 1.0 / math.log(2.0)
LN2 = math.log(2.0)
SCALE = HD ** (-0.5)

NT = (((1,), (1,)), ((), ()))


def attention_body(
    cols_ref, cnt_ref, steps_ref, edge_ref,
    qd_ref, kv_ref,
    dq_ref, dkv_ref, z_ref,
    e_s, dp_s, m_s, dk_s, dv_s, kt_s, dqt_s, z_s,
):
    row = pl.program_id(0)
    blocks = kv_ref.shape[0]

    @pl.when(row == 0)
    def _():
        dk_s[...] = jnp.zeros_like(dk_s)
        dv_s[...] = jnp.zeros_like(dv_s)
        z_s[...] = jnp.zeros_like(z_s)

        @pl.loop(0, blocks)
        def _(b):
            kt_s[b] = kv_ref[b, :, :HD].astype(jnp.float32).T.astype(jnp.bfloat16)

    qs = [qd_ref[0, :, j * HD : (j + 1) * HD] for j in range(GRP)]
    gs = [qd_ref[0, :, (GRP + j) * HD : (GRP + j + 1) * HD] for j in range(GRP)]
    q_all = jnp.concatenate(qs, axis=0)
    g_all = jnp.concatenate(gs, axis=0)

    def dot(a, b):
        return jnp.dot(a, b, preferred_element_type=jnp.float32)

    def dot_nt(a, b):
        return lax.dot_general(a, b, NT, preferred_element_type=jnp.float32)

    def pair(c1, c2):
        k = jnp.concatenate([kv_ref[c1, :, :HD], kv_ref[c2, :, :HD]], axis=0)
        v = jnp.concatenate([kv_ref[c1, :, HD:], kv_ref[c2, :, HD:]], axis=0)
        return k, v

    diag = edge_ref[row, 0]
    first_bias = jnp.where(edge_ref[row, 1] > 0, NEG, 0.0).astype(jnp.float32)
    k0, v0 = pair(0, diag)
    s_all = dot_nt(k0, q_all) * (SCALE * LOG2E)
    dp_all = dot_nt(v0, g_all)
    key_pos = lax.broadcasted_iota(jnp.int32, (BLK, BLK), 0)
    query_pos = lax.broadcasted_iota(jnp.int32, (BLK, BLK), 1)
    causal = key_pos <= query_pos
    state = []
    for j in range(GRP):
        cut = slice(j * BLK, (j + 1) * BLK)
        s = jnp.concatenate(
            [s_all[:BLK, cut] + first_bias, jnp.where(causal, s_all[BLK:, cut], NEG)], axis=0
        )
        dp = dp_all[:, cut]
        m = jnp.max(s, axis=0, keepdims=True)
        e = jnp.exp2(s - m)
        e_s[0, j] = e
        dp_s[0, j] = dp
        m_s[0, j] = jnp.broadcast_to(m, (8, BLK))
        state += [m, jnp.sum(e, axis=0, keepdims=True), jnp.sum(e * dp, axis=0, keepdims=True)]

    def entry(t, j):
        slot = 2 * (t - 1)
        c1 = cols_ref[row, j * blocks + slot]
        c2 = cols_ref[row, j * blocks + slot + 1]
        return slot, c1, c2

    def forward(t, state):
        out = []
        for j in range(GRP):
            m, l, u = state[3 * j : 3 * j + 3]
            slot, c1, c2 = entry(t, j)
            n = cnt_ref[row, j]
            b1 = jnp.where(slot < n, 0.0, NEG).astype(jnp.float32)
            b2 = jnp.where(slot + 1 < n, 0.0, NEG).astype(jnp.float32)
            k, v = pair(c1, c2)
            s = dot_nt(k, qs[j]) * (SCALE * LOG2E)
            s = jnp.concatenate([s[:BLK] + b1, s[BLK:] + b2], axis=0)
            dp = dot_nt(v, gs[j])
            m_new = jnp.maximum(m, jnp.max(s, axis=0, keepdims=True))
            e = jnp.exp2(s - m_new)
            alpha = jnp.exp2(m - m_new)
            e_s[t, j] = e
            dp_s[t, j] = dp
            m_s[t, j] = jnp.broadcast_to(m_new, (8, BLK))
            out += [
                m_new,
                l * alpha + jnp.sum(e, axis=0, keepdims=True),
                u * alpha + jnp.sum(e * dp, axis=0, keepdims=True),
            ]
        return tuple(out)

    steps = steps_ref[row, 0]
    state = lax.fori_loop(1, steps, forward, tuple(state))

    top, inv, pull = [], [], []
    for j in range(GRP):
        m, l, u = state[3 * j : 3 * j + 3]
        inv_l = 1.0 / l
        log_norm = m * LN2 + jnp.log(l)
        top.append(m)
        inv.append(inv_l)
        pull.append((2.0 * ZLOSS) * log_norm - u * inv_l)
        z_s[j : j + 1, :] += log_norm * log_norm

    def weights(t, j):
        factor = jnp.exp2(m_s[t, j][:1] - top[j]) * inv[j]
        probs = e_s[t, j] * factor
        dscore = probs * (dp_s[t, j] + pull[j])
        return probs.astype(jnp.bfloat16), dscore.astype(jnp.bfloat16)

    first = [weights(0, j) for j in range(GRP)]
    p_all = jnp.concatenate([w[0] for w in first], axis=1)
    d_all = jnp.concatenate([w[1] for w in first], axis=1)
    dk = dot(d_all, q_all)
    dv = dot(p_all, g_all)
    dk_s[0] += dk[:BLK]
    dv_s[0] += dv[:BLK]
    dk_s[diag] += dk[BLK:]
    dv_s[diag] += dv[BLK:]
    kt = jnp.concatenate([kt_s[0], kt_s[diag]], axis=1)
    dqt = dot(kt, d_all)
    for j in range(GRP):
        dqt_s[j] = dqt[:, j * BLK : (j + 1) * BLK]

    @pl.loop(1, steps)
    def _(t):
        for j in range(GRP):
            _, c1, c2 = entry(t, j)
            p_low, d_low = weights(t, j)
            dk = dot(d_low, qs[j])
            dv = dot(p_low, gs[j])
            kt = jnp.concatenate([kt_s[c1], kt_s[c2]], axis=1)
            dqt_s[j] += dot(kt, d_low)
            dk_s[c1] += dk[:BLK]
            dv_s[c1] += dv[:BLK]
            dk_s[c2] += dk[BLK:]
            dv_s[c2] += dv[BLK:]

    for j in range(GRP):
        dq_ref[0, :, j * HD : (j + 1) * HD] = (dqt_s[j] * SCALE).T.astype(jnp.bfloat16)

    @pl.when(row == pl.num_programs(0) - 1)
    def _():
        dkv_ref[:, :, :HD] = (dk_s[...] * SCALE).astype(jnp.bfloat16)
        dkv_ref[:, :, HD:] = dv_s[...].astype(jnp.bfloat16)
        z_ref[...] = z_s[...]


def attention(qd, kv, cols, cnt, steps, edge):
    rows = qd.shape[0]
    blocks = kv.shape[0]
    max_steps = blocks // 2
    return pl.pallas_call(
        attention_body,
        out_shape=(
            jax.ShapeDtypeStruct((rows, BLK, GRP * HD), jnp.bfloat16),
            jax.ShapeDtypeStruct((blocks, BLK, 2 * HD), jnp.bfloat16),
            jax.ShapeDtypeStruct((8, BLK), jnp.float32),
        ),
        grid_spec=pltpu.PrefetchScalarGridSpec(
            num_scalar_prefetch=4,
            grid=(rows,),
            in_specs=[
                pl.BlockSpec((1, BLK, 2 * GRP * HD), lambda i, *_: (i, 0, 0)),
                pl.BlockSpec((blocks, BLK, 2 * HD), lambda i, *_: (0, 0, 0)),
            ],
            out_specs=[
                pl.BlockSpec((1, BLK, GRP * HD), lambda i, *_: (i, 0, 0)),
                pl.BlockSpec((blocks, BLK, 2 * HD), lambda i, *_: (0, 0, 0)),
                pl.BlockSpec((8, BLK), lambda i, *_: (0, 0)),
            ],
            scratch_shapes=[
                pltpu.VMEM((max_steps, GRP, 2 * BLK, BLK), jnp.float32),
                pltpu.VMEM((max_steps, GRP, 2 * BLK, BLK), jnp.float32),
                pltpu.VMEM((max_steps, GRP, 8, BLK), jnp.float32),
                pltpu.VMEM((blocks, BLK, HD), jnp.float32),
                pltpu.VMEM((blocks, BLK, HD), jnp.float32),
                pltpu.VMEM((blocks, HD, BLK), jnp.bfloat16),
                pltpu.VMEM((GRP, HD, BLK), jnp.float32),
                pltpu.VMEM((8, BLK), jnp.float32),
            ],
        ),
        compiler_params=pltpu.CompilerParams(
            dimension_semantics=("arbitrary",), vmem_limit_bytes=44 << 20
        ),
        cost_estimate=pl.CostEstimate(
            flops=40_000_000_000, transcendentals=4_000_000, bytes_accessed=9_000_000
        ),
        name="block_attention",
    )(cols, cnt, steps, edge, qd, kv)


def work_lists(mask, part, parts):
    rows, blocks = mask.shape[1:]
    mask = jnp.transpose(mask, (1, 0, 2))
    col = jnp.arange(blocks, dtype=jnp.int32)
    own = jnp.arange(rows, dtype=jnp.int32) * parts + part
    other = (mask > 0) & (col > 0)[None, None, :] & (col[None, :] != own[:, None])[:, None, :]
    other = other.astype(jnp.int32)
    before = (col[None, :] < col[:, None]).astype(jnp.int32)
    rank = jnp.sum(other[:, :, None, :] * before[None, None], axis=3)
    place = (col % parts) * rows + col // parts
    hit = (rank[:, :, None, :] == col[None, None, :, None]) & (other[:, :, None, :] > 0)
    cols = jnp.sum(jnp.where(hit, place[None, None, None, :], 0), axis=3)
    cnt = jnp.sum(other, axis=2)
    steps = 1 + (jnp.max(cnt, axis=1) + 1) // 2
    edge = jnp.stack([part * rows + jnp.arange(rows, dtype=jnp.int32), (own == 0).astype(jnp.int32)], axis=1)
    return cols.reshape(rows, GRP * blocks), cnt, steps[:, None], edge


def body(queries, keys, values, out_grad, block_mask):
    tok = queries.shape[1]
    ctx = lax.axis_size("ctx")
    dps = lax.axis_size("dp")
    parts = ctx // KVH
    blocks = block_mask.shape[1]
    rows = blocks // parts
    me = lax.axis_index("ctx")
    kv_head, part = me // parts, me % parts
    spread = [[u * parts + r for u in range(KVH)] for r in range(parts)]
    quad = [[u * parts + r for r in range(parts)] for u in range(KVH)]
    wide = [[d * ctx + u * parts + r for d in range(dps) for r in range(parts)] for u in range(KVH)]

    def heads_first(*arrays):
        return jnp.concatenate([a[0].reshape(tok, KVH, -1) for a in arrays], axis=2).transpose(1, 0, 2)

    def exchange(a):
        return lax.all_to_all(a, "ctx", 0, 0, axis_index_groups=spread, tiled=True)

    kv_part = exchange(heads_first(keys, values))
    kv = lax.all_gather(kv_part, "ctx", axis=0, axis_index_groups=quad, tiled=True)
    qd = exchange(heads_first(queries, out_grad))

    mask = lax.dynamic_slice(
        block_mask.reshape(H, rows, parts, blocks), (kv_head * GRP, 0, part, 0), (GRP, rows, 1, blocks)
    )[:, :, 0]
    cols, cnt, steps, edge = work_lists(mask, part, parts)
    dq, dkv, z = attention(qd, kv, cols, cnt, steps, edge)

    z_send = jnp.tile(z[:GRP], (dps, 1))
    z_back = lax.all_to_all(z_send, ("dp", "ctx"), 0, 0, axis_index_groups=wide, tiled=True)
    dkv_part = lax.psum_scatter(dkv, "ctx", scatter_dimension=0, axis_index_groups=quad, tiled=True)
    query_grad = exchange(dq).transpose(1, 0, 2).reshape(1, tok, H * HD)
    dkv_back = exchange(dkv_part).transpose(1, 0, 2)
    key_grad = dkv_back[:, :, :HD].reshape(1, tok, KVH * HD)
    value_grad = dkv_back[:, :, HD:].reshape(1, tok, KVH * HD)
    z_own = jnp.sum(z_back)[None] * (ZLOSS / (dps * blocks * BLK))
    return query_grad, key_grad, value_grad, z_own


def solution(mesh):
    return jax.shard_map(
        body,
        mesh=mesh,
        in_specs=(
            P("dp", "ctx", None),
            P("dp", "ctx", None),
            P("dp", "ctx", None),
            P("dp", "ctx", None),
            P(),
        ),
        out_specs=(P("dp", "ctx", None), P("dp", "ctx", None), P("dp", "ctx", None), P("ctx")),
        check_vma=False,
    )
```

time: 1690 us -> 189 us (0.11); the launches traced: 1670 us -> 188 us
  other arithmetic: 528 us -> 5.13 us
  local copies, waits for them, and re-layouts: 528 us -> 16.7 us
  starting transfers between devices: 268 us -> 7.17 us
  matrix products: 124 us -> 0 us
  blocking collectives: 124 us -> 75.5 us
  loops' own time: 47.7 us -> 0 us
  Pallas kernels: 0 us -> 20 us
    gather x331 -> x0, local copies, waits for them, and re-layouts: 301 us -> none  [the longest x94 168 us: pair_blocks(): values_here = value_blocks[block_index].reshape(2 * BLK, HD)]
    all_to_all x4 -> x2, starting transfers between devices: 268 us -> 7.09 us  [exchange(): return lax.all_to_all(a, 'ctx', 0, 0, axis_index_groups=spread, tiled=True)]
    scatter-add x95 -> x0, other arithmetic: 199 us -> none  [the longest x47 99.4 us: grad_step(): kv_acc.at[block_index, :, 0, kv_slot].add(key_part.reshape(2, BLK, HD))]
    convert_element_type x94 -> x2, other arithmetic: 125 us -> 0.01 us  [the longest x1 0.01 us: work_lists(): before = (col[None, :] < col[:, None]).astype(jnp.int32)]
    psum x1 -> x0, blocking collectives: 124 us -> none  [body(): z_total = lax.psum(z_full, ('dp', 'ctx'))]
    dot_general x283 -> x0, matrix products: 124 us -> none  [the longest x47 63.8 us: grad_step(): jnp.einsum('qd,kd->qk', g_tile, values_here, preferred_element_type=jnp.f...]
    lt x141 -> x0, other arithmetic: 90.1 us -> none  [pair_blocks(): usable = 2 * pair_pos + jnp.arange(2, dtype=jnp.int32) < active_count]
    all_to_all x0 -> x3, blocking collectives: none -> 75.5 us  [the longest x2 41.7 us: exchange(): return lax.all_to_all(a, 'ctx', 0, 0, axis_index_groups=spread, tiled=True)]
  transfers between devices with their start and end apart: 4 -> 4, of which waited for: 2 -> 3; matrix products, arithmetic and copies ran while one was open for 2% -> 7% of each run, Pallas kernels for 0% -> 0%
where the time goes in v1:
time: 189 us; the launch traced here: 188 us
  blocking collectives  75.5 us (40%)
  waiting for transfers between devices  47.6 us (25%)
  Pallas kernels  20 us (11%)
  local copies, waits for them, and re-layouts  16.7 us (9%)
  between operations  16 us (8%)
  starting transfers between devices  7.17 us (4%)
  other arithmetic  5.13 us (3%)
    all_to_all x2, blocking collectives, exchange(): return lax.all_to_all(a, 'ctx', 0, 0, axis_index_groups=spread, tiled=True)  41.7 us
    all_to_all x2, waiting for transfers between devices, exchange(): return lax.all_to_all(a, 'ctx', 0, 0, axis_index_groups=spread, tiled=True)  39.6 us
    all_to_all x1, blocking collectives, body(): lax.all_to_all(z_send, ('dp', 'ctx'), 0, 0, axis_index_groups=wide, tiled...  33.8 us
    pallas_call x1, Pallas kernels, attention(): pl.pallas_call(attention_body, out_shape=(jax.ShapeDtypeStruct((rows, BLK...  20 us
    unnamed x17, local copies, waits for them, and re-layouts  12.5 us
    all_gather x1, waiting for transfers between devices, body(): lax.all_gather(kv_part, 'ctx', axis=0, axis_index_groups=quad, tiled=True)  7.99 us
    all_to_all x2, starting transfers between devices, exchange(): return lax.all_to_all(a, 'ctx', 0, 0, axis_index_groups=spread, tiled=True)  7.09 us
  transfers between devices with their start and end apart: 4, of which 3 were waited for; matrix products, arithmetic and copies ran while one was open for 7% of the time, Pallas kernels for 0%

profile of v1, /device:TPU:1, one launch (start us, length us, event | category | flops | bytes accessed | tf_op | source)
XLA Modules:
  0.0 188.2 jit_solution(6142963700519553212)
XLA Ops:
  7.2 1.2 copy.115
  8.4 1.1 copy.116
  9.6 16.7 %all_to_all.29 = bf16[8,128,256]{1,2,0:T(8,128)(2,1)S(1)} all-to-all(bf16[8,128,256]{1,2,0:T(8,128)(2,1)S(1)} %maximum_bitcast_fusion.1), channel_id=1, replica_groups={{0,4,8,12,16,20,24,28},{1,5,9,13,17,21,25,29},{2,6,10,14,18,22,26,30},{..., dimensions={0} | all-to-all | bytes 1048576 | tf_op jit(solution)/shard_map/all_to_all | solution.py:250
  26.2 1.0 copy.117
  27.3 1.6 copy.111
  28.9 0.5 copy.113
  29.4 1.6 copy.112
  31.1 1.3 copy.114
  32.4 2.8 %maximum_bitcast_fusion = bf16[8,128,1024]{2,1,0:T(8,128)(2,1)} fusion(bf16[128,8,512]{2,0,1:T(8,128)(2,1)} %copy.114, bf16[128,8,512]{2,0,1:T(8,128)(2,1)S(1)} %copy.113), kind=kLoop, calls=%fused_computation | loop fusion | flops 4194304 | bytes 4194304 | tf_op jit(solution)/shard_map/transpose | solution.py:247
  35.1 3.6 %all-to-all-start = ((bf16[8,128,1024]{2,1,0:T(8,128)(2,1)}), bf16[8,128,1024]{2,1,0:T(8,128)(2,1)S(1)}, u32[]{:S(2)}, u32[]{:S(2)}) async-start(bf16[8,128,1024]{2,1,0:T(8,128)(2,1)} %maximum_bitcast_fusion), calls=%async_computation | async-start | bytes 4194304 | tf_op jit(solution)/shard_map/all_to_all | solution.py:250
  38.9 0.1 fusion.9
  39.1 0.1 copy.118.cnt_ref
  39.4 0.6 multiply_reduce_fusion
  40.0 0.6 select_reduce_fusion
  40.8 32.5 %all-to-all-done.qd_ref = bf16[8,128,1024]{2,1,0:T(8,128)(2,1)S(1)} async-done(((bf16[8,128,1024]{2,1,0:T(8,128)(2,1)}), bf16[8,128,1024]{2,1,0:T(8,128)(2,1)S(1)}, u32[]{:S(2)}, u32[]{:S(2)}) %all-to-all-start) | async-done | bytes 2097184 | tf_op jit(solution)/shard_map/all_to_all | solution.py:250
  73.3 8.0 %all-gather.2.cloned.1.call-done.kv_ref = bf16[32,128,256]{2,1,0:T(8,128)(2,1)} async-done(((bf16[8,128,256]{2,1,0:T(8,128)(2,1)}), bf16[32,128,256]{2,1,0:T(8,128)(2,1)}) %all-gather.2.cloned.1.call-update) | async-done | bytes 2097168 | tf_op jit(solution)/shard_map/all_gather | solution.py:253
  81.3 1.6 copy-done.4
  82.9 20.0 %block_attention.1 = (bf16[8,128,512]{2,1,0:T(8,128)(2,1)S(1)}, bf16[32,128,256]{2,1,0:T(8,128)(2,1)S(1)}, f32[8,128]{1,0:T(8,128)S(1)}) custom-call(s32[8,128]{1,0:T(8,128)S(1)} %reshape.177.cols_ref, s32[8,4]{1,0:T(8,128)S(1)} %copy.118.cnt_ref, s32[8,1]{1,0:T(8,128)S(1)} %fusion.4.steps_ref, s32[8,2]{1,0:T(8,128)S(1)} %pad_add_fusion.edge_ref, ...), custom_call_target="tpu_custom_call" | custom-call | flops 40000000000 | bytes 9000000 | tf_op jit(solution)/shard_map/block_attention/pallas_call | solution.py:175
  102.9 1.3 copy-done.1
  104.3 1.0 copy-done.2
  105.3 33.8 %all_to_all.30 = f32[64,1,128]{2,1,0:T(1,128)S(1)} all-to-all(f32[64,1,128]{2,1,0:T(1,128)S(1)} %bitcast.39), channel_id=1, replica_groups={{0,1,2,3,32,33,34,35,64,65,66,67,96,97,98,99,128,129,130,131,160,161,16..., dimensions={0} | all-to-all | bytes 65536 | tf_op jit(solution)/shard_map/all_to_all | solution.py:263
  139.0 25.0 %all_to_all.31 = bf16[8,128,512]{2,1,0:T(8,128)(2,1)S(1)} all-to-all(bf16[8,128,512]{2,1,0:T(8,128)(2,1)S(1)} %copy-done.3), channel_id=1, replica_groups={{0,4,8,12,16,20,24,28},{1,5,9,13,17,21,25,29},{2,6,10,14,18,22,26,30},{..., dimensions={0} | all-to-all | bytes 2097152 | tf_op jit(solution)/shard_map/all_to_all | solution.py:250
  164.1 3.5 %all-to-all-start.3 = ((bf16[8,128,256]{2,1,0:T(8,128)(2,1)}), bf16[8,128,256]{2,1,0:T(8,128)(2,1)S(1)}, u32[]{:S(2)}, u32[]{:S(2)}) async-start(bf16[8,128,256]{2,1,0:T(8,128)(2,1)} %reduce-scatter.2.cloned.1.call-done), calls=%async_computation.4 | async-start | bytes 1048576 | tf_op jit(solution)/shard_map/all_to_all | solution.py:250
  167.6 0.7 reduce_sum.39
  168.9 0.7 copy.119
  169.6 1.3 copy.122
  170.9 7.1 %all-to-all-done.3 = bf16[8,128,256]{2,1,0:T(8,128)(2,1)S(1)} async-done(((bf16[8,128,256]{2,1,0:T(8,128)(2,1)}), bf16[8,128,256]{2,1,0:T(8,128)(2,1)S(1)}, u32[]{:S(2)}, u32[]{:S(2)}) %all-to-all-start.3) | async-done | bytes 524320 | tf_op jit(solution)/shard_map/all_to_all | solution.py:250
  178.0 0.1 fusion.10
  178.1 0.2 copy.121
  178.3 0.9 copy.124
  179.2 0.2 copy.120
  179.4 0.9 copy.123
  (32 shorter events, 0.6 us)
Async XLA Ops:
  7.2 31.8 %copy-start = (s32[32,32,32]{2,1,0:T(8,128)S(1)}, s32[32,32,32]{2,1,0:T(8,128)}, u32[]{:S(2)}) copy-start(s32[32,32,32]{2,1,0:T(8,128)} %param.9) | copy-start | bytes 393220
  7.2 74.1 %all-gather.2.cloned.1.call-start = ((), (), s32[]{:S(2)}) async-start(), calls=%async_computation.6 | async-start | bytes 2621440 | tf_op jit(solution)/shard_map/all_gather | solution.py:253
  35.1 38.2 %all-to-all-start = ((bf16[8,128,1024]{2,1,0:T(8,128)(2,1)}), bf16[8,128,1024]{2,1,0:T(8,128)(2,1)S(1)}, u32[]{:S(2)}, u32[]{:S(2)}) async-start(bf16[8,128,1024]{2,1,0:T(8,128)(2,1)} %maximum_bitcast_fusion), calls=%async_computation | async-start | bytes 4194304 | tf_op jit(solution)/shard_map/all_to_all | solution.py:250
  38.8 125.3 %reduce-scatter.2.cloned.1.call-start = ((), (), s32[]{:S(2)}) async-start(), calls=%async_computation.7 | async-start | bytes 2621440 | tf_op jit(solution)/shard_map/reduce_scatter | solution.py:264
  81.3 1.6 copy-start.4
  102.9 1.3 copy-start.1
  104.3 1.0 copy-start.2
  105.2 33.8 %copy-start.3 = (bf16[8,128,512]{2,1,0:T(8,128)(2,1)S(1)}, bf16[8,128,512]{2,1,0:T(8,128)(2,1)}, u32[]{:S(2)}) copy-start(bf16[8,128,512]{2,1,0:T(8,128)(2,1)} %copy-done.2) | copy-start | bytes 3145732
  164.1 13.9 %all-to-all-start.3 = ((bf16[8,128,256]{2,1,0:T(8,128)(2,1)}), bf16[8,128,256]{2,1,0:T(8,128)(2,1)S(1)}, u32[]{:S(2)}, u32[]{:S(2)}) async-start(bf16[8,128,256]{2,1,0:T(8,128)(2,1)} %reduce-scatter.2.cloned.1.call-done), calls=%async_computation.4 | async-start | bytes 1048576 | tf_op jit(solution)/shard_map/all_to_all | solution.py:250
Sparse Core Ops, SparseCore 0:
  27.4 53.8 all-gather.1
  105.4 48.0 reduce-scatter.1

commit v2 on v1

--- a/solution.py
+++ b/solution.py
@@ -1,4 +1,3 @@
-import functools
 import math
 
 import jax
@@ -13,6 +12,7 @@
 HD = 128
 BLK = 128
 GRP = H // KVH
+PARTS = 4
 
 ZLOSS = 0.05
 NEG = -1e30
@@ -203,7 +203,7 @@
             ],
         ),
         compiler_params=pltpu.CompilerParams(
-            dimension_semantics=("arbitrary",), vmem_limit_bytes=44 << 20
+            dimension_semantics=("arbitrary",), vmem_limit_bytes=58 << 20
         ),
         cost_estimate=pl.CostEstimate(
             flops=40_000_000_000, transcendentals=4_000_000, bytes_accessed=9_000_000
@@ -212,61 +212,125 @@
     )(cols, cnt, steps, edge, qd, kv)
 
 
-def work_lists(mask, part, parts):
-    rows, blocks = mask.shape[1:]
+def pack_body(a_ref, b_ref, out_ref, hold, in_sem, out_sem):
+    heads = out_ref.shape[0]
+    width = out_ref.shape[2] // 2
+    loads = [
+        [
+            pltpu.make_async_copy(
+                ref.at[0, :, pl.ds(u * width, width)],
+                hold.at[u, :, pl.ds(n * width, width)],
+                in_sem.at[n, u],
+            )
+            for n, ref in enumerate((a_ref, b_ref))
+        ]
+        for u in range(heads)
+    ]
+    stores = [pltpu.make_async_copy(hold.at[u], out_ref.at[u], out_sem.at[u]) for u in range(heads)]
+    for both in loads:
+        for copy in both:
+            copy.start()
+    for u in range(heads):
+        for copy in loads[u]:
+            copy.wait()
+        stores[u].start()
+    for copy in stores:
+        copy.wait()
+
+
+def pack(a, b):
+    tok = a.shape[1]
+    shape = (KVH, tok, 2 * a.shape[2] // KVH)
+    return pl.pallas_call(
+        pack_body,
+        out_shape=jax.ShapeDtypeStruct(shape, a.dtype),
+        in_specs=[pl.BlockSpec(memory_space=pl.ANY)] * 2,
+        out_specs=pl.BlockSpec(memory_space=pl.ANY),
+        scratch_shapes=[
+            pltpu.VMEM(shape, a.dtype),
+            pltpu.SemaphoreType.DMA((2, KVH)),
+            pltpu.SemaphoreType.DMA((KVH,)),
+        ],
+        cost_estimate=pl.CostEstimate(flops=0, transcendentals=0, bytes_accessed=8 * a.size),
+        name="pack",
+    )(a, b)
+
+
+def block_of(part, i):
+    return (i // 2) * (2 * PARTS) + 2 * part + i % 2
+
+
+def work_lists(mask, part):
+    blocks = mask.shape[2]
+    rows = blocks // PARTS
+    mask = mask.reshape(GRP, rows // 2, PARTS, 2, blocks)
+    mask = lax.dynamic_index_in_dim(mask, part, axis=2, keepdims=False).reshape(GRP, rows, blocks)
     mask = jnp.transpose(mask, (1, 0, 2))
     col = jnp.arange(blocks, dtype=jnp.int32)
-    own = jnp.arange(rows, dtype=jnp.int32) * parts + part
+    row = jnp.arange(rows, dtype=jnp.int32)
+    own = block_of(part, row)
     other = (mask > 0) & (col > 0)[None, None, :] & (col[None, :] != own[:, None])[:, None, :]
     other = other.astype(jnp.int32)
     before = (col[None, :] < col[:, None]).astype(jnp.int32)
     rank = jnp.sum(other[:, :, None, :] * before[None, None], axis=3)
-    place = (col % parts) * rows + col // parts
+    place = (col // 2 % PARTS) * rows + col // (2 * PARTS) * 2 + col % 2
     hit = (rank[:, :, None, :] == col[None, None, :, None]) & (other[:, :, None, :] > 0)
     cols = jnp.sum(jnp.where(hit, place[None, None, None, :], 0), axis=3)
     cnt = jnp.sum(other, axis=2)
     steps = 1 + (jnp.max(cnt, axis=1) + 1) // 2
-    edge = jnp.stack([part * rows + jnp.arange(rows, dtype=jnp.int32), (own == 0).astype(jnp.int32)], axis=1)
+    edge = jnp.stack([part * rows + row, (own == 0).astype(jnp.int32)], axis=1)
     return cols.reshape(rows, GRP * blocks), cnt, steps[:, None], edge
 
 
 def body(queries, keys, values, out_grad, block_mask):
     tok = queries.shape[1]
-    ctx = lax.axis_size("ctx")
     dps = lax.axis_size("dp")
-    parts = ctx // KVH
     blocks = block_mask.shape[1]
-    rows = blocks // parts
     me = lax.axis_index("ctx")
-    kv_head, part = me // parts, me % parts
-    spread = [[u * parts + r for u in range(KVH)] for r in range(parts)]
-    quad = [[u * parts + r for r in range(parts)] for u in range(KVH)]
-    wide = [[d * ctx + u * parts + r for d in range(dps) for r in range(parts)] for u in range(KVH)]
-
-    def heads_first(*arrays):
-        return jnp.concatenate([a[0].reshape(tok, KVH, -1) for a in arrays], axis=2).transpose(1, 0, 2)
+
+    def at(u, x):
+        return (u // 2 * PARTS + x) * 2 + u % 2
+
+    part = me // 2 % PARTS
+    core = me % 2
+    kv_head = me // (2 * PARTS) * 2 + core
+    column = [[at(u, x) for u in range(KVH)] for x in range(PARTS)]
+    ring = [[at(u, x) for x in range(PARTS)] for u in range(KVH)]
+    wide = [[d * PARTS * KVH + at(u, x) for d in range(dps) for x in range(PARTS)] for u in range(KVH)]
 
     def exchange(a):
-        return lax.all_to_all(a, "ctx", 0, 0, axis_index_groups=spread, tiled=True)
-
-    kv_part = exchange(heads_first(keys, values))
-    kv = lax.all_gather(kv_part, "ctx", axis=0, axis_index_groups=quad, tiled=True)
-    qd = exchange(heads_first(queries, out_grad))
-
-    mask = lax.dynamic_slice(
-        block_mask.reshape(H, rows, parts, blocks), (kv_head * GRP, 0, part, 0), (GRP, rows, 1, blocks)
-    )[:, :, 0]
-    cols, cnt, steps, edge = work_lists(mask, part, parts)
+        return lax.all_to_all(a, "ctx", 0, 0, axis_index_groups=column, tiled=True)
+
+    kv_part = exchange(pack(keys, values))
+    qd_send = pack(queries, out_grad)
+    kv_part, qd_send = lax.optimization_barrier((kv_part, qd_send))
+    kv = lax.all_gather(kv_part, "ctx", axis=0, axis_index_groups=ring, tiled=True)
+    qd = exchange(qd_send)
+
+    mask = lax.dynamic_slice(block_mask, (kv_head * GRP, 0, 0), (GRP, blocks, blocks))
+    cols, cnt, steps, edge = work_lists(mask, part)
     dq, dkv, z = attention(qd, kv, cols, cnt, steps, edge)
 
-    z_send = jnp.tile(z[:GRP], (dps, 1))
-    z_back = lax.all_to_all(z_send, ("dp", "ctx"), 0, 0, axis_index_groups=wide, tiled=True)
-    dkv_part = lax.psum_scatter(dkv, "ctx", scatter_dimension=0, axis_index_groups=quad, tiled=True)
+    dkv_part = lax.psum_scatter(dkv, "ctx", scatter_dimension=0, axis_index_groups=ring, tiled=True)
     query_grad = exchange(dq).transpose(1, 0, 2).reshape(1, tok, H * HD)
+
+    half = jnp.arange(PARTS, dtype=jnp.int32)
+    z_send = jnp.where(
+        (half // 2 == core)[:, None, None], jnp.tile(z[:GRP].reshape(2, 2, BLK), (2, 1, 1)), 0.0
+    )
+    z_back = lax.all_to_all(
+        jnp.tile(z_send, (dps, 1, 1)), ("dp", "ctx"), 0, 0, axis_index_groups=wide, tiled=True
+    )
+    z_two = jnp.sum(z_back, axis=(0, 2)) * (ZLOSS / (dps * blocks * BLK))
+    z_mine = jnp.where(core == 0, z_two[0], z_two[1])
+    z_mate = jnp.where(core == 0, z_two[1], z_two[0])
+    swap = [(at(u - u % 2 + x // 2, x), at(u - u % 2 + 1 - x // 2, x)) for u in range(0, KVH, 2) for x in range(PARTS)]
+    z_swap = lax.ppermute(z_mate, "ctx", swap)
+    z_own = jnp.where(part // 2 == core, z_mine, z_swap)[None]
+
     dkv_back = exchange(dkv_part).transpose(1, 0, 2)
     key_grad = dkv_back[:, :, :HD].reshape(1, tok, KVH * HD)
     value_grad = dkv_back[:, :, HD:].reshape(1, tok, KVH * HD)
-    z_own = jnp.sum(z_back)[None] * (ZLOSS / (dps * blocks * BLK))
     return query_grad, key_grad, value_grad, z_own
 
 

time: 189 us -> 171 us (0.905)
  blocking collectives: 75.5 us -> 57.2 us
  starting transfers between devices: 7.17 us -> 20.4 us
  waiting for transfers between devices: 47.6 us -> 37.7 us
  local copies, waits for them, and re-layouts: 16.7 us -> 7 us
  Pallas kernels: 20 us -> 26.5 us
  between operations: 16 us -> 18.7 us
    all_to_all x3 -> x2, blocking collectives: 75.5 us -> 57.2 us  [the longest x1 30 us: body(): lax.all_to_all(jnp.tile(z_send, (dps, 1, 1)), ('dp', 'ctx'), 0, 0, axis_i...]
    all_to_all x2 -> x3, starting transfers between devices: 7.09 us -> 19.1 us  [exchange(): return lax.all_to_all(a, 'ctx', 0, 0, axis_index_groups=column, tiled=True)]
    all_to_all x2 -> x3, waiting for transfers between devices: 39.6 us -> 29.9 us  [exchange(): return lax.all_to_all(a, 'ctx', 0, 0, axis_index_groups=column, tiled=True)]
    unnamed x17 -> x15, local copies, waits for them, and re-layouts: 12.5 us -> 4.45 us
    pallas_call x0 -> x2, Pallas kernels: none -> 4.46 us  [pack(): pl.pallas_call(pack_body, out_shape=jax.ShapeDtypeStruct(shape, a.dtype),...]
    transpose x2 -> x0, other arithmetic: 2.81 us -> none  [heads_first(): jnp.concatenate([a[0].reshape(tok, KVH, -1) for a in arrays], axis=2)]
    pallas_call x1, Pallas kernels: 20 us -> 22 us  [attention(): pl.pallas_call(attention_body, out_shape=(jax.ShapeDtypeStruct((rows, BLK...]
    all_gather x1, waiting for transfers between devices: 7.99 us -> 6.08 us  [body(): lax.all_gather(kv_part, 'ctx', axis=0, axis_index_groups=ring, tiled=True)]
  transfers between devices with their start and end apart: 4 -> 6, of which waited for: 3 -> 5; matrix products, arithmetic and copies ran while one was open for 7% -> 4% of each run, Pallas kernels for 0% -> 1%
where the time goes in v2:
time: 171 us
  blocking collectives  57.2 us (33%)
  waiting for transfers between devices  37.7 us (22%)
  Pallas kernels  26.5 us (15%)
  starting transfers between devices  20.4 us (12%)
  between operations  18.7 us (11%)
  local copies, waits for them, and re-layouts  7 us (4%)
  other arithmetic  3.29 us (2%)
    all_to_all x1, blocking collectives, body(): lax.all_to_all(jnp.tile(z_send, (dps, 1, 1)), ('dp', 'ctx'), 0, 0, axis_i...  30 us
    all_to_all x3, waiting for transfers between devices, exchange(): return lax.all_to_all(a, 'ctx', 0, 0, axis_index_groups=column, tiled=True)  29.9 us
    all_to_all x1, blocking collectives, exchange(): return lax.all_to_all(a, 'ctx', 0, 0, axis_index_groups=column, tiled=True)  27.2 us
    pallas_call x1, Pallas kernels, attention(): pl.pallas_call(attention_body, out_shape=(jax.ShapeDtypeStruct((rows, BLK...  22 us
    all_to_all x3, starting transfers between devices, exchange(): return lax.all_to_all(a, 'ctx', 0, 0, axis_index_groups=column, tiled=True)  19.1 us
    all_gather x1, waiting for transfers between devices, body(): lax.all_gather(kv_part, 'ctx', axis=0, axis_index_groups=ring, tiled=True)  6.08 us
    pallas_call x2, Pallas kernels, pack(): pl.pallas_call(pack_body, out_shape=jax.ShapeDtypeStruct(shape, a.dtype),...  4.46 us
    unnamed x15, local copies, waits for them, and re-layouts  4.45 us
  transfers between devices with their start and end apart: 6, of which 5 were waited for; matrix products, arithmetic and copies ran while one was open for 4% of the time, Pallas kernels for 1%

profile of v2, /device:TPU:1, one launch (start us, length us, event | category | flops | bytes accessed | tf_op | source)
XLA Modules:
  0.0 170.8 jit_solution(13508276621466958056)
XLA Ops:
  7.2 1.9 %pack.2 = bf16[8,128,256]{2,1,0:T(8,128)(2,1)} custom-call(bf16[1,128,1024]{2,1,0:T(8,128)(2,1)} %a_ref.2, bf16[1,128,1024]{2,1,0:T(8,128)(2,1)} %b_ref.2), custom_call_target="tpu_custom_call" | custom-call | bytes 1048576 | tf_op jit(solution)/shard_map/pack/pallas_call | solution.py:244
  9.1 10.3 %all-to-all-start = ((bf16[8,128,256]{2,1,0:T(8,128)(2,1)}), bf16[8,128,256]{2,1,0:T(8,128)(2,1)S(1)}, u32[]{:S(2)}, u32[]{:S(2)}) async-start(bf16[8,128,256]{2,1,0:T(8,128)(2,1)} %pack.2), calls=%async_computation | async-start | bytes 1048576 | tf_op jit(solution)/shard_map/all_to_all | solution.py:302
  19.4 2.6 %pack.3 = bf16[8,128,1024]{2,1,0:T(8,128)(2,1)} custom-call(bf16[1,128,4096]{2,1,0:T(8,128)(2,1)} %a_ref.3, bf16[1,128,4096]{2,1,0:T(8,128)(2,1)} %b_ref.3), custom_call_target="tpu_custom_call" | custom-call | bytes 4194304 | tf_op jit(solution)/shard_map/pack/pallas_call | solution.py:244
  21.9 6.9 %all-to-all-done = bf16[8,128,256]{2,1,0:T(8,128)(2,1)S(1)} async-done(((bf16[8,128,256]{2,1,0:T(8,128)(2,1)}), bf16[8,128,256]{2,1,0:T(8,128)(2,1)S(1)}, u32[]{:S(2)}, u32[]{:S(2)}) %all-to-all-start) | async-done | bytes 524320 | tf_op jit(solution)/shard_map/all_to_all | solution.py:302
  28.9 0.8 copy-done.2
  29.8 4.4 %all-to-all-start.1 = ((bf16[8,128,1024]{2,1,0:T(8,128)(2,1)}), bf16[8,128,1024]{2,1,0:T(8,128)(2,1)S(1)}, u32[]{:S(2)}, u32[]{:S(2)}) async-start(bf16[8,128,1024]{2,1,0:T(8,128)(2,1)} %pack.3), calls=%async_computation.1 | async-start | bytes 4194304 | tf_op jit(solution)/shard_map/all_to_all | solution.py:302
  34.3 0.2 reduce_sum.38.cnt_ref
  34.6 0.6 multiply_reduce_fusion
  35.2 0.6 select_reduce_fusion
  35.9 0.7 reshape.267.cols_ref
  36.6 0.1 reduce_max.9
  36.8 0.7 pad_add_fusion.edge_ref
  37.5 0.6 fusion.10.steps_ref
  38.1 22.5 %all-to-all-done.1.qd_ref = bf16[8,128,1024]{2,1,0:T(8,128)(2,1)S(1)} async-done(((bf16[8,128,1024]{2,1,0:T(8,128)(2,1)}), bf16[8,128,1024]{2,1,0:T(8,128)(2,1)S(1)}, u32[]{:S(2)}, u32[]{:S(2)}) %all-to-all-start.1) | async-done | bytes 2097184 | tf_op jit(solution)/shard_map/all_to_all | solution.py:302
  60.6 6.1 %all-gather.2.cloned.1.call-done.kv_ref = bf16[32,128,256]{2,1,0:T(8,128)(2,1)} async-done(((bf16[8,128,256]{2,1,0:T(8,128)(2,1)}), bf16[32,128,256]{2,1,0:T(8,128)(2,1)}) %all-gather.2.cloned.1.call-update) | async-done | bytes 2097168 | tf_op jit(solution)/shard_map/all_gather | solution.py:307
  66.7 22.0 %block_attention.1 = (bf16[8,128,512]{2,1,0:T(8,128)(2,1)}, bf16[32,128,256]{2,1,0:T(8,128)(2,1)}, f32[8,128]{1,0:T(8,128)}) custom-call(s32[8,128]{1,0:T(8,128)} %reshape.267.cols_ref, s32[8,4]{1,0:T(8,128)} %copy-done.4, s32[8,1]{1,0:T(8,128)} %fusion.10.steps_ref, s32[8,2]{1,0:T(8,128)} %pad_add_fusion.edge_ref, bf16[8,128,1024]{2,1,0:T(8,128)(2,1)} %copy-done.1, ...), custom_call_target="tpu_custom_call" | custom-call | flops 40000000000 | bytes 9000000 | tf_op jit(solution)/shard_map/block_attention/pallas_call | solution.py:175
  88.7 0.6 copy-done.5
  89.4 30.0 %all_to_all.25 = f32[64,2,128]{2,1,0:T(2,128)S(1)} all-to-all(f32[64,2,128]{2,1,0:T(2,128)S(1)} %bitcast.32), channel_id=1, replica_groups={{0,2,4,6,32,34,36,38,64,66,68,70,96,98,100,102,128,130,132,134,160,162,..., dimensions={0} | all-to-all | bytes 131072 | tf_op jit(solution)/shard_map/all_to_all | solution.py:321
  119.4 27.2 %all_to_all.26 = bf16[8,128,512]{2,1,0:T(8,128)(2,1)S(1)} all-to-all(bf16[8,128,512]{2,1,0:T(8,128)(2,1)S(1)} %copy-done.3), channel_id=1, replica_groups={{0,1,8,9,16,17,24,25},{2,3,10,11,18,19,26,27},{4,5,12,13,20,21,28,29},{..., dimensions={0} | all-to-all | bytes 2097152 | tf_op jit(solution)/shard_map/all_to_all | solution.py:302
  146.7 4.4 %all-to-all-start.3 = ((bf16[8,128,256]{2,1,0:T(8,128)(2,1)}), bf16[8,128,256]{2,1,0:T(8,128)(2,1)S(1)}, u32[]{:S(2)}, u32[]{:S(2)}) async-start(bf16[8,128,256]{2,1,0:T(8,128)(2,1)} %reduce-scatter.2.cloned.1.call-done), calls=%async_computation.4 | async-start | bytes 1048576 | tf_op jit(solution)/shard_map/all_to_all | solution.py:302
  151.1 0.2 reduce_sum.39
  151.3 0.6 fusion.28
  154.5 1.3 collective-permute-start
  155.8 1.7 collective-permute-done
  158.1 0.7 copy.77
  158.8 1.3 copy.81
  160.1 0.5 all-to-all-done.3
  160.6 0.1 fusion.27
  160.7 0.2 copy.79
  160.9 0.9 copy.83
  161.8 0.2 copy.78
  162.0 0.9 copy.82
  (35 shorter events, 0.5 us)
Async XLA Ops:
  7.2 22.6 %copy-start = (s32[32,32,32]{2,1,0:T(8,128)S(1)}, s32[32,32,32]{2,1,0:T(8,128)}, u32[]{:S(2)}) copy-start(s32[32,32,32]{2,1,0:T(8,128)} %param.9) | copy-start | bytes 393220
  9.1 19.8 %all-to-all-start = ((bf16[8,128,256]{2,1,0:T(8,128)(2,1)}), bf16[8,128,256]{2,1,0:T(8,128)(2,1)S(1)}, u32[]{:S(2)}, u32[]{:S(2)}) async-start(bf16[8,128,256]{2,1,0:T(8,128)(2,1)} %pack.2), calls=%async_computation | async-start | bytes 1048576 | tf_op jit(solution)/shard_map/all_to_all | solution.py:302
  19.4 47.3 %all-gather.2.cloned.1.call-start = ((), (), s32[]{:S(2)}) async-start(), calls=%async_computation.6 | async-start | bytes 2621440 | tf_op jit(solution)/shard_map/all_gather | solution.py:307
  28.9 0.8 copy-start.2
  29.8 30.7 %all-to-all-start.1 = ((bf16[8,128,1024]{2,1,0:T(8,128)(2,1)}), bf16[8,128,1024]{2,1,0:T(8,128)(2,1)S(1)}, u32[]{:S(2)}, u32[]{:S(2)}) async-start(bf16[8,128,1024]{2,1,0:T(8,128)(2,1)} %pack.3), calls=%async_computation.1 | async-start | bytes 4194304 | tf_op jit(solution)/shard_map/all_to_all | solution.py:302
  34.2 112.5 %reduce-scatter.2.cloned.1.call-start = ((), (), s32[]{:S(2)}) async-start(), calls=%async_computation.7 | async-start | bytes 2621440 | tf_op jit(solution)/shard_map/reduce_scatter | solution.py:314
  34.5 32.1 %copy-start.4 = (s32[8,4]{1,0:T(8,128)}, s32[8,4]{1,0:T(8,128)S(1)}, u32[]{:S(2)}) copy-start(s32[8,4]{1,0:T(8,128)S(1)} %reduce_sum.38.cnt_ref) | copy-start | bytes 388
  60.6 6.1 %copy-start.1 = (bf16[8,128,1024]{2,1,0:T(8,128)(2,1)}, bf16[8,128,1024]{2,1,0:T(8,128)(2,1)S(1)}, u32[]{:S(2)}) copy-start(bf16[8,128,1024]{2,1,0:T(8,128)(2,1)S(1)} %all-to-all-done.1.qd_ref) | copy-start | bytes 6291460
  88.7 0.7 copy-start.5
  88.7 30.8 %copy-start.3 = (bf16[8,128,512]{2,1,0:T(8,128)(2,1)S(1)}, bf16[8,128,512]{2,1,0:T(8,128)(2,1)}, u32[]{:S(2)}) copy-start(bf16[8,128,512]{2,1,0:T(8,128)(2,1)} %get-tuple-element.11) | copy-start | bytes 3145732
  146.7 13.9 %all-to-all-start.3 = ((bf16[8,128,256]{2,1,0:T(8,128)(2,1)}), bf16[8,128,256]{2,1,0:T(8,128)(2,1)S(1)}, u32[]{:S(2)}, u32[]{:S(2)}) async-start(bf16[8,128,256]{2,1,0:T(8,128)(2,1)} %reduce-scatter.2.cloned.1.call-done), calls=%async_computation.4 | async-start | bytes 1048576 | tf_op jit(solution)/shard_map/all_to_all | solution.py:302
  154.5 3.0 %collective-permute-start = (f32[]{:T(128)}, f32[]{:T(128)}, u32[]{:S(2)}, u32[]{:S(2)}) collective-permute-start(f32[]{:T(128)} %select_n.158), channel_id=1, source_target_pairs={{0,1},{2,3},{5,4},{7,6},{8,9},{10,11},{13,12},{15,14},{16,17},{18,... | collective-permute-start | bytes 20 | tf_op jit(solution)/shard_map/ppermute | solution.py:328
Sparse Core Ops, SparseCore 0:
  29.8 36.7 all-gather.1
  88.8 47.2 reduce-scatter.1

commit v3 on v1

v3 whole, which is shorter than its diff:
```python
import math

import jax
import jax.numpy as jnp
from jax import lax
from jax.experimental import pallas as pl
from jax.experimental.pallas import tpu as pltpu
from jax.sharding import PartitionSpec as P

H = 32
KVH = 8
HD = 128
BLK = 128
PAIR = 2
ROWS = 2
Z_ROWS = 64

ZLOSS = 0.05
NEG = -1e30
LOG2E = 1.0 / math.log(2.0)
LN2 = math.log(2.0)
SCALE = HD ** (-0.5)

NT = (((1,), (1,)), ((), ()))


def attention_body(
    cols_ref, cnt_ref, steps_ref, edge_ref,
    qd_ref, own_ref, mate_ref,
    send_ref, give_ref, z_ref,
    kv_s, e_s, dp_s, m_s, dk_s, dv_s, kt_s, dqt_s, sem,
):
    step = pl.program_id(0)
    blocks = kv_s.shape[0]
    half = blocks // 2
    core = edge_ref[0, 2]

    @pl.when(step == 0)
    def _():
        own = pltpu.make_async_copy(
            own_ref.at[:, :, pl.ds(4 * HD, 2 * HD)], kv_s.at[pl.ds(core * half, half)], sem.at[0]
        )
        mate = pltpu.make_async_copy(mate_ref, kv_s.at[pl.ds((1 - core) * half, half)], sem.at[1])
        own.start()
        mate.start()
        dk_s[...] = jnp.zeros_like(dk_s)
        dv_s[...] = jnp.zeros_like(dv_s)
        z_ref[...] = jnp.zeros_like(z_ref)
        own.wait()
        mate.wait()

        @pl.loop(0, blocks // 4)
        def _(b):
            for n in range(4):
                kt_s[4 * b + n] = kv_s[4 * b + n, :, :HD].T

    lanes = [(s, j) for s in range(ROWS) for j in range(PAIR)]
    qs = [qd_ref[s, :, j * HD : (j + 1) * HD] for s, j in lanes]
    gs = [qd_ref[s, :, (PAIR + j) * HD : (PAIR + j + 1) * HD] for s, j in lanes]

    def dot(a, b):
        return jnp.dot(a, b, preferred_element_type=jnp.float32)

    def dot_nt(a, b):
        return lax.dot_general(a, b, NT, preferred_element_type=jnp.float32)

    def pair(c1, c2):
        k = jnp.concatenate([kv_s[c1, :, :HD], kv_s[c2, :, :HD]], axis=0)
        v = jnp.concatenate([kv_s[c1, :, HD:], kv_s[c2, :, HD:]], axis=0)
        return k, v

    key_pos = lax.broadcasted_iota(jnp.int32, (BLK, BLK), 0)
    query_pos = lax.broadcasted_iota(jnp.int32, (BLK, BLK), 1)
    causal = key_pos <= query_pos
    state, row_q, row_g, diags = [], [], [], []
    for s in range(ROWS):
        diag = core * half + ROWS * step + s
        diags.append(diag)
        row_q.append(jnp.concatenate(qs[s * PAIR : (s + 1) * PAIR], axis=0))
        row_g.append(jnp.concatenate(gs[s * PAIR : (s + 1) * PAIR], axis=0))
        k0, v0 = pair(0, diag)
        s_all = dot_nt(k0, row_q[s]) * (SCALE * LOG2E)
        dp_all = dot_nt(v0, row_g[s])
        bias = jnp.where(diag == 0, NEG, 0.0).astype(jnp.float32)
        for j in range(PAIR):
            cut = slice(j * BLK, (j + 1) * BLK)
            sc = jnp.concatenate(
                [s_all[:BLK, cut] + bias, jnp.where(causal, s_all[BLK:, cut], NEG)], axis=0
            )
            dp = dp_all[:, cut]
            m = jnp.max(sc, axis=0, keepdims=True)
            e = jnp.exp2(sc - m)
            n = s * PAIR + j
            e_s[0, n] = e
            dp_s[0, n] = dp
            m_s[0, n] = jnp.broadcast_to(m, (8, BLK))
            state += [m, jnp.sum(e, axis=0, keepdims=True), jnp.sum(e * dp, axis=0, keepdims=True)]

    def entry(t, n):
        slot = 2 * (t - 1)
        return slot, cols_ref[step, n * blocks + slot], cols_ref[step, n * blocks + slot + 1]

    def forward(t, state):
        out = []
        for n in range(len(lanes)):
            m, l, u = state[3 * n : 3 * n + 3]
            slot, c1, c2 = entry(t, n)
            count = cnt_ref[step, n]
            b1 = jnp.where(slot < count, 0.0, NEG).astype(jnp.float32)
            b2 = jnp.where(slot + 1 < count, 0.0, NEG).astype(jnp.float32)
            k, v = pair(c1, c2)
            sc = dot_nt(k, qs[n]) * (SCALE * LOG2E)
            sc = jnp.concatenate([sc[:BLK] + b1, sc[BLK:] + b2], axis=0)
            dp = dot_nt(v, gs[n])
            m_new = jnp.maximum(m, jnp.max(sc, axis=0, keepdims=True))
            e = jnp.exp2(sc - m_new)
            alpha = jnp.exp2(m - m_new)
            e_s[t, n] = e
            dp_s[t, n] = dp
            m_s[t, n] = jnp.broadcast_to(m_new, (8, BLK))
            out += [
                m_new,
                l * alpha + jnp.sum(e, axis=0, keepdims=True),
                u * alpha + jnp.sum(e * dp, axis=0, keepdims=True),
            ]
        return tuple(out)

    steps = steps_ref[step, 0]
    state = lax.fori_loop(1, steps, forward, tuple(state))

    top, inv, pull = [], [], []
    for n, (s, j) in enumerate(lanes):
        m, l, u = state[3 * n : 3 * n + 3]
        inv_l = 1.0 / l
        log_norm = m * LN2 + jnp.log(l)
        top.append(m)
        inv.append(inv_l)
        pull.append((2.0 * ZLOSS) * log_norm - u * inv_l)
        z_ref[j : j + 1, :] += log_norm * log_norm

    def weights(t, n):
        factor = jnp.exp2(m_s[t, n][:1] - top[n]) * inv[n]
        probs = e_s[t, n] * factor
        dscore = probs * (dp_s[t, n] + pull[n])
        return probs.astype(jnp.bfloat16), dscore.astype(jnp.bfloat16)

    dk0, dv0 = [], []
    for s in range(ROWS):
        first = [weights(0, s * PAIR + j) for j in range(PAIR)]
        p_all = jnp.concatenate([w[0] for w in first], axis=1)
        d_all = jnp.concatenate([w[1] for w in first], axis=1)
        dk = dot(d_all, row_q[s])
        dv = dot(p_all, row_g[s])
        dk0.append(dk[:BLK])
        dv0.append(dv[:BLK])
        dk_s[diags[s]] += dk[BLK:]
        dv_s[diags[s]] += dv[BLK:]
        dqt = dot(jnp.concatenate([kt_s[0], kt_s[diags[s]]], axis=1), d_all)
        for j in range(PAIR):
            dqt_s[s * PAIR + j] = dqt[:, j * BLK : (j + 1) * BLK]
    dk_s[0] += sum(dk0[1:], dk0[0])
    dv_s[0] += sum(dv0[1:], dv0[0])

    @pl.loop(1, steps)
    def _(t):
        for n in range(len(lanes)):
            _, c1, c2 = entry(t, n)
            p_low, d_low = weights(t, n)
            dk = dot(d_low, qs[n])
            dv = dot(p_low, gs[n])
            dqt_s[n] += dot(jnp.concatenate([kt_s[c1], kt_s[c2]], axis=1), d_low)
            dk_s[c1] += dk[:BLK]
            dv_s[c1] += dv[:BLK]
            dk_s[c2] += dk[BLK:]
            dv_s[c2] += dv[BLK:]

    for n, (s, j) in enumerate(lanes):
        send_ref[ROWS * step + s, :, j * HD : (j + 1) * HD] = (dqt_s[n] * SCALE).T.astype(jnp.bfloat16)

    @pl.when(step == pl.num_programs(0) - 1)
    def _():
        @pl.loop(0, half)
        def _(i):
            mine = core * half + i
            other = (1 - core) * half + i
            send_ref[i, :, 2 * HD : 3 * HD] = (dk_s[mine] * SCALE).astype(jnp.bfloat16)
            send_ref[i, :, 3 * HD :] = dv_s[mine].astype(jnp.bfloat16)
            give_ref[i, :, :HD] = (dk_s[other] * SCALE).astype(jnp.bfloat16)
            give_ref[i, :, HD:] = dv_s[other].astype(jnp.bfloat16)


def attention(recv, mate, cols, cnt, steps, edge):
    half = recv.shape[0]
    blocks = 2 * half
    lanes = ROWS * PAIR
    max_steps = half
    return pl.pallas_call(
        attention_body,
        out_shape=(
            jax.ShapeDtypeStruct((half, BLK, 4 * HD), jnp.bfloat16),
            jax.ShapeDtypeStruct((half, BLK, 2 * HD), jnp.bfloat16),
            jax.ShapeDtypeStruct((Z_ROWS, BLK), jnp.float32),
        ),
        grid_spec=pltpu.PrefetchScalarGridSpec(
            num_scalar_prefetch=4,
            grid=(half // ROWS,),
            in_specs=[
                pl.BlockSpec((ROWS, BLK, 4 * HD), lambda i, *_: (i, 0, 0)),
                pl.BlockSpec(memory_space=pl.ANY),
                pl.BlockSpec(memory_space=pl.ANY),
            ],
            out_specs=[
                pl.BlockSpec((half, BLK, 4 * HD), lambda i, *_: (0, 0, 0)),
                pl.BlockSpec((half, BLK, 2 * HD), lambda i, *_: (0, 0, 0)),
                pl.BlockSpec((Z_ROWS, BLK), lambda i, *_: (0, 0)),
            ],
            scratch_shapes=[
                pltpu.VMEM((blocks, BLK, 2 * HD), jnp.bfloat16),
                pltpu.VMEM((max_steps, lanes, 2 * BLK, BLK), jnp.float32),
                pltpu.VMEM((max_steps, lanes, 2 * BLK, BLK), jnp.float32),
                pltpu.VMEM((max_steps, lanes, 8, BLK), jnp.float32),
                pltpu.VMEM((blocks, BLK, HD), jnp.float32),
                pltpu.VMEM((blocks, BLK, HD), jnp.float32),
                pltpu.VMEM((blocks, HD, BLK), jnp.bfloat16),
                pltpu.VMEM((lanes, HD, BLK), jnp.float32),
                pltpu.SemaphoreType.DMA((2,)),
            ],
        ),
        compiler_params=pltpu.CompilerParams(
            dimension_semantics=("arbitrary",), vmem_limit_bytes=58 << 20
        ),
        cost_estimate=pl.CostEstimate(
            flops=40_000_000_000, transcendentals=4_000_000, bytes_accessed=9_000_000
        ),
        name="block_attention",
    )(cols, cnt, steps, edge, recv, recv, mate)


def pack_body(q_ref, g_ref, k_ref, v_ref, out_ref, hold, in_sem, out_sem):
    chips = out_ref.shape[0]

    def load(p, n):
        ref, width, start, place = (
            (q_ref, 2 * HD, 2 * HD * p, 0),
            (g_ref, 2 * HD, 2 * HD * p, 2 * HD),
            (k_ref, HD, HD * (p // 2), 4 * HD),
            (v_ref, HD, HD * (p // 2), 5 * HD),
        )[n]
        return pltpu.make_async_copy(
            ref.at[0, :, pl.ds(start, width)], hold.at[p, :, pl.ds(place, width)], in_sem.at[p, n]
        )

    loads = [[load(p, n) for n in range(4)] for p in range(chips)]
    stores = [pltpu.make_async_copy(hold.at[p], out_ref.at[p], out_sem.at[p]) for p in range(chips)]
    for four in loads:
        for copy in four:
            copy.start()
    for p in range(chips):
        for copy in loads[p]:
            copy.wait()
        stores[p].start()
    for copy in stores:
        copy.wait()


def pack(queries, out_grad, keys, values):
    tok = queries.shape[1]
    chips = H // PAIR
    shape = (chips, tok, 6 * HD)
    return pl.pallas_call(
        pack_body,
        out_shape=jax.ShapeDtypeStruct(shape, queries.dtype),
        in_specs=[pl.BlockSpec(memory_space=pl.ANY)] * 4,
        out_specs=pl.BlockSpec(memory_space=pl.ANY),
        scratch_shapes=[
            pltpu.VMEM(shape, queries.dtype),
            pltpu.SemaphoreType.DMA((chips, 4)),
            pltpu.SemaphoreType.DMA((chips,)),
        ],
        name="pack",
    )(queries, out_grad, keys, values)


def merge_body(send_ref, got_ref, out_ref):
    out_ref[...] = (send_ref[...].astype(jnp.float32) + got_ref[...].astype(jnp.float32)).astype(out_ref.dtype)


def merge(send, got):
    part = send.shape[0] // 4
    lower = pl.BlockSpec((part, BLK, 2 * HD), lambda i: (i, 0, 1))
    return pl.pallas_call(
        merge_body,
        out_shape=jax.ShapeDtypeStruct(send.shape, send.dtype),
        grid=(4,),
        in_specs=[lower, pl.BlockSpec((part, BLK, 2 * HD), lambda i: (i, 0, 0))],
        out_specs=lower,
        input_output_aliases={0: 0},
        name="merge",
    )(send, got)


def unpack_body(back_ref, dq_ref, dk_ref, dv_ref):
    for n in range(back_ref.shape[0]):
        dq_ref[0, :, n * 2 * HD : (n + 1) * 2 * HD] = back_ref[n, :, : 2 * HD]
    for g in range(back_ref.shape[0] // 2):
        both = back_ref[2 * g, :, 2 * HD :].astype(jnp.float32) + back_ref[2 * g + 1, :, 2 * HD :].astype(jnp.float32)
        dk_ref[0, :, g * HD : (g + 1) * HD] = both[:, :HD].astype(dk_ref.dtype)
        dv_ref[0, :, g * HD : (g + 1) * HD] = both[:, HD:].astype(dv_ref.dtype)


def unpack(back):
    chips, tok = back.shape[:2]
    cut = 4
    return pl.pallas_call(
        unpack_body,
        out_shape=(
            jax.ShapeDtypeStruct((1, tok, H * HD), back.dtype),
            jax.ShapeDtypeStruct((1, tok, KVH * HD), back.dtype),
            jax.ShapeDtypeStruct((1, tok, KVH * HD), back.dtype),
        ),
        grid=(cut,),
        in_specs=[pl.BlockSpec((chips // cut, tok, 4 * HD), lambda i: (i, 0, 0))],
        out_specs=[
            pl.BlockSpec((1, tok, H * HD // cut), lambda i: (0, 0, i)),
            pl.BlockSpec((1, tok, KVH * HD // cut), lambda i: (0, 0, i)),
            pl.BlockSpec((1, tok, KVH * HD // cut), lambda i: (0, 0, i)),
        ],
        name="unpack",
    )(back)


def work_lists(mask, core):
    blocks = mask.shape[2]
    half = blocks // 2
    mask = lax.dynamic_index_in_dim(mask.reshape(PAIR, half, 2, blocks), core, axis=2, keepdims=False)
    mask = jnp.transpose(mask.reshape(PAIR, half // ROWS, ROWS, blocks), (1, 2, 0, 3))
    col = jnp.arange(blocks, dtype=jnp.int32)
    own = (2 * jnp.arange(half, dtype=jnp.int32) + core).reshape(half // ROWS, ROWS)
    other = (mask > 0) & (col > 0) & (col != own[:, :, None, None])
    other = other.astype(jnp.int32).reshape(half // ROWS, ROWS * PAIR, blocks)
    before = (col[None, :] < col[:, None]).astype(jnp.int32)
    rank = jnp.sum(other[:, :, None, :] * before[None, None], axis=3)
    place = col % 2 * half + col // 2
    hit = (rank[:, :, None, :] == col[None, None, :, None]) & (other[:, :, None, :] > 0)
    cols = jnp.sum(jnp.where(hit, place[None, None, None, :], 0), axis=3)
    cnt = jnp.sum(other, axis=2)
    steps = 1 + (jnp.max(cnt, axis=1) + 1) // 2
    edge = jnp.full((1, 3), core, jnp.int32)
    return cols.reshape(half // ROWS, ROWS * PAIR * blocks), cnt, steps[:, None], edge


def body(queries, keys, values, out_grad, block_mask):
    dps = lax.axis_size("dp")
    ctx = lax.axis_size("ctx")
    blocks = block_mask.shape[1]
    me = lax.axis_index("ctx")
    chip, core = me // 2, me % 2
    same = [[2 * p + c for p in range(ctx // 2)] for c in range(2)]
    mates = [(i, i ^ 1) for i in range(ctx)]
    wide = [[d * ctx + 2 * p + c for d in range(dps) for c in range(2)] for p in range(ctx // 2)]

    def exchange(a):
        return lax.all_to_all(a, "ctx", 0, 0, axis_index_groups=same, tiled=True)

    recv = exchange(pack(queries, out_grad, keys, values))
    mate = lax.ppermute(recv[:, :, 4 * HD :], "ctx", mates)

    mask = lax.dynamic_slice(block_mask, (chip * PAIR, 0, 0), (PAIR, blocks, blocks))
    send, give, z = attention(recv, mate, *work_lists(mask, core))

    z_all = lax.all_gather(z, ("dp", "ctx"), axis_index_groups=wide)
    send = merge(send, lax.ppermute(give, "ctx", mates))
    query_grad, key_grad, value_grad = unpack(exchange(send))
    z_two = jnp.sum(z_all[:, :PAIR], axis=(0, 2)) * (ZLOSS / (dps * blocks * BLK))
    z_own = jnp.where(core == 0, z_two[0], z_two[1])[None]
    return query_grad, key_grad, value_grad, z_own


def solution(mesh):
    return jax.shard_map(
        body,
        mesh=mesh,
        in_specs=(
            P("dp", "ctx", None),
            P("dp", "ctx", None),
            P("dp", "ctx", None),
            P("dp", "ctx", None),
            P(),
        ),
        out_specs=(P("dp", "ctx", None), P("dp", "ctx", None), P("dp", "ctx", None), P("ctx")),
        check_vma=False,
    )
```

time: 189 us -> 191 us (1.011)
  blocking collectives: 75.5 us -> 0 us
  waiting for transfers between devices: 47.6 us -> 103 us
  starting transfers between devices: 7.17 us -> 28.3 us
  Pallas kernels: 20 us -> 31.9 us
  local copies, waits for them, and re-layouts: 16.7 us -> 6.75 us
    all_to_all x3 -> x0, blocking collectives: 75.5 us -> none  [the longest x2 41.7 us: exchange(): return lax.all_to_all(a, 'ctx', 0, 0, axis_index_groups=spread, tiled=True)]
    all_gather x1, waiting for transfers between devices: 7.99 us -> 64 us  [body(): z_all = lax.all_gather(z, ('dp', 'ctx'), axis_index_groups=wide)]
    pallas_call x1 -> x4, Pallas kernels: 20 us -> 31.9 us  [the longest x1 20.7 us: attention(): pl.pallas_call(attention_body, out_shape=(jax.ShapeDtypeStruct((half, BLK...]
    all_to_all x2, starting transfers between devices: 7.09 us -> 18.1 us  [exchange(): return lax.all_to_all(a, 'ctx', 0, 0, axis_index_groups=same, tiled=True)]
    ppermute x0 -> x2, starting transfers between devices: none -> 10.2 us  [the longest x1 8.24 us: body(): mate = lax.ppermute(recv[:, :, 4 * HD:], 'ctx', mates)]
    unnamed x17 -> x8, local copies, waits for them, and re-layouts: 12.5 us -> 2.76 us
    all_to_all x2, waiting for transfers between devices: 39.6 us -> 36.2 us  [exchange(): return lax.all_to_all(a, 'ctx', 0, 0, axis_index_groups=same, tiled=True)]
    ppermute x0 -> x2, waiting for transfers between devices: none -> 2.81 us  [the longest x1 2.81 us: body(): send = merge(send, lax.ppermute(give, 'ctx', mates))]
  transfers between devices with their start and end apart: 4 -> 5, of which waited for: 3 -> 3; matrix products, arithmetic and copies ran while one was open for 7% -> 3% of each run, Pallas kernels for 0% -> 2%
where the time goes in v3:
time: 191 us; the launch traced here: 190 us
  waiting for transfers between devices  103 us (54%)
  Pallas kernels  31.9 us (17%)
  starting transfers between devices  28.3 us (15%)
  between operations  16.7 us (9%)
  local copies, waits for them, and re-layouts  6.75 us (4%)
  other arithmetic  3.59 us (2%)
    all_gather x1, waiting for transfers between devices, body(): z_all = lax.all_gather(z, ('dp', 'ctx'), axis_index_groups=wide)  64 us
    all_to_all x2, waiting for transfers between devices, exchange(): return lax.all_to_all(a, 'ctx', 0, 0, axis_index_groups=same, tiled=True)  36.2 us
    pallas_call x1, Pallas kernels, attention(): pl.pallas_call(attention_body, out_shape=(jax.ShapeDtypeStruct((half, BLK...  20.7 us
    all_to_all x2, starting transfers between devices, exchange(): return lax.all_to_all(a, 'ctx', 0, 0, axis_index_groups=same, tiled=True)  18.1 us
    ppermute x1, starting transfers between devices, body(): mate = lax.ppermute(recv[:, :, 4 * HD:], 'ctx', mates)  8.24 us
  transfers between devices with their start and end apart: 5, of which 3 were waited for; matrix products, arithmetic and copies ran while one was open for 3% of the time, Pallas kernels for 2%

profile of v3, /device:TPU:1, one launch (start us, length us, event | category | flops | bytes accessed | tf_op | source)
XLA Modules:
  0.0 190.2 jit_solution(836020903352324886)
XLA Ops:
  7.2 0.0 copy-start
  7.2 3.8 %pack.1 = bf16[16,128,768]{2,1,0:T(8,128)(2,1)} custom-call(bf16[1,128,4096]{2,1,0:T(8,128)(2,1)} %q_ref.1, bf16[1,128,4096]{2,1,0:T(8,128)(2,1)} %g_ref.1, bf16[1,128,1024]{2,1,0:T(8,128)(2,1)} %k_ref.1, bf16[1,128,1024]{2,1,0:T(8,128)(2,1)} %v_ref.1), custom_call_target="tpu_custom_call" | custom-call | tf_op jit(solution)/shard_map/pack/pallas_call | solution.py:270
  11.0 7.6 %all-to-all-start = ((bf16[16,128,768]{2,1,0:T(8,128)(2,1)}), bf16[16,128,768]{2,1,0:T(8,128)(2,1)}, u32[]{:S(2)}, u32[]{:S(2)}) async-start(bf16[16,128,768]{2,1,0:T(8,128)(2,1)} %pack.1), calls=%async_computation | async-start | bytes 6291456 | tf_op jit(solution)/shard_map/all_to_all | solution.py:363
  18.7 0.0 all-gather.3.cloned.1.call-start
  18.8 0.1 compare_reduce_fusion
  18.9 0.1 iota_compare_fusion.2
  19.0 0.4 fusion.8
  19.3 0.1 copy.43
  19.4 0.1 reduce_max.9
  19.5 0.7 copy.48.cnt_ref
  20.2 0.1 copy.44
  20.3 36.2 %all-to-all-done.qd_ref.own_ref = bf16[16,128,768]{2,1,0:T(8,128)(2,1)} async-done(((bf16[16,128,768]{2,1,0:T(8,128)(2,1)}), bf16[16,128,768]{2,1,0:T(8,128)(2,1)}, u32[]{:S(2)}, u32[]{:S(2)}) %all-to-all-start) | async-done | bytes 3145760 | tf_op jit(solution)/shard_map/all_to_all | solution.py:363
  56.5 1.3 slice.16
  57.7 8.2 %collective-permute-start = (bf16[16,128,256]{2,1,0:T(8,128)(2,1)S(1)}, bf16[16,128,256]{2,1,0:T(8,128)(2,1)S(1)}, u32[]{:S(2)}, u32[]{:S(2)}) collective-permute-start(bf16[16,128,256]{2,1,0:T(8,128)(2,1)S(1)} %slice.16), channel_id=1, source_target_pairs={{0,1},{1,0},{2,3},{3,2},{4,5},{5,4},{6,7},{7,6},{8,9},{9,8},{10,11... | collective-permute-start | bytes 3145736 | tf_op jit(solution)/shard_map/ppermute | solution.py:366
  66.1 0.6 multiply_reduce_fusion
  66.7 0.6 select_reduce_fusion
  67.4 0.7 reshape.142.cols_ref
  68.0 0.6 fusion.4.steps_ref
  68.6 0.5 broadcast_in_dim.18.edge_ref
  69.2 0.4 copy-done.3
  69.6 20.7 %block_attention.1 = (bf16[16,128,512]{2,1,0:T(8,128)(2,1)}, bf16[16,128,256]{2,1,0:T(8,128)(2,1)}, f32[64,128]{1,0:T(8,128)}) custom-call(s32[8,128]{1,0:T(8,128)} %reshape.142.cols_ref, s32[8,4]{1,0:T(8,128)} %copy.48.cnt_ref, s32[8,1]{1,0:T(8,128)} %fusion.4.steps_ref, s32[1,3]{1,0:T(1,128)} %broadcast_in_dim.18.edge_ref, ...), custom_call_target="tpu_custom_call" | custom-call | flops 40000000000 | bytes 9000000 | tf_op jit(solution)/shard_map/block_attention/pallas_call | solution.py:197
  90.3 1.9 %collective-permute-start.1 = (bf16[16,128,256]{2,1,0:T(8,128)(2,1)}, bf16[16,128,256]{2,1,0:T(8,128)(2,1)S(1)}, u32[]{:S(2)}, u32[]{:S(2)}) collective-permute-start(bf16[16,128,256]{2,1,0:T(8,128)(2,1)} %get-tuple-element.11), channel_id=1, source_target_pairs={{0,1},{1,0},{2,3},{3,2},{4,5},{5,4},{6,7},{7,6},{8,9},{9,8},{10,11... | collective-permute-start | bytes 3145736 | tf_op jit(solution)/shard_map/ppermute | solution.py:372
  92.2 0.0 all-gather.3.cloned.1.call-update
  92.2 2.8 %collective-permute-done.1.got_ref = bf16[16,128,256]{2,1,0:T(8,128)(2,1)S(1)} collective-permute-done((bf16[16,128,256]{2,1,0:T(8,128)(2,1)}, bf16[16,128,256]{2,1,0:T(8,128)(2,1)S(1)}, u32[]{:S(2)}, u32[]{:S(2)}) %collective-permute-start.1) | collective-permute-done | bytes 1048608 | tf_op jit(solution)/shard_map/ppermute | solution.py:372
  95.1 1.0 copy-done.2
  96.0 3.7 %merge.1 = bf16[16,128,512]{2,1,0:T(8,128)(2,1)} custom-call(bf16[16,128,512]{2,1,0:T(8,128)(2,1)} %get-tuple-element.10.send_ref, bf16[16,128,256]{2,1,0:T(8,128)(2,1)} %copy-done.2), custom_call_target="tpu_custom_call", output_to_operand_aliasing={{}: (0, {})} | custom-call | tf_op jit(solution)/shard_map/merge/pallas_call | solution.py:291
  99.7 10.4 %all-to-all-start.1 = ((bf16[16,128,512]{2,1,0:T(8,128)(2,1)}), bf16[16,128,512]{2,1,0:T(8,128)(2,1)S(1)}, u32[]{:S(2)}, u32[]{:S(2)}) async-start(bf16[16,128,512]{2,1,0:T(8,128)(2,1)} %merge.1), calls=%async_computation.1 | async-start | bytes 4194304 | tf_op jit(solution)/shard_map/all_to_all | solution.py:363
  110.2 64.0 %all-gather.3.cloned.1.call-done = f32[2048,128]{1,0:T(8,128)} async-done(((f32[64,128]{1,0:T(8,128)}), f32[2048,128]{1,0:T(8,128)}) %all-gather.3.cloned.1.call-update) | async-done | bytes 1048592 | tf_op jit(solution)/shard_map/all_gather | solution.py:371
  174.2 1.0 slice_reduce_fusion
  175.2 0.6 fusion.9
  177.1 1.3 copy-done.1
  178.5 3.7 %unpack.1 = (bf16[1,128,4096]{2,1,0:T(8,128)(2,1)}, bf16[1,128,1024]{2,1,0:T(8,128)(2,1)}, bf16[1,128,1024]{2,1,0:T(8,128)(2,1)}) custom-call(bf16[16,128,512]{2,1,0:T(8,128)(2,1)} %copy-done.1), custom_call_target="tpu_custom_call" | custom-call | tf_op jit(solution)/shard_map/unpack/pallas_call | solution.py:314
  (19 shorter events, 0.1 us)
Async XLA Ops:
  7.2 11.6 %copy-start = (s32[32,32,32]{2,1,0:T(8,128)S(1)}, s32[32,32,32]{2,1,0:T(8,128)}, u32[]{:S(2)}) copy-start(s32[32,32,32]{2,1,0:T(8,128)} %param.9) | copy-start | bytes 393220
  11.0 45.4 %all-to-all-start = ((bf16[16,128,768]{2,1,0:T(8,128)(2,1)}), bf16[16,128,768]{2,1,0:T(8,128)(2,1)}, u32[]{:S(2)}, u32[]{:S(2)}) async-start(bf16[16,128,768]{2,1,0:T(8,128)(2,1)} %pack.1), calls=%async_computation | async-start | bytes 6291456 | tf_op jit(solution)/shard_map/all_to_all | solution.py:363
  18.7 155.5 %all-gather.3.cloned.1.call-start = ((), (), s32[]{:S(2)}) async-start(), calls=%async_computation.2 | async-start | bytes 1081344 | tf_op jit(solution)/shard_map/all_gather | solution.py:371
  57.7 10.9 %collective-permute-start = (bf16[16,128,256]{2,1,0:T(8,128)(2,1)S(1)}, bf16[16,128,256]{2,1,0:T(8,128)(2,1)S(1)}, u32[]{:S(2)}, u32[]{:S(2)}) collective-permute-start(bf16[16,128,256]{2,1,0:T(8,128)(2,1)S(1)} %slice.16), channel_id=1, source_target_pairs={{0,1},{1,0},{2,3},{3,2},{4,5},{5,4},{6,7},{7,6},{8,9},{9,8},{10,11... | collective-permute-start | bytes 3145736 | tf_op jit(solution)/shard_map/ppermute | solution.py:366
  68.6 1.0 copy-start.3
  90.3 4.8 %collective-permute-start.1 = (bf16[16,128,256]{2,1,0:T(8,128)(2,1)}, bf16[16,128,256]{2,1,0:T(8,128)(2,1)S(1)}, u32[]{:S(2)}, u32[]{:S(2)}) collective-permute-start(bf16[16,128,256]{2,1,0:T(8,128)(2,1)} %get-tuple-element.11), channel_id=1, source_target_pairs={{0,1},{1,0},{2,3},{3,2},{4,5},{5,4},{6,7},{7,6},{8,9},{9,8},{10,11... | collective-permute-start | bytes 3145736 | tf_op jit(solution)/shard_map/ppermute | solution.py:372
  95.1 1.0 copy-start.2
  99.7 77.4 %all-to-all-start.1 = ((bf16[16,128,512]{2,1,0:T(8,128)(2,1)}), bf16[16,128,512]{2,1,0:T(8,128)(2,1)S(1)}, u32[]{:S(2)}, u32[]{:S(2)}) async-start(bf16[16,128,512]{2,1,0:T(8,128)(2,1)} %merge.1), calls=%async_computation.1 | async-start | bytes 4194304 | tf_op jit(solution)/shard_map/all_to_all | solution.py:363
  177.1 1.4 copy-start.1
Sparse Core Ops, SparseCore 0:
  92.4 81.7 all-gather.2

commit v4 on v3

--- a/solution.py
+++ b/solution.py
@@ -13,7 +13,7 @@
 BLK = 128
 PAIR = 2
 ROWS = 2
-Z_ROWS = 64
+Z_ROWS = 8
 
 ZLOSS = 0.05
 NEG = -1e30
@@ -281,36 +281,76 @@
     )(queries, out_grad, keys, values)
 
 
-def merge_body(send_ref, got_ref, out_ref):
-    out_ref[...] = (send_ref[...].astype(jnp.float32) + got_ref[...].astype(jnp.float32)).astype(out_ref.dtype)
+def merge_body(send_ref, got_ref, out_ref, own_s, in_sem, out_sem):
+    parts = in_sem.shape[0]
+    part = own_s.shape[0] // parts
+
+    def cut(n):
+        return pl.ds(n * part, part)
+
+    loads = [
+        pltpu.make_async_copy(send_ref.at[cut(n), :, pl.ds(2 * HD, 2 * HD)], own_s.at[cut(n)], in_sem.at[n])
+        for n in range(parts)
+    ]
+    stores = [
+        pltpu.make_async_copy(own_s.at[cut(n)], out_ref.at[cut(n), :, pl.ds(2 * HD, 2 * HD)], out_sem.at[n])
+        for n in range(parts)
+    ]
+    for copy in loads:
+        copy.start()
+    for n in range(parts):
+        loads[n].wait()
+        rows = slice(n * part, (n + 1) * part)
+        both = own_s[rows].astype(jnp.float32) + got_ref[rows].astype(jnp.float32)
+        own_s[rows] = both.astype(own_s.dtype)
+        stores[n].start()
+    for copy in stores:
+        copy.wait()
 
 
 def merge(send, got):
-    part = send.shape[0] // 4
-    lower = pl.BlockSpec((part, BLK, 2 * HD), lambda i: (i, 0, 1))
     return pl.pallas_call(
         merge_body,
         out_shape=jax.ShapeDtypeStruct(send.shape, send.dtype),
-        grid=(4,),
-        in_specs=[lower, pl.BlockSpec((part, BLK, 2 * HD), lambda i: (i, 0, 0))],
-        out_specs=lower,
+        in_specs=[pl.BlockSpec(memory_space=pl.ANY), pl.BlockSpec(memory_space=pltpu.VMEM)],
+        out_specs=pl.BlockSpec(memory_space=pl.ANY),
+        scratch_shapes=[
+            pltpu.VMEM(got.shape, got.dtype),
+            pltpu.SemaphoreType.DMA((4,)),
+            pltpu.SemaphoreType.DMA((4,)),
+        ],
         input_output_aliases={0: 0},
+        compiler_params=pltpu.CompilerParams(vmem_limit_bytes=16 << 20),
         name="merge",
     )(send, got)
 
 
-def unpack_body(back_ref, dq_ref, dk_ref, dv_ref):
-    for n in range(back_ref.shape[0]):
-        dq_ref[0, :, n * 2 * HD : (n + 1) * 2 * HD] = back_ref[n, :, : 2 * HD]
-    for g in range(back_ref.shape[0] // 2):
+def unpack_body(back_ref, dq_ref, dk_ref, dv_ref, dk_s, dv_s, dq_sem, kv_sem):
+    chips = back_ref.shape[0]
+    copies = [
+        pltpu.make_async_copy(
+            back_ref.at[p, :, pl.ds(0, 2 * HD)], dq_ref.at[0, :, pl.ds(p * 2 * HD, 2 * HD)], dq_sem.at[p]
+        )
+        for p in range(chips)
+    ]
+    for copy in copies:
+        copy.start()
+    for g in range(chips // 2):
         both = back_ref[2 * g, :, 2 * HD :].astype(jnp.float32) + back_ref[2 * g + 1, :, 2 * HD :].astype(jnp.float32)
-        dk_ref[0, :, g * HD : (g + 1) * HD] = both[:, :HD].astype(dk_ref.dtype)
-        dv_ref[0, :, g * HD : (g + 1) * HD] = both[:, HD:].astype(dv_ref.dtype)
+        dk_s[:, g * HD : (g + 1) * HD] = both[:, :HD].astype(dk_s.dtype)
+        dv_s[:, g * HD : (g + 1) * HD] = both[:, HD:].astype(dv_s.dtype)
+    copies += [
+        pltpu.make_async_copy(dk_s, dk_ref.at[0], kv_sem.at[0]),
+        pltpu.make_async_copy(dv_s, dv_ref.at[0], kv_sem.at[1]),
+    ]
+    for copy in copies[chips:]:
+        copy.start()
+    for copy in copies:
+        copy.wait()
 
 
 def unpack(back):
     chips, tok = back.shape[:2]
-    cut = 4
     return pl.pallas_call(
         unpack_body,
         out_shape=(
@@ -318,13 +358,15 @@
             jax.ShapeDtypeStruct((1, tok, KVH * HD), back.dtype),
             jax.ShapeDtypeStruct((1, tok, KVH * HD), back.dtype),
         ),
-        grid=(cut,),
-        in_specs=[pl.BlockSpec((chips // cut, tok, 4 * HD), lambda i: (i, 0, 0))],
-        out_specs=[
-            pl.BlockSpec((1, tok, H * HD // cut), lambda i: (0, 0, i)),
-            pl.BlockSpec((1, tok, KVH * HD // cut), lambda i: (0, 0, i)),
-            pl.BlockSpec((1, tok, KVH * HD // cut), lambda i: (0, 0, i)),
+        in_specs=[pl.BlockSpec(memory_space=pltpu.VMEM)],
+        out_specs=[pl.BlockSpec(memory_space=pl.ANY)] * 3,
+        scratch_shapes=[
+            pltpu.VMEM((tok, KVH * HD), back.dtype),
+            pltpu.VMEM((tok, KVH * HD), back.dtype),
+            pltpu.SemaphoreType.DMA((chips,)),
+            pltpu.SemaphoreType.DMA((2,)),
         ],
+        compiler_params=pltpu.CompilerParams(vmem_limit_bytes=16 << 20),
         name="unpack",
     )(back)
 
@@ -357,7 +399,6 @@
     chip, core = me // 2, me % 2
     same = [[2 * p + c for p in range(ctx // 2)] for c in range(2)]
     mates = [(i, i ^ 1) for i in range(ctx)]
-    wide = [[d * ctx + 2 * p + c for d in range(dps) for c in range(2)] for p in range(ctx // 2)]
 
     def exchange(a):
         return lax.all_to_all(a, "ctx", 0, 0, axis_index_groups=same, tiled=True)
@@ -368,11 +409,14 @@
     mask = lax.dynamic_slice(block_mask, (chip * PAIR, 0, 0), (PAIR, blocks, blocks))
     send, give, z = attention(recv, mate, *work_lists(mask, core))
 
-    z_all = lax.all_gather(z, ("dp", "ctx"), axis_index_groups=wide)
     send = merge(send, lax.ppermute(give, "ctx", mates))
-    query_grad, key_grad, value_grad = unpack(exchange(send))
-    z_two = jnp.sum(z_all[:, :PAIR], axis=(0, 2)) * (ZLOSS / (dps * blocks * BLK))
-    z_own = jnp.where(core == 0, z_two[0], z_two[1])[None]
+    send, z = lax.optimization_barrier((send, z))
+    back = exchange(send)
+    z_two = jnp.sum(lax.all_gather(z, "dp"), axis=(0, 2))[:PAIR] * (ZLOSS / (dps * blocks * BLK))
+    z_mine = jnp.where(core == 0, z_two[0], z_two[1])
+    z_mate = jnp.where(core == 0, z_two[1], z_two[0])
+    z_own = (z_mine + lax.ppermute(z_mate, "ctx", mates))[None]
+    query_grad, key_grad, value_grad = unpack(back)
     return query_grad, key_grad, value_grad, z_own
 
 

time: 191 us -> 154 us (0.81)
  waiting for transfers between devices: 103 us -> 39.1 us
  blocking collectives: 0 us -> 33.1 us
  between operations: 16.7 us -> 5.22 us
  starting transfers between devices: 28.3 us -> 36.5 us
  Pallas kernels: 31.9 us -> 29.1 us
    all_gather x1 -> x0, waiting for transfers between devices: 64 us -> none  [body(): z_all = lax.all_gather(z, ('dp', 'ctx'), axis_index_groups=wide)]
    all_gather x0 -> x1, blocking collectives: none -> 33.1 us  [body(): lax.all_gather(z, 'dp')]
    ppermute x0 -> x1, starting transfers between devices: none -> 8.74 us  [body(): z_own = (z_mine + lax.ppermute(z_mate, 'ctx', mates))[None]]
    pallas_call x1, Pallas kernels: 3.69 us -> 0.48 us  [merge(): pl.pallas_call(merge_body, out_shape=jax.ShapeDtypeStruct(send.shape, sen...]
    pallas_call x1, Pallas kernels: 20.7 us -> 23.5 us  [attention(): pl.pallas_call(attention_body, out_shape=(jax.ShapeDtypeStruct((half, BLK...]
    pallas_call x1, Pallas kernels: 3.7 us -> 1.29 us  [unpack(): pl.pallas_call(unpack_body, out_shape=(jax.ShapeDtypeStruct((1, tok, H *...]
  transfers between devices with their start and end apart: 5 -> 5, of which waited for: 3 -> 2; matrix products, arithmetic and copies ran while one was open for 3% -> 3% of each run, Pallas kernels for 2% -> 0%
where the time goes in v4:
time: 154 us; the launch traced here: 153 us
  waiting for transfers between devices  39.1 us (25%)
  starting transfers between devices  36.5 us (24%)
  blocking collectives  33.1 us (21%)
  Pallas kernels  29.1 us (19%)
  local copies, waits for them, and re-layouts  7.46 us (5%)
  between operations  5.22 us (3%)
  other arithmetic  2.68 us (2%)
    all_to_all x2, waiting for transfers between devices, exchange(): return lax.all_to_all(a, 'ctx', 0, 0, axis_index_groups=same, tiled=True)  36.2 us
    all_gather x1, blocking collectives, body(): lax.all_gather(z, 'dp')  33.1 us
    pallas_call x1, Pallas kernels, attention(): pl.pallas_call(attention_body, out_shape=(jax.ShapeDtypeStruct((half, BLK...  23.5 us
    all_to_all x2, starting transfers between devices, exchange(): return lax.all_to_all(a, 'ctx', 0, 0, axis_index_groups=same, tiled=True)  17.6 us
    ppermute x1, starting transfers between devices, body(): z_own = (z_mine + lax.ppermute(z_mate, 'ctx', mates))[None]  8.74 us
    ppermute x1, starting transfers between devices, body(): mate = lax.ppermute(recv[:, :, 4 * HD:], 'ctx', mates)  8.24 us
    pallas_call x1, Pallas kernels, pack(): pl.pallas_call(pack_body, out_shape=jax.ShapeDtypeStruct(shape, queries.d...  3.82 us
    unnamed x10, local copies, waits for them, and re-layouts  3.39 us
  transfers between devices with their start and end apart: 5, of which 2 were waited for; matrix products, arithmetic and copies ran while one was open for 3% of the time, Pallas kernels for 0%

profile of v4, /device:TPU:1, one launch (start us, length us, event | category | flops | bytes accessed | tf_op | source)
XLA Modules:
  0.0 153.2 jit_solution(11645463747800361748)
XLA Ops:
  0.6 0.0 copy-start
  0.6 3.8 %pack.1 = bf16[16,128,768]{2,1,0:T(8,128)(2,1)} custom-call(bf16[1,128,4096]{2,1,0:T(8,128)(2,1)} %q_ref.1, bf16[1,128,4096]{2,1,0:T(8,128)(2,1)} %g_ref.1, bf16[1,128,1024]{2,1,0:T(8,128)(2,1)} %k_ref.1, bf16[1,128,1024]{2,1,0:T(8,128)(2,1)} %v_ref.1), custom_call_target="tpu_custom_call" | custom-call | tf_op jit(solution)/shard_map/pack/pallas_call | solution.py:270
  4.5 7.6 %all-to-all-start = ((bf16[16,128,768]{2,1,0:T(8,128)(2,1)}), bf16[16,128,768]{2,1,0:T(8,128)(2,1)}, u32[]{:S(2)}, u32[]{:S(2)}) async-start(bf16[16,128,768]{2,1,0:T(8,128)(2,1)} %pack.1), calls=%async_computation | async-start | bytes 6291456 | tf_op jit(solution)/shard_map/all_to_all | solution.py:404
  12.2 0.1 compare_reduce_fusion
  12.3 0.1 iota_compare_fusion.2
  12.4 0.4 fusion.8
  12.7 0.1 copy.43
  12.8 0.1 reduce_max.9
  12.9 0.7 copy.48.cnt_ref
  13.6 0.1 copy.44
  13.7 36.2 %all-to-all-done.qd_ref.own_ref = bf16[16,128,768]{2,1,0:T(8,128)(2,1)} async-done(((bf16[16,128,768]{2,1,0:T(8,128)(2,1)}), bf16[16,128,768]{2,1,0:T(8,128)(2,1)}, u32[]{:S(2)}, u32[]{:S(2)}) %all-to-all-start) | async-done | bytes 3145760 | tf_op jit(solution)/shard_map/all_to_all | solution.py:404
  49.9 1.3 slice.18
  51.2 8.2 %collective-permute-start = (bf16[16,128,256]{2,1,0:T(8,128)(2,1)S(1)}, bf16[16,128,256]{2,1,0:T(8,128)(2,1)S(1)}, u32[]{:S(2)}, u32[]{:S(2)}) collective-permute-start(bf16[16,128,256]{2,1,0:T(8,128)(2,1)S(1)} %slice.18), channel_id=1, source_target_pairs={{0,1},{1,0},{2,3},{3,2},{4,5},{5,4},{6,7},{7,6},{8,9},{9,8},{10,11... | collective-permute-start | bytes 3145736 | tf_op jit(solution)/shard_map/ppermute | solution.py:407
  59.6 0.6 multiply_reduce_fusion
  60.2 0.6 select_reduce_fusion
  60.8 0.7 reshape.142.cols_ref
  61.5 0.6 fusion.4.steps_ref
  62.1 0.5 broadcast_in_dim.18.edge_ref
  62.6 0.4 copy-done.4
  63.1 23.5 %block_attention.1 = (bf16[16,128,512]{2,1,0:T(8,128)(2,1)}, bf16[16,128,256]{2,1,0:T(8,128)(2,1)}, f32[8,128]{1,0:T(8,128)}) custom-call(s32[8,128]{1,0:T(8,128)} %reshape.142.cols_ref, s32[8,4]{1,0:T(8,128)} %copy.48.cnt_ref, s32[8,1]{1,0:T(8,128)} %fusion.4.steps_ref, s32[1,3]{1,0:T(1,128)} %broadcast_in_dim.18.edge_ref, ...), custom_call_target="tpu_custom_call" | custom-call | flops 40000000000 | bytes 9000000 | tf_op jit(solution)/shard_map/block_attention/pallas_call | solution.py:197
  86.6 1.9 %collective-permute-start.1 = (bf16[16,128,256]{2,1,0:T(8,128)(2,1)}, bf16[16,128,256]{2,1,0:T(8,128)(2,1)S(1)}, u32[]{:S(2)}, u32[]{:S(2)}) collective-permute-start(bf16[16,128,256]{2,1,0:T(8,128)(2,1)} %get-tuple-element.13), channel_id=1, source_target_pairs={{0,1},{1,0},{2,3},{3,2},{4,5},{5,4},{6,7},{7,6},{8,9},{9,8},{10,11... | collective-permute-start | bytes 3145736 | tf_op jit(solution)/shard_map/ppermute | solution.py:412
  88.5 2.8 %collective-permute-done.1.got_ref = bf16[16,128,256]{2,1,0:T(8,128)(2,1)S(1)} collective-permute-done((bf16[16,128,256]{2,1,0:T(8,128)(2,1)}, bf16[16,128,256]{2,1,0:T(8,128)(2,1)S(1)}, u32[]{:S(2)}, u32[]{:S(2)}) %collective-permute-start.1) | collective-permute-done | bytes 1048608 | tf_op jit(solution)/shard_map/ppermute | solution.py:412
  91.4 1.6 %copy-done.1 = bf16[16,128,512]{2,1,0:T(8,128)(2,1)S(1)} copy-done((bf16[16,128,512]{2,1,0:T(8,128)(2,1)S(1)}, bf16[16,128,512]{2,1,0:T(8,128)(2,1)}, u32[]{:S(2)}) %copy-start.1) | copy-done | bytes 2097176
  93.0 0.5 merge.1
  93.5 1.3 copy-done.2
  94.8 10.0 %all-to-all-start.1 = ((bf16[16,128,512]{2,1,0:T(8,128)(2,1)}), bf16[16,128,512]{2,1,0:T(8,128)(2,1)S(1)}, u32[]{:S(2)}, u32[]{:S(2)}) async-start(bf16[16,128,512]{2,1,0:T(8,128)(2,1)} %copy-done.2), calls=%async_computation.1 | async-start | bytes 4194304 | tf_op jit(solution)/shard_map/all_to_all | solution.py:404
  104.8 33.1 %all-gather = f32[128,128]{1,0:T(8,128)S(1)} all-gather(f32[8,128]{1,0:T(8,128)S(1)} %copy-done.3), channel_id=2, replica_groups=mesh['dp'=16,'ctx'=32] {'dp'}, dimensions={0}, use_global_device_ids=true | all-gather | bytes 69632 | tf_op jit(solution)/shard_map/all_gather | solution.py:415
  138.0 0.1 reduce.2
  138.1 0.1 reshape.144
  138.2 0.6 fusion.9
  141.4 8.7 %collective-permute-start.2 = (f32[]{:T(128)}, f32[]{:T(128)}, u32[]{:S(2)}, u32[]{:S(2)}) collective-permute-start(f32[]{:T(128)} %select_n.69), channel_id=1, source_target_pairs={{0,1},{1,0},{2,3},{3,2},{4,5},{5,4},{6,7},{7,6},{8,9},{9,8},{10,11... | collective-permute-start | bytes 20 | tf_op jit(solution)/shard_map/ppermute | solution.py:418
  150.7 1.3 unpack.1
  (23 shorter events, 0.1 us)
Async XLA Ops:
  0.6 11.5 %copy-start = (s32[32,32,32]{2,1,0:T(8,128)S(1)}, s32[32,32,32]{2,1,0:T(8,128)}, u32[]{:S(2)}) copy-start(s32[32,32,32]{2,1,0:T(8,128)} %param.9) | copy-start | bytes 393220
  4.5 45.4 %all-to-all-start = ((bf16[16,128,768]{2,1,0:T(8,128)(2,1)}), bf16[16,128,768]{2,1,0:T(8,128)(2,1)}, u32[]{:S(2)}, u32[]{:S(2)}) async-start(bf16[16,128,768]{2,1,0:T(8,128)(2,1)} %pack.1), calls=%async_computation | async-start | bytes 6291456 | tf_op jit(solution)/shard_map/all_to_all | solution.py:404
  51.2 10.9 %collective-permute-start = (bf16[16,128,256]{2,1,0:T(8,128)(2,1)S(1)}, bf16[16,128,256]{2,1,0:T(8,128)(2,1)S(1)}, u32[]{:S(2)}, u32[]{:S(2)}) collective-permute-start(bf16[16,128,256]{2,1,0:T(8,128)(2,1)S(1)} %slice.18), channel_id=1, source_target_pairs={{0,1},{1,0},{2,3},{3,2},{4,5},{5,4},{6,7},{7,6},{8,9},{9,8},{10,11... | collective-permute-start | bytes 3145736 | tf_op jit(solution)/shard_map/ppermute | solution.py:407
  62.1 1.0 copy-start.4
  86.6 4.8 %collective-permute-start.1 = (bf16[16,128,256]{2,1,0:T(8,128)(2,1)}, bf16[16,128,256]{2,1,0:T(8,128)(2,1)S(1)}, u32[]{:S(2)}, u32[]{:S(2)}) collective-permute-start(bf16[16,128,256]{2,1,0:T(8,128)(2,1)} %get-tuple-element.13), channel_id=1, source_target_pairs={{0,1},{1,0},{2,3},{3,2},{4,5},{5,4},{6,7},{7,6},{8,9},{9,8},{10,11... | collective-permute-start | bytes 3145736 | tf_op jit(solution)/shard_map/ppermute | solution.py:412
  91.4 1.6 %copy-start.1 = (bf16[16,128,512]{2,1,0:T(8,128)(2,1)S(1)}, bf16[16,128,512]{2,1,0:T(8,128)(2,1)}, u32[]{:S(2)}) copy-start(bf16[16,128,512]{2,1,0:T(8,128)(2,1)} %get-tuple-element.12.send_ref) | copy-start | bytes 6291460
  93.5 1.4 copy-start.2
  94.8 10.0 %copy-start.3 = (f32[8,128]{1,0:T(8,128)S(1)}, f32[8,128]{1,0:T(8,128)}, u32[]{:S(2)}) copy-start(f32[8,128]{1,0:T(8,128)} %get-tuple-element.19) | copy-start | bytes 12292
  94.8 55.9 %all-to-all-start.1 = ((bf16[16,128,512]{2,1,0:T(8,128)(2,1)}), bf16[16,128,512]{2,1,0:T(8,128)(2,1)S(1)}, u32[]{:S(2)}, u32[]{:S(2)}) async-start(bf16[16,128,512]{2,1,0:T(8,128)(2,1)} %copy-done.2), calls=%async_computation.1 | async-start | bytes 4194304 | tf_op jit(solution)/shard_map/all_to_all | solution.py:404
  141.4 8.7 %collective-permute-start.2 = (f32[]{:T(128)}, f32[]{:T(128)}, u32[]{:S(2)}, u32[]{:S(2)}) collective-permute-start(f32[]{:T(128)} %select_n.69), channel_id=1, source_target_pairs={{0,1},{1,0},{2,3},{3,2},{4,5},{5,4},{6,7},{7,6},{8,9},{9,8},{10,11... | collective-permute-start | bytes 20 | tf_op jit(solution)/shard_map/ppermute | solution.py:418

commit v5 on v4

--- a/solution.py
+++ b/solution.py
@@ -12,7 +12,7 @@
 HD = 128
 BLK = 128
 PAIR = 2
-ROWS = 2
+ROWS = 4
 Z_ROWS = 8
 
 ZLOSS = 0.05
@@ -281,7 +281,7 @@
     )(queries, out_grad, keys, values)
 
 
-def merge_body(send_ref, got_ref, out_ref, own_s, in_sem, out_sem):
+def merge_body(send_ref, got_ref, out_ref, own_s, got_s, in_sem, got_sem, out_sem):
     parts = in_sem.shape[0]
     part = own_s.shape[0] // parts
 
@@ -296,12 +296,15 @@
         pltpu.make_async_copy(own_s.at[cut(n)], out_ref.at[cut(n), :, pl.ds(2 * HD, 2 * HD)], out_sem.at[n])
         for n in range(parts)
     ]
-    for copy in loads:
-        copy.start()
+    gets = [pltpu.make_async_copy(got_ref.at[cut(n)], got_s.at[cut(n)], got_sem.at[n]) for n in range(parts)]
+    for n in range(parts):
+        loads[n].start()
+        gets[n].start()
     for n in range(parts):
         loads[n].wait()
+        gets[n].wait()
         rows = slice(n * part, (n + 1) * part)
-        both = own_s[rows].astype(jnp.float32) + got_ref[rows].astype(jnp.float32)
+        both = own_s[rows].astype(jnp.float32) + got_s[rows].astype(jnp.float32)
         own_s[rows] = both.astype(own_s.dtype)
         stores[n].start()
     for copy in stores:
@@ -312,15 +315,17 @@
     return pl.pallas_call(
         merge_body,
         out_shape=jax.ShapeDtypeStruct(send.shape, send.dtype),
-        in_specs=[pl.BlockSpec(memory_space=pl.ANY), pl.BlockSpec(memory_space=pltpu.VMEM)],
+        in_specs=[pl.BlockSpec(memory_space=pl.ANY)] * 2,
         out_specs=pl.BlockSpec(memory_space=pl.ANY),
         scratch_shapes=[
             pltpu.VMEM(got.shape, got.dtype),
+            pltpu.VMEM(got.shape, got.dtype),
+            pltpu.SemaphoreType.DMA((4,)),
             pltpu.SemaphoreType.DMA((4,)),
             pltpu.SemaphoreType.DMA((4,)),
         ],
         input_output_aliases={0: 0},
-        compiler_params=pltpu.CompilerParams(vmem_limit_bytes=16 << 20),
+        compiler_params=pltpu.CompilerParams(vmem_limit_bytes=60 << 20),
         name="merge",
     )(send, got)
 
@@ -403,19 +408,19 @@
     def exchange(a):
         return lax.all_to_all(a, "ctx", 0, 0, axis_index_groups=same, tiled=True)
 
-    recv = exchange(pack(queries, out_grad, keys, values))
+    mask = lax.dynamic_slice(block_mask, (chip * PAIR, 0, 0), (PAIR, blocks, blocks))
+    recv, lists = lax.optimization_barrier(
+        (exchange(pack(queries, out_grad, keys, values)), work_lists(mask, core))
+    )
     mate = lax.ppermute(recv[:, :, 4 * HD :], "ctx", mates)
-
-    mask = lax.dynamic_slice(block_mask, (chip * PAIR, 0, 0), (PAIR, blocks, blocks))
-    send, give, z = attention(recv, mate, *work_lists(mask, core))
-
-    send = merge(send, lax.ppermute(give, "ctx", mates))
-    send, z = lax.optimization_barrier((send, z))
+    send, give, z = attention(recv, mate, *lists)
+
+    got = lax.ppermute(give, "ctx", mates)
+    z_mine = jnp.where(core == 0, z[:1], z[1:2])
+    z_mine = z_mine + lax.ppermute(jnp.where(core == 0, z[1:2], z[:1]), "ctx", mates)
+    send, z_mine = lax.optimization_barrier((merge(send, got), z_mine))
     back = exchange(send)
-    z_two = jnp.sum(lax.all_gather(z, "dp"), axis=(0, 2))[:PAIR] * (ZLOSS / (dps * blocks * BLK))
-    z_mine = jnp.where(core == 0, z_two[0], z_two[1])
-    z_mate = jnp.where(core == 0, z_two[1], z_two[0])
-    z_own = (z_mine + lax.ppermute(z_mate, "ctx", mates))[None]
+    z_own = jnp.sum(lax.all_gather(z_mine, "dp"))[None] * (ZLOSS / (dps * blocks * BLK))
     query_grad, key_grad, value_grad = unpack(back)
     return query_grad, key_grad, value_grad, z_own
 

time: 154 us -> 144 us (0.935)
  the two profiles are of different devices: /device:TPU:1 before, /device:TPU:2 now
where the time goes in v5:
time: 144 us; the launch traced here: 143 us
  blocking collectives  38.1 us (26%)
  waiting for transfers between devices  36.5 us (25%)
  starting transfers between devices  30.8 us (21%)
  Pallas kernels  25.5 us (18%)
  local copies, waits for them, and re-layouts  5.31 us (4%)
  other arithmetic  4.48 us (3%)
  between operations  2.58 us (2%)
    all_gather x1, blocking collectives, body(): lax.all_gather(z_mine, 'dp')  38.1 us
    all_to_all x2, waiting for transfers between devices, exchange(): return lax.all_to_all(a, 'ctx', 0, 0, axis_index_groups=same, tiled=True)  33.5 us
    all_to_all x2, starting transfers between devices, exchange(): return lax.all_to_all(a, 'ctx', 0, 0, axis_index_groups=same, tiled=True)  23.9 us
    pallas_call x1, Pallas kernels, attention(): pl.pallas_call(attention_body, out_shape=(jax.ShapeDtypeStruct((half, BLK...  18 us
    pallas_call x1, Pallas kernels, pack(): pl.pallas_call(pack_body, out_shape=jax.ShapeDtypeStruct(shape, queries.d...  3.82 us
    ppermute x1, starting transfers between devices, body(): got = lax.ppermute(give, 'ctx', mates)  3.13 us
  transfers between devices with their start and end apart: 5, of which 3 were waited for; matrix products, arithmetic and copies ran while one was open for 4% of the time, Pallas kernels for 0%

profile of v5, /device:TPU:2, one launch (start us, length us, event | category | flops | bytes accessed | tf_op | source)
XLA Modules:
  0.0 143.4 jit_solution(11352460301193419237)
XLA Ops:
  0.6 0.0 copy-start
  0.6 3.8 %pack.1 = bf16[16,128,768]{2,1,0:T(8,128)(2,1)} custom-call(bf16[1,128,4096]{2,1,0:T(8,128)(2,1)} %q_ref.1, bf16[1,128,4096]{2,1,0:T(8,128)(2,1)} %g_ref.1, bf16[1,128,1024]{2,1,0:T(8,128)(2,1)} %k_ref.1, bf16[1,128,1024]{2,1,0:T(8,128)(2,1)} %v_ref.1), custom_call_target="tpu_custom_call" | custom-call | tf_op jit(solution)/shard_map/pack/pallas_call | solution.py:270
  4.5 10.1 %all-to-all-start = ((bf16[16,128,768]{2,1,0:T(8,128)(2,1)}), bf16[16,128,768]{2,1,0:T(8,128)(2,1)}, u32[]{:S(2)}, u32[]{:S(2)}) async-start(bf16[16,128,768]{2,1,0:T(8,128)(2,1)} %pack.1), calls=%async_computation | async-start | bytes 6291456 | tf_op jit(solution)/shard_map/all_to_all | solution.py:409
  14.7 0.1 iota_compare_fusion.2
  14.8 0.2 fusion.5
  15.0 0.1 copy.35
  15.1 0.1 reduce_max.9
  15.2 0.1 copy.36
  15.4 0.6 multiply_reduce_fusion
  16.0 0.6 select_reduce_fusion
  16.6 0.7 reshape.144.cols_ref
  17.3 0.6 fusion.3.steps_ref
  17.9 33.5 %all-to-all-done.qd_ref.own_ref = bf16[16,128,768]{2,1,0:T(8,128)(2,1)} async-done(((bf16[16,128,768]{2,1,0:T(8,128)(2,1)}), bf16[16,128,768]{2,1,0:T(8,128)(2,1)}, u32[]{:S(2)}, u32[]{:S(2)}) %all-to-all-start) | async-done | bytes 3145760 | tf_op jit(solution)/shard_map/all_to_all | solution.py:409
  51.4 0.5 broadcast_in_dim.16.edge_ref
  51.9 1.3 slice.11
  53.2 1.9 %collective-permute-start = (bf16[16,128,256]{2,1,0:T(8,128)(2,1)S(1)}, bf16[16,128,256]{2,1,0:T(8,128)(2,1)S(1)}, u32[]{:S(2)}, u32[]{:S(2)}) collective-permute-start(bf16[16,128,256]{2,1,0:T(8,128)(2,1)S(1)} %slice.11), channel_id=1, source_target_pairs={{0,1},{1,0},{2,3},{3,2},{4,5},{5,4},{6,7},{7,6},{8,9},{9,8},{10,11... | collective-permute-start | bytes 3145736 | tf_op jit(solution)/shard_map/ppermute | solution.py:415
  55.1 0.7 copy.40.cnt_ref
  55.8 2.0 %collective-permute-done.mate_ref = bf16[16,128,256]{2,1,0:T(8,128)(2,1)S(1)} collective-permute-done((bf16[16,128,256]{2,1,0:T(8,128)(2,1)S(1)}, bf16[16,128,256]{2,1,0:T(8,128)(2,1)S(1)}, u32[]{:S(2)}, u32[]{:S(2)}) %collective-permute-start) | collective-permute-done | bytes 1048608 | tf_op jit(solution)/shard_map/ppermute | solution.py:415
  57.8 1.0 copy-done.2
  58.7 18.0 %block_attention.1 = (bf16[16,128,512]{2,1,0:T(8,128)(2,1)}, bf16[16,128,256]{2,1,0:T(8,128)(2,1)}, f32[8,128]{1,0:T(8,128)}) custom-call(s32[4,256]{1,0:T(4,128)} %reshape.144.cols_ref, s32[4,8]{1,0:T(4,128)} %copy.40.cnt_ref, s32[4,1]{1,0:T(4,128)} %fusion.3.steps_ref, s32[1,3]{1,0:T(1,128)} %broadcast_in_dim.16.edge_ref, ...), custom_call_target="tpu_custom_call" | custom-call | flops 40000000000 | bytes 9000000 | tf_op jit(solution)/shard_map/block_attention/pallas_call | solution.py:197
  76.8 3.1 %collective-permute-start.1 = (bf16[16,128,256]{2,1,0:T(8,128)(2,1)}, bf16[16,128,256]{2,1,0:T(8,128)(2,1)S(1)}, u32[]{:S(2)}, u32[]{:S(2)}) collective-permute-start(bf16[16,128,256]{2,1,0:T(8,128)(2,1)} %get-tuple-element.23), channel_id=1, source_target_pairs={{0,1},{1,0},{2,3},{3,2},{4,5},{5,4},{6,7},{7,6},{8,9},{9,8},{10,11... | collective-permute-start | bytes 3145736 | tf_op jit(solution)/shard_map/ppermute | solution.py:418
  79.9 0.8 broadcast_select_fusion
  80.7 1.9 %collective-permute-start.2 = (f32[1,128]{1,0:T(1,128)S(1)}, f32[1,128]{1,0:T(1,128)S(1)}, u32[]{:S(2)}, u32[]{:S(2)}) collective-permute-start(f32[1,128]{1,0:T(1,128)S(1)} %broadcast_select_fusion), channel_id=1, source_target_pairs={{0,1},{1,0},{2,3},{3,2},{4,5},{5,4},{6,7},{7,6},{8,9},{9,8},{10,11... | collective-permute-start | bytes 1544 | tf_op jit(solution)/shard_map/ppermute | solution.py:420
  82.6 1.1 collective-permute-done.2
  83.7 0.8 fusion.8
  84.4 1.0 copy-done.1
  85.4 2.4 %merge.1 = bf16[16,128,512]{2,1,0:T(8,128)(2,1)} custom-call(bf16[16,128,512]{2,1,0:T(8,128)(2,1)} %get-tuple-element.22.send_ref, bf16[16,128,256]{2,1,0:T(8,128)(2,1)} %copy-done.1), custom_call_target="tpu_custom_call", output_to_operand_aliasing={{}: (0, {})} | custom-call | tf_op jit(solution)/shard_map/merge/pallas_call | solution.py:315
  87.8 13.7 %all-to-all-start.1 = ((bf16[16,128,512]{2,1,0:T(8,128)(2,1)}), bf16[16,128,512]{2,1,0:T(8,128)(2,1)S(1)}, u32[]{:S(2)}, u32[]{:S(2)}) async-start(bf16[16,128,512]{2,1,0:T(8,128)(2,1)} %merge.1), calls=%async_computation.1 | async-start | bytes 4194304 | tf_op jit(solution)/shard_map/all_to_all | solution.py:409
  101.6 38.1 %all-gather.1 = f32[16,1,128]{2,1,0:T(1,128)S(1)} all-gather(f32[1,1,128]{2,1,0:T(1,128)S(1)} %bitcast.18), channel_id=2, replica_groups=mesh['dp'=16,'ctx'=32] {'dp'}, dimensions={0}, use_global_device_ids=true | all-gather | bytes 8704 | tf_op jit(solution)/shard_map/all_gather | solution.py:423
  139.7 0.6 reduce.2
  140.9 0.0 all-to-all-done.1.back_ref
  140.9 1.3 unpack.1
  (15 shorter events, 0.1 us)
Async XLA Ops:
  0.6 14.0 %copy-start = (s32[32,32,32]{2,1,0:T(8,128)S(1)}, s32[32,32,32]{2,1,0:T(8,128)}, u32[]{:S(2)}) copy-start(s32[32,32,32]{2,1,0:T(8,128)} %param.9) | copy-start | bytes 393220
  4.5 46.9 %all-to-all-start = ((bf16[16,128,768]{2,1,0:T(8,128)(2,1)}), bf16[16,128,768]{2,1,0:T(8,128)(2,1)}, u32[]{:S(2)}, u32[]{:S(2)}) async-start(bf16[16,128,768]{2,1,0:T(8,128)(2,1)} %pack.1), calls=%async_computation | async-start | bytes 6291456 | tf_op jit(solution)/shard_map/all_to_all | solution.py:409
  53.2 4.6 %collective-permute-start = (bf16[16,128,256]{2,1,0:T(8,128)(2,1)S(1)}, bf16[16,128,256]{2,1,0:T(8,128)(2,1)S(1)}, u32[]{:S(2)}, u32[]{:S(2)}) collective-permute-start(bf16[16,128,256]{2,1,0:T(8,128)(2,1)S(1)} %slice.11), channel_id=1, source_target_pairs={{0,1},{1,0},{2,3},{3,2},{4,5},{5,4},{6,7},{7,6},{8,9},{9,8},{10,11... | collective-permute-start | bytes 3145736 | tf_op jit(solution)/shard_map/ppermute | solution.py:415
  57.8 1.0 copy-start.2
  76.8 7.7 %collective-permute-start.1 = (bf16[16,128,256]{2,1,0:T(8,128)(2,1)}, bf16[16,128,256]{2,1,0:T(8,128)(2,1)S(1)}, u32[]{:S(2)}, u32[]{:S(2)}) collective-permute-start(bf16[16,128,256]{2,1,0:T(8,128)(2,1)} %get-tuple-element.23), channel_id=1, source_target_pairs={{0,1},{1,0},{2,3},{3,2},{4,5},{5,4},{6,7},{7,6},{8,9},{9,8},{10,11... | collective-permute-start | bytes 3145736 | tf_op jit(solution)/shard_map/ppermute | solution.py:418
  80.7 3.0 %collective-permute-start.2 = (f32[1,128]{1,0:T(1,128)S(1)}, f32[1,128]{1,0:T(1,128)S(1)}, u32[]{:S(2)}, u32[]{:S(2)}) collective-permute-start(f32[1,128]{1,0:T(1,128)S(1)} %broadcast_select_fusion), channel_id=1, source_target_pairs={{0,1},{1,0},{2,3},{3,2},{4,5},{5,4},{6,7},{7,6},{8,9},{9,8},{10,11... | collective-permute-start | bytes 1544 | tf_op jit(solution)/shard_map/ppermute | solution.py:420
  84.4 1.0 copy-start.1
  87.8 53.1 %all-to-all-start.1 = ((bf16[16,128,512]{2,1,0:T(8,128)(2,1)}), bf16[16,128,512]{2,1,0:T(8,128)(2,1)S(1)}, u32[]{:S(2)}, u32[]{:S(2)}) async-start(bf16[16,128,512]{2,1,0:T(8,128)(2,1)} %merge.1), calls=%async_computation.1 | async-start | bytes 4194304 | tf_op jit(solution)/shard_map/all_to_all | solution.py:409

commit v6 on v5

--- a/solution.py
+++ b/solution.py
@@ -13,6 +13,7 @@
 BLK = 128
 PAIR = 2
 ROWS = 4
+GROUP = 8
 Z_ROWS = 8
 
 ZLOSS = 0.05
@@ -25,10 +26,10 @@
 
 
 def attention_body(
-    cols_ref, cnt_ref, steps_ref, edge_ref,
+    half_ref, lane_ref, groups_ref, edge_ref,
     qd_ref, own_ref, mate_ref,
     send_ref, give_ref, z_ref,
-    kv_s, e_s, dp_s, m_s, dk_s, dv_s, kt_s, dqt_s, sem,
+    kv_s, qg_s, e_s, dp_s, m_s, top_s, sum_s, pull_s, dk_s, dv_s, kt_s, dqt_s, sem,
 ):
     step = pl.program_id(0)
     blocks = kv_s.shape[0]
@@ -57,6 +58,13 @@
     lanes = [(s, j) for s in range(ROWS) for j in range(PAIR)]
     qs = [qd_ref[s, :, j * HD : (j + 1) * HD] for s, j in lanes]
     gs = [qd_ref[s, :, (PAIR + j) * HD : (PAIR + j + 1) * HD] for s, j in lanes]
+    for n in range(len(lanes)):
+        qg_s[n, :, :HD] = qs[n]
+        qg_s[n, :, HD:] = gs[n]
+    base = e_s.shape[0] - len(lanes)
+
+    def wide(x):
+        return jnp.broadcast_to(x, (8, BLK))
 
     def dot(a, b):
         return jnp.dot(a, b, preferred_element_type=jnp.float32)
@@ -72,7 +80,7 @@
     key_pos = lax.broadcasted_iota(jnp.int32, (BLK, BLK), 0)
     query_pos = lax.broadcasted_iota(jnp.int32, (BLK, BLK), 1)
     causal = key_pos <= query_pos
-    state, row_q, row_g, diags = [], [], [], []
+    row_q, row_g, diags = [], [], []
     for s in range(ROWS):
         diag = core * half + ROWS * step + s
         diags.append(diag)
@@ -91,62 +99,60 @@
             m = jnp.max(sc, axis=0, keepdims=True)
             e = jnp.exp2(sc - m)
             n = s * PAIR + j
-            e_s[0, n] = e
-            dp_s[0, n] = dp
-            m_s[0, n] = jnp.broadcast_to(m, (8, BLK))
-            state += [m, jnp.sum(e, axis=0, keepdims=True), jnp.sum(e * dp, axis=0, keepdims=True)]
-
-    def entry(t, n):
-        slot = 2 * (t - 1)
-        return slot, cols_ref[step, n * blocks + slot], cols_ref[step, n * blocks + slot + 1]
-
-    def forward(t, state):
-        out = []
-        for n in range(len(lanes)):
-            m, l, u = state[3 * n : 3 * n + 3]
-            slot, c1, c2 = entry(t, n)
-            count = cnt_ref[step, n]
-            b1 = jnp.where(slot < count, 0.0, NEG).astype(jnp.float32)
-            b2 = jnp.where(slot + 1 < count, 0.0, NEG).astype(jnp.float32)
-            k, v = pair(c1, c2)
-            sc = dot_nt(k, qs[n]) * (SCALE * LOG2E)
+            e_s[base + n] = e
+            dp_s[base + n] = dp
+            m_s[base + n] = wide(m)
+            top_s[n] = wide(m)
+            sum_s[n] = wide(jnp.sum(e, axis=0, keepdims=True))
+            pull_s[n] = wide(jnp.sum(e * dp, axis=0, keepdims=True))
+
+    def entry(i):
+        h1, h2 = half_ref[step, 2 * i], half_ref[step, 2 * i + 1]
+        return lane_ref[step, i], h1, h2, jnp.maximum(h1 - 1, 0), jnp.maximum(h2 - 1, 0)
+
+    groups = groups_ref[step, 0]
+
+    @pl.loop(0, groups)
+    def _(g):
+        for k in range(GROUP):
+            i = g * GROUP + k
+            n, h1, h2, c1, c2 = entry(i)
+            b1 = jnp.where(h1 > 0, 0.0, NEG).astype(jnp.float32)
+            b2 = jnp.where(h2 > 0, 0.0, NEG).astype(jnp.float32)
+            key, value = pair(c1, c2)
+            sc = dot_nt(key, qg_s[n, :, :HD]) * (SCALE * LOG2E)
             sc = jnp.concatenate([sc[:BLK] + b1, sc[BLK:] + b2], axis=0)
-            dp = dot_nt(v, gs[n])
-            m_new = jnp.maximum(m, jnp.max(sc, axis=0, keepdims=True))
-            e = jnp.exp2(sc - m_new)
-            alpha = jnp.exp2(m - m_new)
-            e_s[t, n] = e
-            dp_s[t, n] = dp
-            m_s[t, n] = jnp.broadcast_to(m_new, (8, BLK))
-            out += [
-                m_new,
-                l * alpha + jnp.sum(e, axis=0, keepdims=True),
-                u * alpha + jnp.sum(e * dp, axis=0, keepdims=True),
-            ]
-        return tuple(out)
-
-    steps = steps_ref[step, 0]
-    state = lax.fori_loop(1, steps, forward, tuple(state))
-
-    top, inv, pull = [], [], []
+            dp = dot_nt(value, qg_s[n, :, HD:])
+            m = jnp.max(sc, axis=0, keepdims=True)
+            e = jnp.exp2(sc - m)
+            e_s[i] = e
+            dp_s[i] = dp
+            m = wide(m)
+            m_s[i] = m
+            old = top_s[n]
+            new = jnp.maximum(old, m)
+            keep, take = jnp.exp2(old - new), jnp.exp2(m - new)
+            top_s[n] = new
+            sum_s[n] = sum_s[n] * keep + wide(jnp.sum(e, axis=0, keepdims=True)) * take
+            pull_s[n] = pull_s[n] * keep + wide(jnp.sum(e * dp, axis=0, keepdims=True)) * take
+
     for n, (s, j) in enumerate(lanes):
-        m, l, u = state[3 * n : 3 * n + 3]
+        l = sum_s[n]
         inv_l = 1.0 / l
-        log_norm = m * LN2 + jnp.log(l)
-        top.append(m)
-        inv.append(inv_l)
-        pull.append((2.0 * ZLOSS) * log_norm - u * inv_l)
-        z_ref[j : j + 1, :] += log_norm * log_norm
-
-    def weights(t, n):
-        factor = jnp.exp2(m_s[t, n][:1] - top[n]) * inv[n]
-        probs = e_s[t, n] * factor
-        dscore = probs * (dp_s[t, n] + pull[n])
+        log_norm = top_s[n] * LN2 + jnp.log(l)
+        sum_s[n] = inv_l
+        pull_s[n] = (2.0 * ZLOSS) * log_norm - pull_s[n] * inv_l
+        z_ref[j : j + 1, :] += log_norm[:1] * log_norm[:1]
+
+    def weights(i, n):
+        factor = (jnp.exp2(m_s[i] - top_s[n]) * sum_s[n])[:1]
+        probs = e_s[i] * factor
+        dscore = probs * (dp_s[i] + pull_s[n][:1])
         return probs.astype(jnp.bfloat16), dscore.astype(jnp.bfloat16)
 
     dk0, dv0 = [], []
     for s in range(ROWS):
-        first = [weights(0, s * PAIR + j) for j in range(PAIR)]
+        first = [weights(base + s * PAIR + j, s * PAIR + j) for j in range(PAIR)]
         p_all = jnp.concatenate([w[0] for w in first], axis=1)
         d_all = jnp.concatenate([w[1] for w in first], axis=1)
         dk = dot(d_all, row_q[s])
@@ -161,13 +167,14 @@
     dk_s[0] += sum(dk0[1:], dk0[0])
     dv_s[0] += sum(dv0[1:], dv0[0])
 
-    @pl.loop(1, steps)
-    def _(t):
-        for n in range(len(lanes)):
-            _, c1, c2 = entry(t, n)
-            p_low, d_low = weights(t, n)
-            dk = dot(d_low, qs[n])
-            dv = dot(p_low, gs[n])
+    @pl.loop(0, groups)
+    def _(g):
+        for k in range(GROUP):
+            i = g * GROUP + k
+            n, _, _, c1, c2 = entry(i)
+            p_low, d_low = weights(i, n)
+            dk = dot(d_low, qg_s[n, :, :HD])
+            dv = dot(p_low, qg_s[n, :, HD:])
             dqt_s[n] += dot(jnp.concatenate([kt_s[c1], kt_s[c2]], axis=1), d_low)
             dk_s[c1] += dk[:BLK]
             dv_s[c1] += dv[:BLK]
@@ -189,11 +196,11 @@
             give_ref[i, :, HD:] = dv_s[other].astype(jnp.bfloat16)
 
 
-def attention(recv, mate, cols, cnt, steps, edge):
+def attention(recv, mate, halves, lane, groups, edge):
     half = recv.shape[0]
     blocks = 2 * half
     lanes = ROWS * PAIR
-    max_steps = half
+    items = half * lanes
     return pl.pallas_call(
         attention_body,
         out_shape=(
@@ -216,9 +223,13 @@
             ],
             scratch_shapes=[
                 pltpu.VMEM((blocks, BLK, 2 * HD), jnp.bfloat16),
-                pltpu.VMEM((max_steps, lanes, 2 * BLK, BLK), jnp.float32),
-                pltpu.VMEM((max_steps, lanes, 2 * BLK, BLK), jnp.float32),
-                pltpu.VMEM((max_steps, lanes, 8, BLK), jnp.float32),
+                pltpu.VMEM((lanes, BLK, 2 * HD), jnp.bfloat16),
+                pltpu.VMEM((items, 2 * BLK, BLK), jnp.float32),
+                pltpu.VMEM((items, 2 * BLK, BLK), jnp.float32),
+                pltpu.VMEM((items, 8, BLK), jnp.float32),
+                pltpu.VMEM((lanes, 8, BLK), jnp.float32),
+                pltpu.VMEM((lanes, 8, BLK), jnp.float32),
+                pltpu.VMEM((lanes, 8, BLK), jnp.float32),
                 pltpu.VMEM((blocks, BLK, HD), jnp.float32),
                 pltpu.VMEM((blocks, BLK, HD), jnp.float32),
                 pltpu.VMEM((blocks, HD, BLK), jnp.bfloat16),
@@ -227,13 +238,13 @@
             ],
         ),
         compiler_params=pltpu.CompilerParams(
-            dimension_semantics=("arbitrary",), vmem_limit_bytes=58 << 20
+            dimension_semantics=("arbitrary",), vmem_limit_bytes=51 << 20
         ),
         cost_estimate=pl.CostEstimate(
             flops=40_000_000_000, transcendentals=4_000_000, bytes_accessed=9_000_000
         ),
         name="block_attention",
-    )(cols, cnt, steps, edge, recv, recv, mate)
+    )(halves, lane, groups, edge, recv, recv, mate)
 
 
 def pack_body(q_ref, g_ref, k_ref, v_ref, out_ref, hold, in_sem, out_sem):
@@ -385,15 +396,23 @@
     own = (2 * jnp.arange(half, dtype=jnp.int32) + core).reshape(half // ROWS, ROWS)
     other = (mask > 0) & (col > 0) & (col != own[:, :, None, None])
     other = other.astype(jnp.int32).reshape(half // ROWS, ROWS * PAIR, blocks)
+    lanes = ROWS * PAIR
     before = (col[None, :] < col[:, None]).astype(jnp.int32)
     rank = jnp.sum(other[:, :, None, :] * before[None, None], axis=3)
-    place = col % 2 * half + col // 2
-    hit = (rank[:, :, None, :] == col[None, None, :, None]) & (other[:, :, None, :] > 0)
-    cols = jnp.sum(jnp.where(hit, place[None, None, None, :], 0), axis=3)
-    cnt = jnp.sum(other, axis=2)
-    steps = 1 + (jnp.max(cnt, axis=1) + 1) // 2
+    pairs = (jnp.sum(other, axis=2) + 1) // 2
+    ahead = jnp.arange(lanes, dtype=jnp.int32)
+    start = jnp.sum(jnp.where(ahead[None, :] < ahead[:, None], pairs[:, None, :], 0), axis=2)
+    slot = jnp.where(other > 0, 2 * start[:, :, None] + rank, -1)
+    place = col % 2 * half + col // 2 + 1
+    spots = jnp.arange(lanes * blocks, dtype=jnp.int32)
+    hit = slot[:, None] == spots[None, :, None, None]
+    halves = jnp.sum(jnp.where(hit, place, 0), axis=(2, 3))
+    item = jnp.arange(lanes * half, dtype=jnp.int32)
+    ends = start + pairs
+    lane = jnp.minimum(jnp.sum((ends[:, None, :] <= item[None, :, None]).astype(jnp.int32), axis=2), lanes - 1)
+    groups = (jnp.sum(pairs, axis=1, keepdims=True) + GROUP - 1) // GROUP
     edge = jnp.full((1, 3), core, jnp.int32)
-    return cols.reshape(half // ROWS, ROWS * PAIR * blocks), cnt, steps[:, None], edge
+    return halves, lane, groups, edge
 
 
 def body(queries, keys, values, out_grad, block_mask):
@@ -404,6 +423,7 @@
     chip, core = me // 2, me % 2
     same = [[2 * p + c for p in range(ctx // 2)] for c in range(2)]
     mates = [(i, i ^ 1) for i in range(ctx)]
+    wide = [[d * ctx + 2 * p + c for d in range(dps) for c in range(2)] for p in range(ctx // 2)]
 
     def exchange(a):
         return lax.all_to_all(a, "ctx", 0, 0, axis_index_groups=same, tiled=True)
@@ -416,11 +436,11 @@
     send, give, z = attention(recv, mate, *lists)
 
     got = lax.ppermute(give, "ctx", mates)
-    z_mine = jnp.where(core == 0, z[:1], z[1:2])
-    z_mine = z_mine + lax.ppermute(jnp.where(core == 0, z[1:2], z[:1]), "ctx", mates)
-    send, z_mine = lax.optimization_barrier((merge(send, got), z_mine))
+    send, z = lax.optimization_barrier((merge(send, got), z[:PAIR]))
     back = exchange(send)
-    z_own = jnp.sum(lax.all_gather(z_mine, "dp"))[None] * (ZLOSS / (dps * blocks * BLK))
+    z_all = lax.all_gather(z, ("dp", "ctx"), axis_index_groups=wide)
+    z_two = jnp.sum(z_all, axis=(0, 2)) * (ZLOSS / (dps * blocks * BLK))
+    z_own = jnp.where(core == 0, z_two[0], z_two[1])[None]
     query_grad, key_grad, value_grad = unpack(back)
     return query_grad, key_grad, value_grad, z_own
 

time: 144 us -> 137 us (0.951)
  the two profiles are of different devices: /device:TPU:2 before, /device:TPU:1 now
where the time goes in v6:
time: 137 us
  blocking collectives  41 us (30%)
  waiting for transfers between devices  40.2 us (29%)
  Pallas kernels  23.7 us (17%)
  starting transfers between devices  23.5 us (17%)
  between operations  3.32 us (2%)
  local copies, waits for them, and re-layouts  3.16 us (2%)
  other arithmetic  1.85 us (1%)
    all_gather x1, blocking collectives, body(): z_all = lax.all_gather(z, ('dp', 'ctx'), axis_index_groups=wide)  41 us
    all_to_all x2, waiting for transfers between devices, exchange(): return lax.all_to_all(a, 'ctx', 0, 0, axis_index_groups=same, tiled=True)  35.6 us
    pallas_call x1, Pallas kernels, attention(): pl.pallas_call(attention_body, out_shape=(jax.ShapeDtypeStruct((half, BLK...  16.2 us
    all_to_all x2, starting transfers between devices, exchange(): return lax.all_to_all(a, 'ctx', 0, 0, axis_index_groups=same, tiled=True)  13 us
    ppermute x1, starting transfers between devices, body(): mate = lax.ppermute(recv[:, :, 4 * HD:], 'ctx', mates)  8.24 us
    pallas_call x1, Pallas kernels, pack(): pl.pallas_call(pack_body, out_shape=jax.ShapeDtypeStruct(shape, queries.d...  3.82 us
  transfers between devices with their start and end apart: 4, of which 3 were waited for; matrix products, arithmetic and copies ran while one was open for 2% of the time, Pallas kernels for 0%

profile of v6, /device:TPU:1, one launch (start us, length us, event | category | flops | bytes accessed | tf_op | source)
XLA Modules:
  0.0 136.6 jit_solution(3812157718522566233)
XLA Ops:
  0.6 0.0 copy-start
  0.6 3.8 %pack.1 = bf16[16,128,768]{2,1,0:T(8,128)(2,1)} custom-call(bf16[1,128,4096]{2,1,0:T(8,128)(2,1)} %q_ref.1, bf16[1,128,4096]{2,1,0:T(8,128)(2,1)} %g_ref.1, bf16[1,128,1024]{2,1,0:T(8,128)(2,1)} %k_ref.1, bf16[1,128,1024]{2,1,0:T(8,128)(2,1)} %v_ref.1), custom_call_target="tpu_custom_call" | custom-call | tf_op jit(solution)/shard_map/pack/pallas_call | solution.py:281
  4.5 7.6 %all-to-all-start = ((bf16[16,128,768]{2,1,0:T(8,128)(2,1)}), bf16[16,128,768]{2,1,0:T(8,128)(2,1)}, u32[]{:S(2)}, u32[]{:S(2)}) async-start(bf16[16,128,768]{2,1,0:T(8,128)(2,1)} %pack.1), calls=%async_computation | async-start | bytes 6291456 | tf_op jit(solution)/shard_map/all_to_all | solution.py:429
  12.2 0.0 copy-done
  12.3 0.1 iota_compare_fusion.3
  12.3 0.2 fusion.8
  12.6 0.1 fusion.2
  12.7 0.1 copy.48
  12.8 0.1 copy.43
  12.9 0.1 copy.44
  13.1 0.1 select_reduce_fusion.1
  13.2 0.1 convert_reduce_fusion
  13.3 0.6 multiply_reduce_fusion
  13.9 0.1 add_select_fusion
  14.0 0.2 select_reduce_fusion.half_ref
  14.3 35.6 %all-to-all-done.qd_ref.own_ref = bf16[16,128,768]{2,1,0:T(8,128)(2,1)} async-done(((bf16[16,128,768]{2,1,0:T(8,128)(2,1)}), bf16[16,128,768]{2,1,0:T(8,128)(2,1)}, u32[]{:S(2)}, u32[]{:S(2)}) %all-to-all-start) | async-done | bytes 3145760 | tf_op jit(solution)/shard_map/all_to_all | solution.py:429
  49.9 1.3 slice.12
  51.2 8.2 %collective-permute-start = (bf16[16,128,256]{2,1,0:T(8,128)(2,1)S(1)}, bf16[16,128,256]{2,1,0:T(8,128)(2,1)S(1)}, u32[]{:S(2)}, u32[]{:S(2)}) collective-permute-start(bf16[16,128,256]{2,1,0:T(8,128)(2,1)S(1)} %slice.12), channel_id=1, source_target_pairs={{0,1},{1,0},{2,3},{3,2},{4,5},{5,4},{6,7},{7,6},{8,9},{9,8},{10,11... | collective-permute-start | bytes 3145736 | tf_op jit(solution)/shard_map/ppermute | solution.py:435
  59.5 2.3 %collective-permute-done.mate_ref = bf16[16,128,256]{2,1,0:T(8,128)(2,1)S(1)} collective-permute-done((bf16[16,128,256]{2,1,0:T(8,128)(2,1)S(1)}, bf16[16,128,256]{2,1,0:T(8,128)(2,1)S(1)}, u32[]{:S(2)}, u32[]{:S(2)}) %collective-permute-start) | collective-permute-done | bytes 1048608 | tf_op jit(solution)/shard_map/ppermute | solution.py:435
  61.7 16.2 %block_attention.1 = (bf16[16,128,512]{2,1,0:T(8,128)(2,1)}, bf16[16,128,256]{2,1,0:T(8,128)(2,1)S(1)}, f32[8,128]{1,0:T(8,128)S(1)}) custom-call(s32[4,256]{1,0:T(4,128)S(1)} %select_reduce_fusion.half_ref, s32[4,128]{1,0:T(4,128)S(1)} %broadcast_minimum_fusion.lane_ref, s32[4,1]{1,0:T(4,128)S(1)} %add_select_fusion.2.groups_ref, ...), custom_call_target="tpu_custom_call" | custom-call | flops 40000000000 | bytes 9000000 | tf_op jit(solution)/shard_map/block_attention/pallas_call | solution.py:204
  77.9 2.3 %collective-permute-start.1 = (bf16[16,128,256]{2,1,0:T(8,128)(2,1)S(1)}, bf16[16,128,256]{2,1,0:T(8,128)(2,1)S(1)}, u32[]{:S(2)}, u32[]{:S(2)}) collective-permute-start(bf16[16,128,256]{2,1,0:T(8,128)(2,1)S(1)} %get-tuple-element.23), channel_id=1, source_target_pairs={{0,1},{1,0},{2,3},{3,2},{4,5},{5,4},{6,7},{7,6},{8,9},{9,8},{10,11... | collective-permute-start | bytes 3145736 | tf_op jit(solution)/shard_map/ppermute | solution.py:438
  80.2 2.3 %collective-permute-done.1.got_ref = bf16[16,128,256]{2,1,0:T(8,128)(2,1)S(1)} collective-permute-done((bf16[16,128,256]{2,1,0:T(8,128)(2,1)S(1)}, bf16[16,128,256]{2,1,0:T(8,128)(2,1)S(1)}, u32[]{:S(2)}, u32[]{:S(2)}) %collective-permute-start.1) | collective-permute-done | bytes 1048608 | tf_op jit(solution)/shard_map/ppermute | solution.py:438
  82.5 0.0 copy-start.1
  82.5 1.0 copy-done.1
  83.4 2.4 %merge.1 = bf16[16,128,512]{2,1,0:T(8,128)(2,1)} custom-call(bf16[16,128,512]{2,1,0:T(8,128)(2,1)} %get-tuple-element.22.send_ref, bf16[16,128,256]{2,1,0:T(8,128)(2,1)} %copy-done.1), custom_call_target="tpu_custom_call", output_to_operand_aliasing={{}: (0, {})} | custom-call | tf_op jit(solution)/shard_map/merge/pallas_call | solution.py:326
  85.8 5.3 %all-to-all-start.1 = ((bf16[16,128,512]{2,1,0:T(8,128)(2,1)}), bf16[16,128,512]{2,1,0:T(8,128)(2,1)S(1)}, u32[]{:S(2)}, u32[]{:S(2)}) async-start(bf16[16,128,512]{2,1,0:T(8,128)(2,1)} %merge.1), calls=%async_computation.1 | async-start | bytes 4194304 | tf_op jit(solution)/shard_map/all_to_all | solution.py:429
  91.2 41.0 %all-gather.1 = f32[32,2,128]{2,1,0:T(2,128)S(1)} all-gather(f32[1,2,128]{2,1,0:T(2,128)S(1)} %bitcast.20), channel_id=2, replica_groups={{0,1,32,33,64,65,96,97,128,129,160,161,192,193,224,225,256,257,288,289,..., dimensions={0}, use_global_device_ids=true | all-gather | bytes 33792 | tf_op jit(solution)/shard_map/all_gather | solution.py:441
  132.1 0.1 reduce_sum.69
  132.3 0.6 fusion.13
  134.2 0.0 all-to-all-done.1.back_ref
  134.2 1.3 unpack.1
  (18 shorter events, 0.2 us)
Async XLA Ops:
  0.6 11.6 %copy-start = (s32[32,32,32]{2,1,0:T(8,128)S(1)}, s32[32,32,32]{2,1,0:T(8,128)}, u32[]{:S(2)}) copy-start(s32[32,32,32]{2,1,0:T(8,128)} %param.9) | copy-start | bytes 393220
  4.5 45.4 %all-to-all-start = ((bf16[16,128,768]{2,1,0:T(8,128)(2,1)}), bf16[16,128,768]{2,1,0:T(8,128)(2,1)}, u32[]{:S(2)}, u32[]{:S(2)}) async-start(bf16[16,128,768]{2,1,0:T(8,128)(2,1)} %pack.1), calls=%async_computation | async-start | bytes 6291456 | tf_op jit(solution)/shard_map/all_to_all | solution.py:429
  51.2 10.5 %collective-permute-start = (bf16[16,128,256]{2,1,0:T(8,128)(2,1)S(1)}, bf16[16,128,256]{2,1,0:T(8,128)(2,1)S(1)}, u32[]{:S(2)}, u32[]{:S(2)}) collective-permute-start(bf16[16,128,256]{2,1,0:T(8,128)(2,1)S(1)} %slice.12), channel_id=1, source_target_pairs={{0,1},{1,0},{2,3},{3,2},{4,5},{5,4},{6,7},{7,6},{8,9},{9,8},{10,11... | collective-permute-start | bytes 3145736 | tf_op jit(solution)/shard_map/ppermute | solution.py:435
  77.9 4.6 %collective-permute-start.1 = (bf16[16,128,256]{2,1,0:T(8,128)(2,1)S(1)}, bf16[16,128,256]{2,1,0:T(8,128)(2,1)S(1)}, u32[]{:S(2)}, u32[]{:S(2)}) collective-permute-start(bf16[16,128,256]{2,1,0:T(8,128)(2,1)S(1)} %get-tuple-element.23), channel_id=1, source_target_pairs={{0,1},{1,0},{2,3},{3,2},{4,5},{5,4},{6,7},{7,6},{8,9},{9,8},{10,11... | collective-permute-start | bytes 3145736 | tf_op jit(solution)/shard_map/ppermute | solution.py:438
  82.5 1.0 copy-start.1
  85.8 48.3 %all-to-all-start.1 = ((bf16[16,128,512]{2,1,0:T(8,128)(2,1)}), bf16[16,128,512]{2,1,0:T(8,128)(2,1)S(1)}, u32[]{:S(2)}, u32[]{:S(2)}) async-start(bf16[16,128,512]{2,1,0:T(8,128)(2,1)} %merge.1), calls=%async_computation.1 | async-start | bytes 4194304 | tf_op jit(solution)/shard_map/all_to_all | solution.py:429

commit v7 on v6

--- a/solution.py
+++ b/solution.py
@@ -13,7 +13,7 @@
 BLK = 128
 PAIR = 2
 ROWS = 4
-GROUP = 8
+GROUPS = (8, 4, 2)
 Z_ROWS = 8
 
 ZLOSS = 0.05
@@ -110,31 +110,39 @@
         h1, h2 = half_ref[step, 2 * i], half_ref[step, 2 * i + 1]
         return lane_ref[step, i], h1, h2, jnp.maximum(h1 - 1, 0), jnp.maximum(h2 - 1, 0)
 
-    groups = groups_ref[step, 0]
-
-    @pl.loop(0, groups)
-    def _(g):
-        for k in range(GROUP):
-            i = g * GROUP + k
-            n, h1, h2, c1, c2 = entry(i)
-            b1 = jnp.where(h1 > 0, 0.0, NEG).astype(jnp.float32)
-            b2 = jnp.where(h2 > 0, 0.0, NEG).astype(jnp.float32)
-            key, value = pair(c1, c2)
-            sc = dot_nt(key, qg_s[n, :, :HD]) * (SCALE * LOG2E)
-            sc = jnp.concatenate([sc[:BLK] + b1, sc[BLK:] + b2], axis=0)
-            dp = dot_nt(value, qg_s[n, :, HD:])
-            m = jnp.max(sc, axis=0, keepdims=True)
-            e = jnp.exp2(sc - m)
-            e_s[i] = e
-            dp_s[i] = dp
-            m = wide(m)
-            m_s[i] = m
-            old = top_s[n]
-            new = jnp.maximum(old, m)
-            keep, take = jnp.exp2(old - new), jnp.exp2(m - new)
-            top_s[n] = new
-            sum_s[n] = sum_s[n] * keep + wide(jnp.sum(e, axis=0, keepdims=True)) * take
-            pull_s[n] = pull_s[n] * keep + wide(jnp.sum(e * dp, axis=0, keepdims=True)) * take
+    def over_items(one):
+        done = 0
+        for n, size in enumerate(GROUPS):
+            count = groups_ref[step, n]
+
+            @pl.loop(0, count)
+            def _(g, done=done, size=size):
+                for k in range(size):
+                    one(done + g * size + k)
+
+            done = done + count * size
+
+    @over_items
+    def _(i):
+        n, h1, h2, c1, c2 = entry(i)
+        b1 = jnp.where(h1 > 0, 0.0, NEG).astype(jnp.float32)
+        b2 = jnp.where(h2 > 0, 0.0, NEG).astype(jnp.float32)
+        key, value = pair(c1, c2)
+        sc = dot_nt(key, qg_s[n, :, :HD]) * (SCALE * LOG2E)
+        sc = jnp.concatenate([sc[:BLK] + b1, sc[BLK:] + b2], axis=0)
+        dp = dot_nt(value, qg_s[n, :, HD:])
+        m = jnp.max(sc, axis=0, keepdims=True)
+        e = jnp.exp2(sc - m)
+        e_s[i] = e
+        dp_s[i] = dp
+        m = wide(m)
+        m_s[i] = m
+        old = top_s[n]
+        new = jnp.maximum(old, m)
+        keep, take = jnp.exp2(old - new), jnp.exp2(m - new)
+        top_s[n] = new
+        sum_s[n] = sum_s[n] * keep + wide(jnp.sum(e, axis=0, keepdims=True)) * take
+        pull_s[n] = pull_s[n] * keep + wide(jnp.sum(e * dp, axis=0, keepdims=True)) * take
 
     for n, (s, j) in enumerate(lanes):
         l = sum_s[n]
@@ -167,19 +175,17 @@
     dk_s[0] += sum(dk0[1:], dk0[0])
     dv_s[0] += sum(dv0[1:], dv0[0])
 
-    @pl.loop(0, groups)
-    def _(g):
-        for k in range(GROUP):
-            i = g * GROUP + k
-            n, _, _, c1, c2 = entry(i)
-            p_low, d_low = weights(i, n)
-            dk = dot(d_low, qg_s[n, :, :HD])
-            dv = dot(p_low, qg_s[n, :, HD:])
-            dqt_s[n] += dot(jnp.concatenate([kt_s[c1], kt_s[c2]], axis=1), d_low)
-            dk_s[c1] += dk[:BLK]
-            dv_s[c1] += dv[:BLK]
-            dk_s[c2] += dk[BLK:]
-            dv_s[c2] += dv[BLK:]
+    @over_items
+    def _(i):
+        n, _, _, c1, c2 = entry(i)
+        p_low, d_low = weights(i, n)
+        dk = dot(d_low, qg_s[n, :, :HD])
+        dv = dot(p_low, qg_s[n, :, HD:])
+        dqt_s[n] += dot(jnp.concatenate([kt_s[c1], kt_s[c2]], axis=1), d_low)
+        dk_s[c1] += dk[:BLK]
+        dv_s[c1] += dv[:BLK]
+        dk_s[c2] += dk[BLK:]
+        dv_s[c2] += dv[BLK:]
 
     for n, (s, j) in enumerate(lanes):
         send_ref[ROWS * step + s, :, j * HD : (j + 1) * HD] = (dqt_s[n] * SCALE).T.astype(jnp.bfloat16)
@@ -410,7 +416,13 @@
     item = jnp.arange(lanes * half, dtype=jnp.int32)
     ends = start + pairs
     lane = jnp.minimum(jnp.sum((ends[:, None, :] <= item[None, :, None]).astype(jnp.int32), axis=2), lanes - 1)
-    groups = (jnp.sum(pairs, axis=1, keepdims=True) + GROUP - 1) // GROUP
+    left = jnp.sum(pairs, axis=1)
+    groups = []
+    for size, spare in zip(GROUPS, GROUPS[1:] + (1,)):
+        count = (left + size - 1 - spare * (spare > 1)) // size
+        groups.append(jnp.maximum(count, 0))
+        left = jnp.maximum(left - count * size, 0)
+    groups = jnp.stack(groups, axis=1)
     edge = jnp.full((1, 3), core, jnp.int32)
     return halves, lane, groups, edge
 

time: 137 us -> 138 us (level)
  no operation moved by 1% of the time
where the time goes in v7:
time: 138 us; the launch traced here: 137 us
  blocking collectives  40.6 us (29%)
  waiting for transfers between devices  40.1 us (29%)
  starting transfers between devices  24.7 us (18%)
  Pallas kernels  23.6 us (17%)
  between operations  3.3 us (2%)
  local copies, waits for them, and re-layouts  3.16 us (2%)
  other arithmetic  1.95 us (1%)
    all_gather x1, blocking collectives, body(): z_all = lax.all_gather(z, ('dp', 'ctx'), axis_index_groups=wide)  40.6 us
    all_to_all x2, waiting for transfers between devices, exchange(): return lax.all_to_all(a, 'ctx', 0, 0, axis_index_groups=same, tiled=True)  35.6 us
    pallas_call x1, Pallas kernels, attention(): pl.pallas_call(attention_body, out_shape=(jax.ShapeDtypeStruct((half, BLK...  16.1 us
    all_to_all x2, starting transfers between devices, exchange(): return lax.all_to_all(a, 'ctx', 0, 0, axis_index_groups=same, tiled=True)  14.2 us
    ppermute x1, starting transfers between devices, body(): mate = lax.ppermute(recv[:, :, 4 * HD:], 'ctx', mates)  8.24 us
    pallas_call x1, Pallas kernels, pack(): pl.pallas_call(pack_body, out_shape=jax.ShapeDtypeStruct(shape, queries.d...  3.82 us
  transfers between devices with their start and end apart: 4, of which 3 were waited for; matrix products, arithmetic and copies ran while one was open for 2% of the time, Pallas kernels for 0%

profile of v7, /device:TPU:1, one launch (start us, length us, event | category | flops | bytes accessed | tf_op | source)
XLA Modules:
  0.0 137.5 jit_solution(2893078775624198174)
XLA Ops:
  0.6 0.0 copy-start
  0.6 3.8 %pack.1 = bf16[16,128,768]{2,1,0:T(8,128)(2,1)} custom-call(bf16[1,128,4096]{2,1,0:T(8,128)(2,1)} %q_ref.1, bf16[1,128,4096]{2,1,0:T(8,128)(2,1)} %g_ref.1, bf16[1,128,1024]{2,1,0:T(8,128)(2,1)} %k_ref.1, bf16[1,128,1024]{2,1,0:T(8,128)(2,1)} %v_ref.1), custom_call_target="tpu_custom_call" | custom-call | tf_op jit(solution)/shard_map/pack/pallas_call | solution.py:287
  4.5 7.6 %all-to-all-start = ((bf16[16,128,768]{2,1,0:T(8,128)(2,1)}), bf16[16,128,768]{2,1,0:T(8,128)(2,1)}, u32[]{:S(2)}, u32[]{:S(2)}) async-start(bf16[16,128,768]{2,1,0:T(8,128)(2,1)} %pack.1), calls=%async_computation | async-start | bytes 6291456 | tf_op jit(solution)/shard_map/all_to_all | solution.py:441
  12.2 0.0 copy-done
  12.3 0.1 iota_compare_fusion.3
  12.3 0.2 fusion.13
  12.6 0.1 fusion.2
  12.7 0.1 copy.40
  12.8 0.1 copy.35
  12.9 0.1 copy.36
  13.1 0.1 pad_add_fusion.groups_ref
  13.2 0.1 select_reduce_fusion.1
  13.3 0.1 convert_reduce_fusion
  13.4 0.6 multiply_reduce_fusion
  14.0 0.1 add_select_fusion
  14.1 0.2 select_reduce_fusion.half_ref
  14.4 35.6 %all-to-all-done.qd_ref.own_ref = bf16[16,128,768]{2,1,0:T(8,128)(2,1)} async-done(((bf16[16,128,768]{2,1,0:T(8,128)(2,1)}), bf16[16,128,768]{2,1,0:T(8,128)(2,1)}, u32[]{:S(2)}, u32[]{:S(2)}) %all-to-all-start) | async-done | bytes 3145760 | tf_op jit(solution)/shard_map/all_to_all | solution.py:441
  49.9 1.3 slice.12
  51.2 8.2 %collective-permute-start = (bf16[16,128,256]{2,1,0:T(8,128)(2,1)S(1)}, bf16[16,128,256]{2,1,0:T(8,128)(2,1)S(1)}, u32[]{:S(2)}, u32[]{:S(2)}) collective-permute-start(bf16[16,128,256]{2,1,0:T(8,128)(2,1)S(1)} %slice.12), channel_id=1, source_target_pairs={{0,1},{1,0},{2,3},{3,2},{4,5},{5,4},{6,7},{7,6},{8,9},{9,8},{10,11... | collective-permute-start | bytes 3145736 | tf_op jit(solution)/shard_map/ppermute | solution.py:447
  59.5 2.3 %collective-permute-done.mate_ref = bf16[16,128,256]{2,1,0:T(8,128)(2,1)S(1)} collective-permute-done((bf16[16,128,256]{2,1,0:T(8,128)(2,1)S(1)}, bf16[16,128,256]{2,1,0:T(8,128)(2,1)S(1)}, u32[]{:S(2)}, u32[]{:S(2)}) %collective-permute-start) | collective-permute-done | bytes 1048608 | tf_op jit(solution)/shard_map/ppermute | solution.py:447
  61.7 16.1 %block_attention.1 = (bf16[16,128,512]{2,1,0:T(8,128)(2,1)}, bf16[16,128,256]{2,1,0:T(8,128)(2,1)S(1)}, f32[8,128]{1,0:T(8,128)S(1)}) custom-call(s32[4,256]{1,0:T(4,128)S(1)} %select_reduce_fusion.half_ref, s32[4,128]{1,0:T(4,128)S(1)} %broadcast_minimum_fusion.lane_ref, s32[4,3]{1,0:T(4,128)S(1)} %pad_add_fusion.groups_ref, ...), custom_call_target="tpu_custom_call" | custom-call | flops 40000000000 | bytes 9000000 | tf_op jit(solution)/shard_map/block_attention/pallas_call | solution.py:210
  77.9 2.3 %collective-permute-start.1 = (bf16[16,128,256]{2,1,0:T(8,128)(2,1)S(1)}, bf16[16,128,256]{2,1,0:T(8,128)(2,1)S(1)}, u32[]{:S(2)}, u32[]{:S(2)}) collective-permute-start(bf16[16,128,256]{2,1,0:T(8,128)(2,1)S(1)} %get-tuple-element.23), channel_id=1, source_target_pairs={{0,1},{1,0},{2,3},{3,2},{4,5},{5,4},{6,7},{7,6},{8,9},{9,8},{10,11... | collective-permute-start | bytes 3145736 | tf_op jit(solution)/shard_map/ppermute | solution.py:450
  80.2 2.3 %collective-permute-done.1.got_ref = bf16[16,128,256]{2,1,0:T(8,128)(2,1)S(1)} collective-permute-done((bf16[16,128,256]{2,1,0:T(8,128)(2,1)S(1)}, bf16[16,128,256]{2,1,0:T(8,128)(2,1)S(1)}, u32[]{:S(2)}, u32[]{:S(2)}) %collective-permute-start.1) | collective-permute-done | bytes 1048608 | tf_op jit(solution)/shard_map/ppermute | solution.py:450
  82.4 0.0 copy-start.1
  82.4 1.0 copy-done.1
  83.4 2.4 %merge.1 = bf16[16,128,512]{2,1,0:T(8,128)(2,1)} custom-call(bf16[16,128,512]{2,1,0:T(8,128)(2,1)} %get-tuple-element.22.send_ref, bf16[16,128,256]{2,1,0:T(8,128)(2,1)} %copy-done.1), custom_call_target="tpu_custom_call", output_to_operand_aliasing={{}: (0, {})} | custom-call | tf_op jit(solution)/shard_map/merge/pallas_call | solution.py:332
  85.8 6.6 %all-to-all-start.1 = ((bf16[16,128,512]{2,1,0:T(8,128)(2,1)}), bf16[16,128,512]{2,1,0:T(8,128)(2,1)S(1)}, u32[]{:S(2)}, u32[]{:S(2)}) async-start(bf16[16,128,512]{2,1,0:T(8,128)(2,1)} %merge.1), calls=%async_computation.1 | async-start | bytes 4194304 | tf_op jit(solution)/shard_map/all_to_all | solution.py:441
  92.4 40.6 %all-gather.1 = f32[32,2,128]{2,1,0:T(2,128)S(1)} all-gather(f32[1,2,128]{2,1,0:T(2,128)S(1)} %bitcast.19), channel_id=2, replica_groups={{0,1,32,33,64,65,96,97,128,129,160,161,192,193,224,225,256,257,288,289,..., dimensions={0}, use_global_device_ids=true | all-gather | bytes 33792 | tf_op jit(solution)/shard_map/all_gather | solution.py:453
  133.0 0.1 reduce_sum.72
  133.1 0.6 fusion.18
  135.0 0.0 all-to-all-done.1.back_ref
  135.0 1.3 unpack.1
  (17 shorter events, 0.2 us)
Async XLA Ops:
  0.6 11.5 %copy-start = (s32[32,32,32]{2,1,0:T(8,128)S(1)}, s32[32,32,32]{2,1,0:T(8,128)}, u32[]{:S(2)}) copy-start(s32[32,32,32]{2,1,0:T(8,128)} %param.9) | copy-start | bytes 393220
  4.5 45.4 %all-to-all-start = ((bf16[16,128,768]{2,1,0:T(8,128)(2,1)}), bf16[16,128,768]{2,1,0:T(8,128)(2,1)}, u32[]{:S(2)}, u32[]{:S(2)}) async-start(bf16[16,128,768]{2,1,0:T(8,128)(2,1)} %pack.1), calls=%async_computation | async-start | bytes 6291456 | tf_op jit(solution)/shard_map/all_to_all | solution.py:441
  51.2 10.5 %collective-permute-start = (bf16[16,128,256]{2,1,0:T(8,128)(2,1)S(1)}, bf16[16,128,256]{2,1,0:T(8,128)(2,1)S(1)}, u32[]{:S(2)}, u32[]{:S(2)}) collective-permute-start(bf16[16,128,256]{2,1,0:T(8,128)(2,1)S(1)} %slice.12), channel_id=1, source_target_pairs={{0,1},{1,0},{2,3},{3,2},{4,5},{5,4},{6,7},{7,6},{8,9},{9,8},{10,11... | collective-permute-start | bytes 3145736 | tf_op jit(solution)/shard_map/ppermute | solution.py:447
  77.9 4.6 %collective-permute-start.1 = (bf16[16,128,256]{2,1,0:T(8,128)(2,1)S(1)}, bf16[16,128,256]{2,1,0:T(8,128)(2,1)S(1)}, u32[]{:S(2)}, u32[]{:S(2)}) collective-permute-start(bf16[16,128,256]{2,1,0:T(8,128)(2,1)S(1)} %get-tuple-element.23), channel_id=1, source_target_pairs={{0,1},{1,0},{2,3},{3,2},{4,5},{5,4},{6,7},{7,6},{8,9},{9,8},{10,11... | collective-permute-start | bytes 3145736 | tf_op jit(solution)/shard_map/ppermute | solution.py:450
  82.4 1.0 copy-start.1
  85.8 49.2 %all-to-all-start.1 = ((bf16[16,128,512]{2,1,0:T(8,128)(2,1)}), bf16[16,128,512]{2,1,0:T(8,128)(2,1)S(1)}, u32[]{:S(2)}, u32[]{:S(2)}) async-start(bf16[16,128,512]{2,1,0:T(8,128)(2,1)} %merge.1), calls=%async_computation.1 | async-start | bytes 4194304 | tf_op jit(solution)/shard_map/all_to_all | solution.py:441

commit v8 on v7

--- a/solution.py
+++ b/solution.py
@@ -298,7 +298,7 @@
     )(queries, out_grad, keys, values)
 
 
-def merge_body(send_ref, got_ref, out_ref, own_s, got_s, in_sem, got_sem, out_sem):
+def merge_body(send_ref, got_ref, out_ref, own_s, in_sem, out_sem):
     parts = in_sem.shape[0]
     part = own_s.shape[0] // parts
 
@@ -313,15 +313,12 @@
         pltpu.make_async_copy(own_s.at[cut(n)], out_ref.at[cut(n), :, pl.ds(2 * HD, 2 * HD)], out_sem.at[n])
         for n in range(parts)
     ]
-    gets = [pltpu.make_async_copy(got_ref.at[cut(n)], got_s.at[cut(n)], got_sem.at[n]) for n in range(parts)]
     for n in range(parts):
         loads[n].start()
-        gets[n].start()
     for n in range(parts):
         loads[n].wait()
-        gets[n].wait()
         rows = slice(n * part, (n + 1) * part)
-        both = own_s[rows].astype(jnp.float32) + got_s[rows].astype(jnp.float32)
+        both = own_s[rows].astype(jnp.float32) + got_ref[rows].astype(jnp.float32)
         own_s[rows] = both.astype(own_s.dtype)
         stores[n].start()
     for copy in stores:
@@ -332,17 +329,15 @@
     return pl.pallas_call(
         merge_body,
         out_shape=jax.ShapeDtypeStruct(send.shape, send.dtype),
-        in_specs=[pl.BlockSpec(memory_space=pl.ANY)] * 2,
+        in_specs=[pl.BlockSpec(memory_space=pl.ANY), pl.BlockSpec(memory_space=pltpu.VMEM)],
         out_specs=pl.BlockSpec(memory_space=pl.ANY),
         scratch_shapes=[
             pltpu.VMEM(got.shape, got.dtype),
-            pltpu.VMEM(got.shape, got.dtype),
-            pltpu.SemaphoreType.DMA((4,)),
             pltpu.SemaphoreType.DMA((4,)),
             pltpu.SemaphoreType.DMA((4,)),
         ],
         input_output_aliases={0: 0},
-        compiler_params=pltpu.CompilerParams(vmem_limit_bytes=60 << 20),
+        compiler_params=pltpu.CompilerParams(vmem_limit_bytes=52 << 20),
         name="merge",
     )(send, got)
 

time: 138 us -> 135 us (0.978)
  no operation moved by 1% of the time
where the time goes in v8:
time: 135 us
  waiting for transfers between devices  40.1 us (30%)
  blocking collectives  40 us (30%)
  Pallas kernels  23.7 us (18%)
  starting transfers between devices  23.4 us (17%)
  between operations  3.3 us (2%)
  local copies, waits for them, and re-layouts  2.21 us (2%)
  other arithmetic  1.95 us (1%)
    all_gather x1, blocking collectives, body(): z_all = lax.all_gather(z, ('dp', 'ctx'), axis_index_groups=wide)  40 us
    all_to_all x2, waiting for transfers between devices, exchange(): return lax.all_to_all(a, 'ctx', 0, 0, axis_index_groups=same, tiled=True)  35.6 us
    pallas_call x1, Pallas kernels, attention(): pl.pallas_call(attention_body, out_shape=(jax.ShapeDtypeStruct((half, BLK...  16.5 us
    all_to_all x2, starting transfers between devices, exchange(): return lax.all_to_all(a, 'ctx', 0, 0, axis_index_groups=same, tiled=True)  12.9 us
    ppermute x1, starting transfers between devices, body(): mate = lax.ppermute(recv[:, :, 4 * HD:], 'ctx', mates)  8.24 us
    pallas_call x1, Pallas kernels, pack(): pl.pallas_call(pack_body, out_shape=jax.ShapeDtypeStruct(shape, queries.d...  3.82 us
  transfers between devices with their start and end apart: 4, of which 3 were waited for; matrix products, arithmetic and copies ran while one was open for 2% of the time, Pallas kernels for 0%

profile of v8, /device:TPU:1, one launch (start us, length us, event | category | flops | bytes accessed | tf_op | source)
XLA Modules:
  0.0 134.7 jit_solution(1353360946838796851)
XLA Ops:
  0.6 0.0 copy-start
  0.6 3.8 %pack.1 = bf16[16,128,768]{2,1,0:T(8,128)(2,1)} custom-call(bf16[1,128,4096]{2,1,0:T(8,128)(2,1)} %q_ref.1, bf16[1,128,4096]{2,1,0:T(8,128)(2,1)} %g_ref.1, bf16[1,128,1024]{2,1,0:T(8,128)(2,1)} %k_ref.1, bf16[1,128,1024]{2,1,0:T(8,128)(2,1)} %v_ref.1), custom_call_target="tpu_custom_call" | custom-call | tf_op jit(solution)/shard_map/pack/pallas_call | solution.py:287
  4.5 7.6 %all-to-all-start = ((bf16[16,128,768]{2,1,0:T(8,128)(2,1)}), bf16[16,128,768]{2,1,0:T(8,128)(2,1)}, u32[]{:S(2)}, u32[]{:S(2)}) async-start(bf16[16,128,768]{2,1,0:T(8,128)(2,1)} %pack.1), calls=%async_computation | async-start | bytes 6291456 | tf_op jit(solution)/shard_map/all_to_all | solution.py:436
  12.2 0.0 copy-done
  12.3 0.1 iota_compare_fusion.3
  12.3 0.2 fusion.13
  12.6 0.1 fusion.2
  12.7 0.1 copy.40
  12.8 0.1 copy.35
  12.9 0.1 copy.36
  13.1 0.1 pad_add_fusion.groups_ref
  13.2 0.1 select_reduce_fusion.1
  13.3 0.1 convert_reduce_fusion
  13.4 0.6 multiply_reduce_fusion
  14.0 0.1 add_select_fusion
  14.1 0.2 select_reduce_fusion.half_ref
  14.4 35.6 %all-to-all-done.qd_ref.own_ref = bf16[16,128,768]{2,1,0:T(8,128)(2,1)} async-done(((bf16[16,128,768]{2,1,0:T(8,128)(2,1)}), bf16[16,128,768]{2,1,0:T(8,128)(2,1)}, u32[]{:S(2)}, u32[]{:S(2)}) %all-to-all-start) | async-done | bytes 3145760 | tf_op jit(solution)/shard_map/all_to_all | solution.py:436
  49.9 1.3 slice.12
  51.2 8.2 %collective-permute-start = (bf16[16,128,256]{2,1,0:T(8,128)(2,1)S(1)}, bf16[16,128,256]{2,1,0:T(8,128)(2,1)S(1)}, u32[]{:S(2)}, u32[]{:S(2)}) collective-permute-start(bf16[16,128,256]{2,1,0:T(8,128)(2,1)S(1)} %slice.12), channel_id=1, source_target_pairs={{0,1},{1,0},{2,3},{3,2},{4,5},{5,4},{6,7},{7,6},{8,9},{9,8},{10,11... | collective-permute-start | bytes 3145736 | tf_op jit(solution)/shard_map/ppermute | solution.py:442
  59.5 2.3 %collective-permute-done.mate_ref = bf16[16,128,256]{2,1,0:T(8,128)(2,1)S(1)} collective-permute-done((bf16[16,128,256]{2,1,0:T(8,128)(2,1)S(1)}, bf16[16,128,256]{2,1,0:T(8,128)(2,1)S(1)}, u32[]{:S(2)}, u32[]{:S(2)}) %collective-permute-start) | collective-permute-done | bytes 1048608 | tf_op jit(solution)/shard_map/ppermute | solution.py:442
  61.7 16.5 %block_attention.1 = (bf16[16,128,512]{2,1,0:T(8,128)(2,1)}, bf16[16,128,256]{2,1,0:T(8,128)(2,1)S(1)}, f32[8,128]{1,0:T(8,128)S(1)}) custom-call(s32[4,256]{1,0:T(4,128)S(1)} %select_reduce_fusion.half_ref, s32[4,128]{1,0:T(4,128)S(1)} %broadcast_minimum_fusion.lane_ref, s32[4,3]{1,0:T(4,128)S(1)} %pad_add_fusion.groups_ref, ...), custom_call_target="tpu_custom_call" | custom-call | flops 40000000000 | bytes 9000000 | tf_op jit(solution)/shard_map/block_attention/pallas_call | solution.py:210
  78.3 2.3 %collective-permute-start.1 = (bf16[16,128,256]{2,1,0:T(8,128)(2,1)S(1)}, bf16[16,128,256]{2,1,0:T(8,128)(2,1)S(1)}, u32[]{:S(2)}, u32[]{:S(2)}) collective-permute-start(bf16[16,128,256]{2,1,0:T(8,128)(2,1)S(1)} %get-tuple-element.23), channel_id=1, source_target_pairs={{0,1},{1,0},{2,3},{3,2},{4,5},{5,4},{6,7},{7,6},{8,9},{9,8},{10,11... | collective-permute-start | bytes 3145736 | tf_op jit(solution)/shard_map/ppermute | solution.py:445
  80.6 2.3 %collective-permute-done.1.got_ref = bf16[16,128,256]{2,1,0:T(8,128)(2,1)S(1)} collective-permute-done((bf16[16,128,256]{2,1,0:T(8,128)(2,1)S(1)}, bf16[16,128,256]{2,1,0:T(8,128)(2,1)S(1)}, u32[]{:S(2)}, u32[]{:S(2)}) %collective-permute-start.1) | collective-permute-done | bytes 1048608 | tf_op jit(solution)/shard_map/ppermute | solution.py:445
  82.8 2.1 %merge.1 = bf16[16,128,512]{2,1,0:T(8,128)(2,1)} custom-call(bf16[16,128,512]{2,1,0:T(8,128)(2,1)} %get-tuple-element.22.send_ref, bf16[16,128,256]{2,1,0:T(8,128)(2,1)S(1)} %collective-permute-done.1.got_ref), custom_call_target="tpu_custom_call", output_to_operand_aliasing={{}: (0, {})} | custom-call | tf_op jit(solution)/shard_map/merge/pallas_call | solution.py:329
  84.9 5.3 %all-to-all-start.1 = ((bf16[16,128,512]{2,1,0:T(8,128)(2,1)}), bf16[16,128,512]{2,1,0:T(8,128)(2,1)S(1)}, u32[]{:S(2)}, u32[]{:S(2)}) async-start(bf16[16,128,512]{2,1,0:T(8,128)(2,1)} %merge.1), calls=%async_computation.1 | async-start | bytes 4194304 | tf_op jit(solution)/shard_map/all_to_all | solution.py:436
  90.2 40.0 %all-gather.1 = f32[32,2,128]{2,1,0:T(2,128)S(1)} all-gather(f32[1,2,128]{2,1,0:T(2,128)S(1)} %bitcast.19), channel_id=2, replica_groups={{0,1,32,33,64,65,96,97,128,129,160,161,192,193,224,225,256,257,288,289,..., dimensions={0}, use_global_device_ids=true | all-gather | bytes 33792 | tf_op jit(solution)/shard_map/all_gather | solution.py:448
  130.2 0.1 reduce_sum.72
  130.3 0.6 fusion.18
  132.2 0.0 all-to-all-done.1.back_ref
  132.2 1.3 unpack.1
  (17 shorter events, 0.2 us)
Async XLA Ops:
  0.6 11.5 %copy-start = (s32[32,32,32]{2,1,0:T(8,128)S(1)}, s32[32,32,32]{2,1,0:T(8,128)}, u32[]{:S(2)}) copy-start(s32[32,32,32]{2,1,0:T(8,128)} %param.9) | copy-start | bytes 393220
  4.5 45.4 %all-to-all-start = ((bf16[16,128,768]{2,1,0:T(8,128)(2,1)}), bf16[16,128,768]{2,1,0:T(8,128)(2,1)}, u32[]{:S(2)}, u32[]{:S(2)}) async-start(bf16[16,128,768]{2,1,0:T(8,128)(2,1)} %pack.1), calls=%async_computation | async-start | bytes 6291456 | tf_op jit(solution)/shard_map/all_to_all | solution.py:436
  51.2 10.5 %collective-permute-start = (bf16[16,128,256]{2,1,0:T(8,128)(2,1)S(1)}, bf16[16,128,256]{2,1,0:T(8,128)(2,1)S(1)}, u32[]{:S(2)}, u32[]{:S(2)}) collective-permute-start(bf16[16,128,256]{2,1,0:T(8,128)(2,1)S(1)} %slice.12), channel_id=1, source_target_pairs={{0,1},{1,0},{2,3},{3,2},{4,5},{5,4},{6,7},{7,6},{8,9},{9,8},{10,11... | collective-permute-start | bytes 3145736 | tf_op jit(solution)/shard_map/ppermute | solution.py:442
  78.3 4.6 %collective-permute-start.1 = (bf16[16,128,256]{2,1,0:T(8,128)(2,1)S(1)}, bf16[16,128,256]{2,1,0:T(8,128)(2,1)S(1)}, u32[]{:S(2)}, u32[]{:S(2)}) collective-permute-start(bf16[16,128,256]{2,1,0:T(8,128)(2,1)S(1)} %get-tuple-element.23), channel_id=1, source_target_pairs={{0,1},{1,0},{2,3},{3,2},{4,5},{5,4},{6,7},{7,6},{8,9},{9,8},{10,11... | collective-permute-start | bytes 3145736 | tf_op jit(solution)/shard_map/ppermute | solution.py:445
  84.9 47.3 %all-to-all-start.1 = ((bf16[16,128,512]{2,1,0:T(8,128)(2,1)}), bf16[16,128,512]{2,1,0:T(8,128)(2,1)S(1)}, u32[]{:S(2)}, u32[]{:S(2)}) async-start(bf16[16,128,512]{2,1,0:T(8,128)(2,1)} %merge.1), calls=%async_computation.1 | async-start | bytes 4194304 | tf_op jit(solution)/shard_map/all_to_all | solution.py:436

commit v9 on v8

--- a/solution.py
+++ b/solution.py
@@ -13,7 +13,7 @@
 BLK = 128
 PAIR = 2
 ROWS = 4
-GROUPS = (8, 4, 2)
+GROUPS = (16, 8, 4)
 Z_ROWS = 8
 
 ZLOSS = 0.05

time: 135 us -> 137 us (1.015)
  blocking collectives: 40 us -> 42.8 us
  starting transfers between devices: 23.4 us -> 21.9 us
    all_gather x1, blocking collectives: 40 us -> 42.8 us  [body(): z_all = lax.all_gather(z, ('dp', 'ctx'), axis_index_groups=wide)]
    all_to_all x2, starting transfers between devices: 12.9 us -> 11.4 us  [exchange(): return lax.all_to_all(a, 'ctx', 0, 0, axis_index_groups=same, tiled=True)]
where the time goes in v9:
time: 137 us
  blocking collectives  42.8 us (31%)
  waiting for transfers between devices  40.1 us (29%)
  Pallas kernels  24.3 us (18%)
  starting transfers between devices  21.9 us (16%)
  between operations  3.3 us (2%)
  local copies, waits for them, and re-layouts  2.21 us (2%)
  other arithmetic  1.95 us (1%)
    all_gather x1, blocking collectives, body(): z_all = lax.all_gather(z, ('dp', 'ctx'), axis_index_groups=wide)  42.8 us
    all_to_all x2, waiting for transfers between devices, exchange(): return lax.all_to_all(a, 'ctx', 0, 0, axis_index_groups=same, tiled=True)  35.6 us
    pallas_call x1, Pallas kernels, attention(): pl.pallas_call(attention_body, out_shape=(jax.ShapeDtypeStruct((half, BLK...  17.2 us
    all_to_all x2, starting transfers between devices, exchange(): return lax.all_to_all(a, 'ctx', 0, 0, axis_index_groups=same, tiled=True)  11.4 us
    ppermute x1, starting transfers between devices, body(): mate = lax.ppermute(recv[:, :, 4 * HD:], 'ctx', mates)  8.24 us
    pallas_call x1, Pallas kernels, pack(): pl.pallas_call(pack_body, out_shape=jax.ShapeDtypeStruct(shape, queries.d...  3.82 us
  transfers between devices with their start and end apart: 4, of which 3 were waited for; matrix products, arithmetic and copies ran while one was open for 2% of the time, Pallas kernels for 0%

profile of v9, /device:TPU:1, one launch (start us, length us, event | category | flops | bytes accessed | tf_op | source)
XLA Modules:
  0.0 136.6 jit_solution(4241175987140115934)
XLA Ops:
  0.6 0.0 copy-start
  0.6 3.8 %pack.1 = bf16[16,128,768]{2,1,0:T(8,128)(2,1)} custom-call(bf16[1,128,4096]{2,1,0:T(8,128)(2,1)} %q_ref.1, bf16[1,128,4096]{2,1,0:T(8,128)(2,1)} %g_ref.1, bf16[1,128,1024]{2,1,0:T(8,128)(2,1)} %k_ref.1, bf16[1,128,1024]{2,1,0:T(8,128)(2,1)} %v_ref.1), custom_call_target="tpu_custom_call" | custom-call | tf_op jit(solution)/shard_map/pack/pallas_call | solution.py:287
  4.5 7.6 %all-to-all-start = ((bf16[16,128,768]{2,1,0:T(8,128)(2,1)}), bf16[16,128,768]{2,1,0:T(8,128)(2,1)}, u32[]{:S(2)}, u32[]{:S(2)}) async-start(bf16[16,128,768]{2,1,0:T(8,128)(2,1)} %pack.1), calls=%async_computation | async-start | bytes 6291456 | tf_op jit(solution)/shard_map/all_to_all | solution.py:436
  12.2 0.0 copy-done
  12.3 0.1 iota_compare_fusion.3
  12.3 0.2 fusion.13
  12.6 0.1 fusion.2
  12.7 0.1 copy.40
  12.8 0.1 copy.35
  12.9 0.1 copy.36
  13.1 0.1 pad_add_fusion.groups_ref
  13.2 0.1 select_reduce_fusion.1
  13.3 0.1 convert_reduce_fusion
  13.4 0.6 multiply_reduce_fusion
  14.0 0.1 add_select_fusion
  14.1 0.2 select_reduce_fusion.half_ref
  14.4 35.6 %all-to-all-done.qd_ref.own_ref = bf16[16,128,768]{2,1,0:T(8,128)(2,1)} async-done(((bf16[16,128,768]{2,1,0:T(8,128)(2,1)}), bf16[16,128,768]{2,1,0:T(8,128)(2,1)}, u32[]{:S(2)}, u32[]{:S(2)}) %all-to-all-start) | async-done | bytes 3145760 | tf_op jit(solution)/shard_map/all_to_all | solution.py:436
  49.9 1.3 slice.12
  51.2 8.2 %collective-permute-start = (bf16[16,128,256]{2,1,0:T(8,128)(2,1)S(1)}, bf16[16,128,256]{2,1,0:T(8,128)(2,1)S(1)}, u32[]{:S(2)}, u32[]{:S(2)}) collective-permute-start(bf16[16,128,256]{2,1,0:T(8,128)(2,1)S(1)} %slice.12), channel_id=1, source_target_pairs={{0,1},{1,0},{2,3},{3,2},{4,5},{5,4},{6,7},{7,6},{8,9},{9,8},{10,11... | collective-permute-start | bytes 3145736 | tf_op jit(solution)/shard_map/ppermute | solution.py:442
  59.5 2.3 %collective-permute-done.mate_ref = bf16[16,128,256]{2,1,0:T(8,128)(2,1)S(1)} collective-permute-done((bf16[16,128,256]{2,1,0:T(8,128)(2,1)S(1)}, bf16[16,128,256]{2,1,0:T(8,128)(2,1)S(1)}, u32[]{:S(2)}, u32[]{:S(2)}) %collective-permute-start) | collective-permute-done | bytes 1048608 | tf_op jit(solution)/shard_map/ppermute | solution.py:442
  61.7 17.2 %block_attention.1 = (bf16[16,128,512]{2,1,0:T(8,128)(2,1)}, bf16[16,128,256]{2,1,0:T(8,128)(2,1)S(1)}, f32[8,128]{1,0:T(8,128)S(1)}) custom-call(s32[4,256]{1,0:T(4,128)S(1)} %select_reduce_fusion.half_ref, s32[4,128]{1,0:T(4,128)S(1)} %broadcast_minimum_fusion.lane_ref, s32[4,3]{1,0:T(4,128)S(1)} %pad_add_fusion.groups_ref, ...), custom_call_target="tpu_custom_call" | custom-call | flops 40000000000 | bytes 9000000 | tf_op jit(solution)/shard_map/block_attention/pallas_call | solution.py:210
  78.9 2.3 %collective-permute-start.1 = (bf16[16,128,256]{2,1,0:T(8,128)(2,1)S(1)}, bf16[16,128,256]{2,1,0:T(8,128)(2,1)S(1)}, u32[]{:S(2)}, u32[]{:S(2)}) collective-permute-start(bf16[16,128,256]{2,1,0:T(8,128)(2,1)S(1)} %get-tuple-element.23), channel_id=1, source_target_pairs={{0,1},{1,0},{2,3},{3,2},{4,5},{5,4},{6,7},{7,6},{8,9},{9,8},{10,11... | collective-permute-start | bytes 3145736 | tf_op jit(solution)/shard_map/ppermute | solution.py:445
  81.2 2.3 %collective-permute-done.1.got_ref = bf16[16,128,256]{2,1,0:T(8,128)(2,1)S(1)} collective-permute-done((bf16[16,128,256]{2,1,0:T(8,128)(2,1)S(1)}, bf16[16,128,256]{2,1,0:T(8,128)(2,1)S(1)}, u32[]{:S(2)}, u32[]{:S(2)}) %collective-permute-start.1) | collective-permute-done | bytes 1048608 | tf_op jit(solution)/shard_map/ppermute | solution.py:445
  83.5 2.1 %merge.1 = bf16[16,128,512]{2,1,0:T(8,128)(2,1)} custom-call(bf16[16,128,512]{2,1,0:T(8,128)(2,1)} %get-tuple-element.22.send_ref, bf16[16,128,256]{2,1,0:T(8,128)(2,1)S(1)} %collective-permute-done.1.got_ref), custom_call_target="tpu_custom_call", output_to_operand_aliasing={{}: (0, {})} | custom-call | tf_op jit(solution)/shard_map/merge/pallas_call | solution.py:329
  85.5 3.7 %all-to-all-start.1 = ((bf16[16,128,512]{2,1,0:T(8,128)(2,1)}), bf16[16,128,512]{2,1,0:T(8,128)(2,1)S(1)}, u32[]{:S(2)}, u32[]{:S(2)}) async-start(bf16[16,128,512]{2,1,0:T(8,128)(2,1)} %merge.1), calls=%async_computation.1 | async-start | bytes 4194304 | tf_op jit(solution)/shard_map/all_to_all | solution.py:436
  89.3 42.8 %all-gather.1 = f32[32,2,128]{2,1,0:T(2,128)S(1)} all-gather(f32[1,2,128]{2,1,0:T(2,128)S(1)} %bitcast.19), channel_id=2, replica_groups={{0,1,32,33,64,65,96,97,128,129,160,161,192,193,224,225,256,257,288,289,..., dimensions={0}, use_global_device_ids=true | all-gather | bytes 33792 | tf_op jit(solution)/shard_map/all_gather | solution.py:448
  132.1 0.1 reduce_sum.72
  132.2 0.6 fusion.18
  134.1 0.0 all-to-all-done.1.back_ref
  134.1 1.3 unpack.1
  (17 shorter events, 0.2 us)
Async XLA Ops:
  0.6 11.5 %copy-start = (s32[32,32,32]{2,1,0:T(8,128)S(1)}, s32[32,32,32]{2,1,0:T(8,128)}, u32[]{:S(2)}) copy-start(s32[32,32,32]{2,1,0:T(8,128)} %param.9) | copy-start | bytes 393220
  4.5 45.4 %all-to-all-start = ((bf16[16,128,768]{2,1,0:T(8,128)(2,1)}), bf16[16,128,768]{2,1,0:T(8,128)(2,1)}, u32[]{:S(2)}, u32[]{:S(2)}) async-start(bf16[16,128,768]{2,1,0:T(8,128)(2,1)} %pack.1), calls=%async_computation | async-start | bytes 6291456 | tf_op jit(solution)/shard_map/all_to_all | solution.py:436
  51.2 10.5 %collective-permute-start = (bf16[16,128,256]{2,1,0:T(8,128)(2,1)S(1)}, bf16[16,128,256]{2,1,0:T(8,128)(2,1)S(1)}, u32[]{:S(2)}, u32[]{:S(2)}) collective-permute-start(bf16[16,128,256]{2,1,0:T(8,128)(2,1)S(1)} %slice.12), channel_id=1, source_target_pairs={{0,1},{1,0},{2,3},{3,2},{4,5},{5,4},{6,7},{7,6},{8,9},{9,8},{10,11... | collective-permute-start | bytes 3145736 | tf_op jit(solution)/shard_map/ppermute | solution.py:442
  78.9 4.6 %collective-permute-start.1 = (bf16[16,128,256]{2,1,0:T(8,128)(2,1)S(1)}, bf16[16,128,256]{2,1,0:T(8,128)(2,1)S(1)}, u32[]{:S(2)}, u32[]{:S(2)}) collective-permute-start(bf16[16,128,256]{2,1,0:T(8,128)(2,1)S(1)} %get-tuple-element.23), channel_id=1, source_target_pairs={{0,1},{1,0},{2,3},{3,2},{4,5},{5,4},{6,7},{7,6},{8,9},{9,8},{10,11... | collective-permute-start | bytes 3145736 | tf_op jit(solution)/shard_map/ppermute | solution.py:445
  85.5 48.6 %all-to-all-start.1 = ((bf16[16,128,512]{2,1,0:T(8,128)(2,1)}), bf16[16,128,512]{2,1,0:T(8,128)(2,1)S(1)}, u32[]{:S(2)}, u32[]{:S(2)}) async-start(bf16[16,128,512]{2,1,0:T(8,128)(2,1)} %merge.1), calls=%async_computation.1 | async-start | bytes 4194304 | tf_op jit(solution)/shard_map/all_to_all | solution.py:436
